TPU v7x, 32 devices: a whole 2x2x4 slice. The times are simulated.
32 devices in a mesh: ctx: 8 (over z, y), fsdp: 4 (over x, core).
Axes of the slice: x: 2, y: 2, z: 4, core: 2. Of those that a mesh axis runs over, the one named last changes fastest.
Arguments:
- tokens: bfloat16 [4, 1024, 2048], P('fsdp', 'ctx'), may hold values from -6 to 6
- layer_input: bfloat16 [4, 1024, 256], P('fsdp', 'ctx'), may hold values from -6 to 6
- cotangent: bfloat16 [4, 1024, 2048], P('fsdp', 'ctx'), may hold values from -6 to 6
- doc_lengths: int32 [4, 4], P('fsdp'), may hold values from 1 to 512, 1024 in all within a row
- pair_of: int32 [8], replicated, may hold values from 0 to 7, each once
- w_query: float32 [2048, 2048], P(('ctx', 'fsdp')), may hold values from -0.125 to 0.125
- w_key: float32 [2048, 512], P(('ctx', 'fsdp')), may hold values from -0.125 to 0.125
- w_value: float32 [2048, 512], P(('ctx', 'fsdp')), may hold values from -0.125 to 0.125
- w_out: float32 [2048, 2048], P(('ctx', 'fsdp')), may hold values from -0.125 to 0.125
- w_left: float32 [2048, 64], P(('ctx', 'fsdp')), may hold values from -0.125 to 0.125
- w_right: float32 [64, 2048], P(None, ('ctx', 'fsdp')), may hold values from -0.75 to 0.75
- norm_gains: float32 [6, 2048], P(None, ('ctx', 'fsdp')), may hold values from 0.5 to 1.5
- qk_gain: float32 [2, 256], P(None, ('ctx', 'fsdp')), may hold values from 0.25 to 0.5
- w_gate: float32 [2048, 8192], P(('ctx', 'fsdp')), may hold values from -0.125 to 0.125
- w_up: float32 [2048, 8192], P(('ctx', 'fsdp')), may hold values from -0.125 to 0.125
- w_down: float32 [8192, 2048], P(('ctx', 'fsdp')), may hold values from -0.0625 to 0.0625
- w_pgate: float32 [2048, 256], P(('ctx', 'fsdp')), may hold values from -0.125 to 0.125
- w_pproj: float32 [256, 2048], P(None, ('ctx', 'fsdp')), may hold values from -0.375 to 0.375
Outputs:
- output: bfloat16 [4, 1024, 2048], P('fsdp', 'ctx')
- d_tokens: bfloat16 [4, 1024, 2048], P('fsdp', 'ctx')
- d_layer_input: bfloat16 [4, 1024, 256], P('fsdp', 'ctx')
- grad_query: float32 [2048, 2048], P(('ctx', 'fsdp'))
- grad_key: float32 [2048, 512], P(('ctx', 'fsdp'))
- grad_value: float32 [2048, 512], P(('ctx', 'fsdp'))
- grad_out: float32 [2048, 2048], P(('ctx', 'fsdp'))
- grad_left: float32 [2048, 64], P(('ctx', 'fsdp'))
- grad_right: float32 [64, 2048], P(None, ('ctx', 'fsdp'))
- grad_gains: float32 [6, 2048], P(None, ('ctx', 'fsdp'))
- grad_qk: float32 [2, 256], P(None, ('ctx', 'fsdp'))
- grad_gate: float32 [2048, 8192], P(('ctx', 'fsdp'))
- grad_up: float32 [2048, 8192], P(('ctx', 'fsdp'))
- grad_down: float32 [8192, 2048], P(('ctx', 'fsdp'))
- grad_pgate: float32 [2048, 256], P(('ctx', 'fsdp'))
- grad_pproj: float32 [256, 2048], P(None, ('ctx', 'fsdp'))
Inputs may be any that keep to these rules, and one draw needn't show every extreme that they name: `doc_lengths`: each row sums to 1024; its longest document has exactly 512 tokens. A permutation: index c of ctx holds, in this order, blocks pair_of[c] and 15 - pair_of[c] of 64 tokens of its stream.
All inputs are finite; a program needn't handle non-finite values.
Results may differ from a plain program's by a relative error of at most 0.02.
The roundings to bfloat16 on the way count: a program that leaves them out, or rounds other values in their place, can miss the bound.
Values may be sent and summed in bfloat16 or wider, within the bound.
No kernel may reach another device: no remote copies, remote signals or barrier semaphores. Data moves between devices by JAX's collectives and lax.ppermute only.
A program may use at most 448 MiB of HBM per device.

v0:
```python
import jax
import jax.numpy as jnp
from jax import lax
from jax.sharding import PartitionSpec as P

H = 8
KVH = 2
HD = 256


EPSILON = 1e-06
ROPE_BASE = 1000000.0
HALF_ROOT = 0.7071067811865476
MASKED = -1e30


def rms_norm(values_in, gain_in):
    return (
        values_in
        * lax.rsqrt(jnp.mean(values_in * values_in, axis=-1, keepdims=True) + EPSILON)
        * gain_in
    )


def gelu_tanh(values_in):
    return jax.nn.gelu(values_in, approximate=True)


def glu_piece(gate_in, up_in):
    return gelu_tanh(gate_in) * up_in


def tables(rel_pos, head_size):
    frequency = ROPE_BASE ** (-2.0 * jnp.arange(head_size // 2, dtype=jnp.float32) / head_size)
    angles = rel_pos.astype(jnp.float32)[:, None] * frequency[None, :]
    return (jnp.cos(angles)[:, None, :], jnp.sin(angles)[:, None, :])


def rotate(values_in, cos_tab, sine_tab):
    half_width = values_in.shape[-1] // 2
    first_half = values_in[..., :half_width]
    second_half = values_in[..., half_width:]
    return jnp.concatenate(
        [
            first_half * cos_tab - second_half * sine_tab,
            second_half * cos_tab + first_half * sine_tab,
        ],
        axis=-1,
    )


def layout(pair_of, lengths, row_count):
    dev_count = pair_of.shape[0]
    local_row = jnp.arange(row_count * dev_count, dtype=jnp.int32) % row_count
    half_rows = row_count // 2
    pair_idx = jnp.repeat(pair_of, row_count)
    block_idx = jnp.where(local_row < half_rows, pair_idx, 2 * dev_count - 1 - pair_idx)
    position = block_idx * half_rows + local_row % half_rows
    doc_ends = jnp.cumsum(lengths, dtype=jnp.int32)
    before = doc_ends[None, :] <= position[:, None]
    segment = jnp.sum(before.astype(jnp.int32), axis=1, dtype=jnp.int32)
    doc_start = jnp.sum(jnp.where(before, lengths[None, :], 0), axis=1, dtype=jnp.int32)
    return (position, segment, position - doc_start)


def times_plain(left_in, right_in):
    return jnp.dot(left_in, right_in, preferred_element_type=jnp.float32)


def times_transposed(left_in, right_in):
    return jnp.einsum("ra,ba->rb", left_in, right_in, preferred_element_type=jnp.float32)


def contract_rows(left_in, right_in):
    return jnp.einsum("ra,rb->ab", left_in, right_in, preferred_element_type=jnp.float32)


def fetch_small(
    w_query, w_key, w_value, w_out, w_left, w_right, norm_gains, qk_gain, w_pgate, w_pproj
):
    return (
        lax.all_gather(w_query.astype(jnp.bfloat16), ("ctx", "fsdp"), axis=0, tiled=True),
        lax.all_gather(w_key.astype(jnp.bfloat16), ("ctx", "fsdp"), axis=0, tiled=True),
        lax.all_gather(w_value.astype(jnp.bfloat16), ("ctx", "fsdp"), axis=0, tiled=True),
        lax.all_gather(w_out.astype(jnp.bfloat16), ("ctx", "fsdp"), axis=0, tiled=True),
        lax.all_gather(w_left.astype(jnp.bfloat16), ("ctx", "fsdp"), axis=0, tiled=True),
        lax.all_gather(w_right.astype(jnp.bfloat16), ("ctx", "fsdp"), axis=1, tiled=True),
        lax.all_gather(norm_gains.astype(jnp.bfloat16), ("ctx", "fsdp"), axis=1, tiled=True),
        lax.all_gather(qk_gain.astype(jnp.bfloat16), ("ctx", "fsdp"), axis=1, tiled=True),
        lax.all_gather(w_pgate.astype(jnp.bfloat16), ("ctx", "fsdp"), axis=0, tiled=True),
        lax.all_gather(w_pproj.astype(jnp.bfloat16), ("ctx", "fsdp"), axis=1, tiled=True),
    )


def local(
    tokens,
    layer_input,
    cotangent,
    doc_lengths,
    pair_of,
    w_query,
    w_key,
    w_value,
    w_out,
    w_left,
    w_right,
    norm_gains,
    qk_gain,
    w_gate,
    w_up,
    w_down,
    w_pgate,
    w_pproj,
):
    row_count = tokens.shape[1]
    seq_len = row_count * lax.axis_size("ctx")
    ctx_index = lax.axis_index("ctx")
    group_size = H // KVH
    position, segment, relative = layout(pair_of, doc_lengths[0], row_count)
    own_pos = lax.dynamic_slice_in_dim(position, ctx_index * row_count, row_count)
    own_seg = lax.dynamic_slice_in_dim(segment, ctx_index * row_count, row_count)
    own_rel = lax.dynamic_slice_in_dim(relative, ctx_index * row_count, row_count)
    cos_tab, sine_tab = tables(own_rel, HD)
    gate_low_shard = w_gate.astype(jnp.bfloat16)
    up_low_shard = w_up.astype(jnp.bfloat16)
    down_low_shard = w_down.astype(jnp.bfloat16)
    small_mats = fetch_small(
        w_query, w_key, w_value, w_out, w_left, w_right, norm_gains, qk_gain, w_pgate, w_pproj
    )
    q_mat, k_mat, v_mat, o_mat, left_mat, right_mat, gain_rows, qk_rows, pgate_mat, pproj_mat = (
        small_mats
    )
    gain_vals = gain_rows.astype(jnp.float32)
    qk_vals = qk_rows.astype(jnp.float32)
    token_vals = tokens[0].astype(jnp.float32)
    extra_vals = layer_input[0].astype(jnp.float32)
    normed = rms_norm(token_vals, gain_vals[0])
    normed_low = normed.astype(jnp.bfloat16)
    q_raw = times_plain(normed_low, q_mat).reshape(row_count, H, HD)
    k_raw = times_plain(normed_low, k_mat).reshape(row_count, KVH, HD)
    v_raw = times_plain(normed_low, v_mat).reshape(row_count, KVH, HD)

    def rotated(raw_in, gain_in):
        return rotate(rms_norm(raw_in, gain_in), cos_tab, sine_tab)

    def unit_norm(raw_in):
        return rms_norm(raw_in, 1.0)

    query_rows = rotated(q_raw, qk_vals[0]).astype(jnp.bfloat16)
    key_rows = rotated(k_raw, qk_vals[1]).astype(jnp.bfloat16)
    value_rows = unit_norm(v_raw).astype(jnp.bfloat16)
    all_keys, all_values = (
        lax.all_gather(key_rows.reshape(row_count, KVH * HD), "ctx", axis=0, tiled=True),
        lax.all_gather(value_rows.reshape(row_count, KVH * HD), "ctx", axis=0, tiled=True),
    )
    key_block = min(512, seq_len)
    block_count = seq_len // key_block
    key_tiles = all_keys.reshape(block_count, key_block, KVH, HD)
    value_tiles = all_values.reshape(block_count, key_block, KVH, HD)
    pos_tiles = position.reshape(block_count, key_block)
    seg_tiles = segment.reshape(block_count, key_block)
    query_heads = query_rows.reshape(row_count, KVH, group_size, HD)

    def visible_of(pos_blk, seg_blk):
        return (seg_blk[None, :] == own_seg[:, None]) & (pos_blk[None, :] <= own_pos[:, None])

    def scores_of(key_blk, visible):
        scores = jnp.einsum(
            "rkgd,skd->kgrs", query_heads, key_blk, preferred_element_type=jnp.float32
        )
        return jnp.where(visible[None, None], scores, MASKED)

    def total_step(carried, tile_in):
        key_blk, pos_blk, seg_blk = tile_in
        visible = visible_of(pos_blk, seg_blk)

        def total_update(state_in):
            scores = scores_of(key_blk, visible)
            new_top = jnp.maximum(state_in[0], jnp.max(scores, axis=-1))
            new_total = state_in[1] * jnp.exp(state_in[0] - new_top) + jnp.sum(
                jnp.exp(scores - new_top[..., None]), axis=-1
            )
            return (new_top, new_total)

        def total_unchanged(state_in):
            return state_in

        return (lax.cond(jnp.any(visible), total_update, total_unchanged, carried), None)

    start_state = (
        jnp.full((KVH, group_size, row_count), MASKED, jnp.float32),
        jnp.zeros((KVH, group_size, row_count), jnp.float32),
    )
    (top_run, total_run), _ = lax.scan(total_step, start_state, (key_tiles, pos_tiles, seg_tiles))
    log_total = top_run + jnp.log(total_run)

    def output_step(out_acc, tile_in):
        key_blk, value_blk, pos_blk, seg_blk = tile_in
        visible = visible_of(pos_blk, seg_blk)

        def output_update(acc_in):
            prob_low = jnp.exp(scores_of(key_blk, visible) - log_total[..., None]).astype(
                jnp.bfloat16
            )
            return acc_in + jnp.einsum(
                "kgrs,skd->rkgd", prob_low, value_blk, preferred_element_type=jnp.float32
            )

        def output_unchanged(acc_in):
            return acc_in

        return (lax.cond(jnp.any(visible), output_update, output_unchanged, out_acc), None)

    head_out, _ = lax.scan(
        output_step,
        jnp.zeros((row_count, KVH, group_size, HD), jnp.float32),
        (key_tiles, value_tiles, pos_tiles, seg_tiles),
    )
    heads_low = head_out.reshape(row_count, H * HD).astype(jnp.bfloat16)
    projected = times_plain(heads_low, o_mat)
    gated_sum = token_vals + rms_norm(projected, gain_vals[1])
    left_low = times_plain(normed_low, left_mat).astype(jnp.bfloat16)
    right_out = times_plain(left_low, right_mat)
    laurel = normed + rms_norm(right_out, gain_vals[2])
    joined = (gated_sum + laurel) * HALF_ROOT
    ff_in = rms_norm(joined, gain_vals[3]).astype(jnp.bfloat16)
    pieces = (
        lax.all_gather(gate_low_shard, ("ctx", "fsdp"), axis=0, tiled=True),
        lax.all_gather(up_low_shard, ("ctx", "fsdp"), axis=0, tiled=True),
    )
    columns = ff_in
    gate_proj = times_plain(columns, pieces[0])
    up_proj = times_plain(columns, pieces[1])
    hidden = glu_piece(gate_proj, up_proj).astype(jnp.bfloat16)
    columns = hidden
    down_proj = times_plain(
        columns, lax.all_gather(down_low_shard, ("ctx", "fsdp"), axis=0, tiled=True)
    )
    after_ff = joined + rms_norm(down_proj, gain_vals[4])
    after_low = after_ff.astype(jnp.bfloat16)
    per_gate = times_plain(after_low, pgate_mat)
    per_mix = glu_piece(per_gate, extra_vals).astype(jnp.bfloat16)
    per_out = times_plain(per_mix, pproj_mat)
    output = after_ff + rms_norm(per_out, gain_vals[5])
    d_output = cotangent[0].astype(jnp.float32)
    back_small = fetch_small(
        w_query, w_key, w_value, w_out, w_left, w_right, norm_gains, qk_gain, w_pgate, w_pproj
    )
    (
        q_back,
        k_back,
        v_back,
        o_back,
        left_back,
        right_back,
        gain_back_rows,
        qk_back_rows,
        pgate_back,
        pproj_back,
    ) = back_small
    gain_back = gain_back_rows.astype(jnp.float32)
    qk_back = qk_back_rows.astype(jnp.float32)
    _, norm_pull = jax.vjp(rms_norm, per_out, gain_back[5])
    d_per_out, d_gain_ple = norm_pull(d_output)
    d_per_low = d_per_out.astype(jnp.bfloat16)
    grad_pproj = contract_rows(per_mix, d_per_low)
    d_per_mix = times_transposed(d_per_low, pproj_back)
    _, glu_pull = jax.vjp(glu_piece, per_gate, extra_vals)
    d_per_gate, d_extra = glu_pull(d_per_mix)
    d_pgate_low = d_per_gate.astype(jnp.bfloat16)
    grad_pgate = contract_rows(after_low, d_pgate_low)
    d_after = d_output + times_transposed(d_pgate_low, pgate_back)
    _, norm_pull = jax.vjp(rms_norm, down_proj, gain_back[4])
    d_down, d_gain_post_ff = norm_pull(d_after)
    d_down_low = d_down.astype(jnp.bfloat16)
    d_hidden = times_transposed(
        d_down_low, lax.all_gather(down_low_shard, ("ctx", "fsdp"), axis=0, tiled=True)
    )
    grad_down = lax.psum_scatter(
        contract_rows(hidden, d_down_low), ("ctx", "fsdp"), scatter_dimension=0, tiled=True
    )
    _, glu_pull = jax.vjp(glu_piece, gate_proj, up_proj)
    d_gate, d_up = glu_pull(d_hidden)
    d_gate_low = d_gate.astype(jnp.bfloat16)
    d_up_low = d_up.astype(jnp.bfloat16)
    grad_gate = lax.psum_scatter(
        contract_rows(ff_in, d_gate_low), ("ctx", "fsdp"), scatter_dimension=0, tiled=True
    )
    grad_up = lax.psum_scatter(
        contract_rows(ff_in, d_up_low), ("ctx", "fsdp"), scatter_dimension=0, tiled=True
    )
    pieces = (
        lax.all_gather(gate_low_shard, ("ctx", "fsdp"), axis=0, tiled=True),
        lax.all_gather(up_low_shard, ("ctx", "fsdp"), axis=0, tiled=True),
    )
    term = times_transposed(d_gate_low, pieces[0]) + times_transposed(d_up_low, pieces[1])
    _, norm_pull = jax.vjp(rms_norm, joined, gain_back[3])
    d_joined_norm, d_gain_pre_ff = norm_pull(term)
    d_joined = d_after + d_joined_norm
    d_branch = d_joined * HALF_ROOT
    _, norm_pull = jax.vjp(rms_norm, projected, gain_back[1])
    d_projected, d_gain_post_attn = norm_pull(d_branch)
    _, norm_pull = jax.vjp(rms_norm, right_out, gain_back[2])
    d_right, d_gain_laurel = norm_pull(d_branch)
    d_proj_low = d_projected.astype(jnp.bfloat16)
    d_right_low = d_right.astype(jnp.bfloat16)
    grad_out = contract_rows(heads_low, d_proj_low)
    grad_right = contract_rows(left_low, d_right_low)
    d_left_low = times_transposed(d_right_low, right_back).astype(jnp.bfloat16)
    grad_left = contract_rows(normed_low, d_left_low)
    d_heads = (
        times_transposed(d_proj_low, o_back)
        .astype(jnp.bfloat16)
        .reshape(row_count, KVH, group_size, HD)
    )
    row_delta = jnp.transpose(jnp.sum(d_heads.astype(jnp.float32) * head_out, axis=-1), (1, 2, 0))

    def grad_step(d_query_acc, tile_in):
        key_blk, value_blk, pos_blk, seg_blk = tile_in
        visible = visible_of(pos_blk, seg_blk)

        def grad_update(acc_in):
            probs_full = jnp.exp(scores_of(key_blk, visible) - log_total[..., None])
            d_probs = jnp.einsum(
                "rkgd,skd->kgrs", d_heads, value_blk, preferred_element_type=jnp.float32
            )
            d_scores = (probs_full * (d_probs - row_delta[..., None])).astype(jnp.bfloat16)
            new_acc = acc_in + jnp.einsum(
                "kgrs,skd->rkgd", d_scores, key_blk, preferred_element_type=jnp.float32
            )
            d_key_blk = jnp.einsum(
                "kgrs,rkgd->skd", d_scores, query_heads, preferred_element_type=jnp.float32
            )
            d_value_blk = jnp.einsum(
                "kgrs,rkgd->skd",
                probs_full.astype(jnp.bfloat16),
                d_heads,
                preferred_element_type=jnp.float32,
            )
            return (new_acc, d_key_blk, d_value_blk)

        def skipped(acc_in):
            empty_blk = jnp.zeros((key_block, KVH, HD), jnp.float32)
            return (acc_in, empty_blk, empty_blk)

        new_acc, d_key_blk, d_value_blk = lax.cond(
            jnp.any(visible), grad_update, skipped, d_query_acc
        )
        return (new_acc, (d_key_blk, d_value_blk))

    d_query, (key_grads, value_grads) = lax.scan(
        grad_step,
        jnp.zeros((row_count, KVH, group_size, HD), jnp.float32),
        (key_tiles, value_tiles, pos_tiles, seg_tiles),
    )
    own_dk, own_dv = (
        lax.psum_scatter(
            key_grads.reshape(seq_len, KVH * HD).astype(jnp.bfloat16),
            "ctx",
            scatter_dimension=0,
            tiled=True,
        ).astype(jnp.float32),
        lax.psum_scatter(
            value_grads.reshape(seq_len, KVH * HD).astype(jnp.bfloat16),
            "ctx",
            scatter_dimension=0,
            tiled=True,
        ).astype(jnp.float32),
    )
    _, rot_pull = jax.vjp(rotated, q_raw, qk_back[0])
    d_q_raw, d_gain_query = rot_pull(d_query.reshape(row_count, H, HD))
    _, rot_pull = jax.vjp(rotated, k_raw, qk_back[1])
    d_k_raw, d_gain_key = rot_pull(own_dk.reshape(row_count, KVH, HD))
    _, unit_pull = jax.vjp(unit_norm, v_raw)
    (d_v_raw,) = unit_pull(own_dv.reshape(row_count, KVH, HD))
    d_q_low = d_q_raw.reshape(row_count, H * HD).astype(jnp.bfloat16)
    d_k_low = d_k_raw.reshape(row_count, KVH * HD).astype(jnp.bfloat16)
    d_v_low = d_v_raw.reshape(row_count, KVH * HD).astype(jnp.bfloat16)
    grad_query = contract_rows(normed_low, d_q_low)
    grad_key = contract_rows(normed_low, d_k_low)
    grad_value = contract_rows(normed_low, d_v_low)
    d_normed = (
        d_branch
        + times_transposed(d_left_low, left_back)
        + times_transposed(d_q_low, q_back)
        + times_transposed(d_k_low, k_back)
        + times_transposed(d_v_low, v_back)
    )
    _, norm_pull = jax.vjp(rms_norm, token_vals, gain_back[0])
    d_tokens_norm, d_gain_input = norm_pull(d_normed)
    d_tokens = d_branch + d_tokens_norm
    grad_gains = jnp.stack(
        [d_gain_input, d_gain_post_attn, d_gain_laurel, d_gain_pre_ff, d_gain_post_ff, d_gain_ple]
    )
    grad_qk = jnp.stack([d_gain_query, d_gain_key])
    small_sums = (
        lax.psum_scatter(grad_query, ("ctx", "fsdp"), scatter_dimension=0, tiled=True),
        lax.psum_scatter(grad_key, ("ctx", "fsdp"), scatter_dimension=0, tiled=True),
        lax.psum_scatter(grad_value, ("ctx", "fsdp"), scatter_dimension=0, tiled=True),
        lax.psum_scatter(grad_out, ("ctx", "fsdp"), scatter_dimension=0, tiled=True),
        lax.psum_scatter(grad_left, ("ctx", "fsdp"), scatter_dimension=0, tiled=True),
        lax.psum_scatter(grad_right, ("ctx", "fsdp"), scatter_dimension=1, tiled=True),
        lax.psum_scatter(grad_gains, ("ctx", "fsdp"), scatter_dimension=1, tiled=True),
        lax.psum_scatter(grad_qk, ("ctx", "fsdp"), scatter_dimension=1, tiled=True),
        lax.psum_scatter(grad_pgate, ("ctx", "fsdp"), scatter_dimension=0, tiled=True),
        lax.psum_scatter(grad_pproj, ("ctx", "fsdp"), scatter_dimension=1, tiled=True),
    )
    return (
        output.astype(jnp.bfloat16)[None],
        d_tokens.astype(jnp.bfloat16)[None],
        d_extra.astype(jnp.bfloat16)[None],
        small_sums[0],
        small_sums[1],
        small_sums[2],
        small_sums[3],
        small_sums[4],
        small_sums[5],
        small_sums[6],
        small_sums[7],
        grad_gate,
        grad_up,
        grad_down,
        small_sums[8],
        small_sums[9],
    )


def solution(mesh):
    placed = (
        P("fsdp", "ctx", None),
        P("fsdp", "ctx", None),
        P("fsdp", "ctx", None),
        P("fsdp", None),
        P(),
        P(("ctx", "fsdp"), None),
        P(("ctx", "fsdp"), None),
        P(("ctx", "fsdp"), None),
        P(("ctx", "fsdp"), None),
        P(("ctx", "fsdp"), None),
        P(None, ("ctx", "fsdp")),
        P(None, ("ctx", "fsdp")),
        P(None, ("ctx", "fsdp")),
        P(("ctx", "fsdp"), None),
        P(("ctx", "fsdp"), None),
        P(("ctx", "fsdp"), None),
        P(("ctx", "fsdp"), None),
        P(None, ("ctx", "fsdp")),
    )
    return jax.shard_map(
        local,
        mesh=mesh,
        in_specs=placed,
        out_specs=(
            P("fsdp", "ctx", None),
            P("fsdp", "ctx", None),
            P("fsdp", "ctx", None),
            P(("ctx", "fsdp"), None),
            P(("ctx", "fsdp"), None),
            P(("ctx", "fsdp"), None),
            P(("ctx", "fsdp"), None),
            P(("ctx", "fsdp"), None),
            P(None, ("ctx", "fsdp")),
            P(None, ("ctx", "fsdp")),
            P(None, ("ctx", "fsdp")),
            P(("ctx", "fsdp"), None),
            P(("ctx", "fsdp"), None),
            P(("ctx", "fsdp"), None),
            P(("ctx", "fsdp"), None),
            P(None, ("ctx", "fsdp")),
        ),
        check_vma=False,
    )
```

profile of v0, /device:TPU:1, one launch (start us, length us, event | category | flops | bytes accessed | tf_op | source)
XLA Modules:
  0.0 4770.2 jit_solution(1663320039960221838)
XLA Ops:
  11.2 43.3 all-gather
  56.1 36.4 all-gather.1
  104.7 24.5 all-gather.20.cloned.1.call-done
  147.8 41.4 all_gather.66
  190.5 38.9 all_gather.67
  241.0 50.9 %all-gather.18.cloned.1.call-done = bf16[2048,2048]{1,0:T(8,128)(2,1)} async-done(((bf16[64,2048]{1,0:T(8,128)(2,1)}), bf16[2048,2048]{1,0:T(8,128)(2,1)}) %all-gather.18.cloned.1.call-update) | async-done | bytes 8388624 | tf_op jit(solution)/shard_map/all_gather | solution.py:82
  291.9 12.3 copy.141
  304.2 6.4 multiply_reduce_fusion.16
  311.7 4.9 while.42
  317.3 9.0 while.43
  327.4 43.8 all-gather.24.cloned.1.call-done
  371.3 5.0 multiply_reduce_fusion.15
  379.4 188.7 %all-gather.26.cloned.1.call-done = bf16[2048,8192]{1,0:T(8,128)(2,1)} async-done(((bf16[64,8192]{1,0:T(8,128)(2,1)}), bf16[2048,8192]{1,0:T(8,128)(2,1)}) %all-gather.26.cloned.1.call-update) | async-done | bytes 33554448 | tf_op jit(solution)/shard_map/all_gather | solution.py:228
  568.1 17.8 fusion.152
  585.9 178.6 %all-gather.28.cloned.1.call-done = bf16[2048,8192]{1,0:T(8,128)(2,1)} async-done(((bf16[64,8192]{1,0:T(8,128)(2,1)}), bf16[2048,8192]{1,0:T(8,128)(2,1)}) %all-gather.28.cloned.1.call-update) | async-done | bytes 33554448 | tf_op jit(solution)/shard_map/all_gather | solution.py:229
  764.5 18.4 multiply_convert_fusion.1
  782.9 177.5 %all-gather.30.cloned.1.call-done = bf16[8192,2048]{1,0:T(8,128)(2,1)} async-done(((bf16[256,2048]{1,0:T(8,128)(2,1)}), bf16[8192,2048]{1,0:T(8,128)(2,1)}) %all-gather.30.cloned.1.call-update) | async-done | bytes 33554448 | tf_op jit(solution)/shard_map/all_gather | solution.py:237
  960.4 14.1 multiply_reduce_fusion.12
  976.7 38.9 all-gather.32.cloned.1.call-done
  1017.4 54.2 %all-gather.34.cloned.1.call-done = bf16[256,2048]{0,1:T(8,128)(2,1)} async-done(((bf16[256,64]{0,1:T(8,128)(2,1)}), bf16[256,2048]{0,1:T(8,128)(2,1)}) %all-gather.34.cloned.1.call-update) | async-done | bytes 1048592 | tf_op jit(solution)/shard_map/all_gather | solution.py:91
  1080.5 20.5 multiply_convert_fusion
  1101.0 17.3 fusion.153
  1118.4 18.7 multiply_reduce_fusion.2
  1142.9 7.2 convolution_convert_fusion
  1156.6 13.5 while.44
  1158.1 4.2 conditional.8
  1164.8 4.2 conditional.8
  1182.1 6.4 fusion.154
  1190.0 44.1 reduce-scatter.20.cloned.1.call-done
  1246.5 54.0 %reduce-scatter.22.cloned.1.call-done = bf16[128,512]{1,0:T(8,128)(2,1)} async-done(((bf16[1024,512]{1,0:T(8,128)(2,1)}), bf16[128,512]{1,0:T(8,128)(2,1)}) %reduce-scatter.22.cloned.1.call-update) | async-done | bytes 131088 | tf_op jit(solution)/shard_map/reduce_scatter | solution.py:363
  1325.0 8.3 fusion.91
  1334.5 8.2 fusion.155
  1344.5 23.2 fusion.156
  1369.3 23.2 fusion.157
  1394.2 23.2 fusion.158
  1417.4 15.3 reduce-scatter.44.cloned.1.call-done
  1434.2 41.5 all-reduce.4
  1477.6 88.3 %reduce-scatter.46.cloned.1.call-done = f32[64,6]{1,0:T(8,128)} async-done(((f32[2048,6]{1,0:T(8,128)}), f32[64,6]{1,0:T(8,128)}) %reduce-scatter.46.cloned.1.call-update) | async-done | bytes 1552
  1567.2 132.0 %reduce-scatter.32.cloned.1.call-done = f32[64,64]{1,0:T(8,128)} async-done(((f32[2048,64]{1,0:T(8,128)}), f32[64,64]{1,0:T(8,128)}) %reduce-scatter.32.cloned.1.call-update) | async-done | bytes 16400 | tf_op jit(solution)/shard_map/reduce_scatter | solution.py:401
  1699.2 135.4 %reduce-scatter.40.cloned.1.call-done = f32[64,256]{1,0:T(8,128)} async-done(((f32[2048,256]{1,0:T(8,128)}), f32[64,256]{1,0:T(8,128)}) %reduce-scatter.40.cloned.1.call-update) | async-done | bytes 65552 | tf_op jit(solution)/shard_map/reduce_scatter | solution.py:405
  1834.7 135.3 %reduce-scatter.42.cloned.1.call-done = f32[256,64]{0,1:T(8,128)} async-done(((f32[256,2048]{0,1:T(8,128)}), f32[256,64]{0,1:T(8,128)}) %reduce-scatter.42.cloned.1.call-update) | async-done | bytes 65552 | tf_op jit(solution)/shard_map/reduce_scatter | solution.py:406
  1970.0 139.6 %reduce-scatter.26.cloned.1.call-done = f32[64,512]{1,0:T(8,128)} async-done(((f32[2048,512]{1,0:T(8,128)}), f32[64,512]{1,0:T(8,128)}) %reduce-scatter.26.cloned.1.call-update) | async-done | bytes 131088 | tf_op jit(solution)/shard_map/reduce_scatter | solution.py:398
  2109.6 139.7 %reduce-scatter.28.cloned.1.call-done = f32[64,512]{1,0:T(8,128)} async-done(((f32[2048,512]{1,0:T(8,128)}), f32[64,512]{1,0:T(8,128)}) %reduce-scatter.28.cloned.1.call-update) | async-done | bytes 131088 | tf_op jit(solution)/shard_map/reduce_scatter | solution.py:399
  2249.3 187.5 %reduce-scatter.24.cloned.1.call-done = f32[64,2048]{1,0:T(8,128)} async-done(((f32[2048,2048]{1,0:T(8,128)}), f32[64,2048]{1,0:T(8,128)}) %reduce-scatter.24.cloned.1.call-update) | async-done | bytes 524304 | tf_op jit(solution)/shard_map/reduce_scatter | solution.py:397
  2436.7 187.5 %reduce-scatter.30.cloned.1.call-done = f32[64,2048]{1,0:T(8,128)} async-done(((f32[2048,2048]{1,0:T(8,128)}), f32[64,2048]{1,0:T(8,128)}) %reduce-scatter.30.cloned.1.call-update) | async-done | bytes 524304 | tf_op jit(solution)/shard_map/reduce_scatter | solution.py:400
  2624.2 712.5 %reduce-scatter.34.cloned.1.call-done = f32[64,8192]{1,0:T(8,128)} async-done(((f32[2048,8192]{1,0:T(8,128)}), f32[64,8192]{1,0:T(8,128)}) %reduce-scatter.34.cloned.1.call-update) | async-done | bytes 2097168 | tf_op jit(solution)/shard_map/reduce_scatter | solution.py:286
  3336.7 713.2 %reduce-scatter.36.cloned.1.call-done = f32[64,8192]{1,0:T(8,128)} async-done(((f32[2048,8192]{1,0:T(8,128)}), f32[64,8192]{1,0:T(8,128)}) %reduce-scatter.36.cloned.1.call-update) | async-done | bytes 2097168 | tf_op jit(solution)/shard_map/reduce_scatter | solution.py:289
  4049.9 713.3 %reduce-scatter.38.cloned.1.call-done = f32[256,2048]{1,0:T(8,128)} async-done(((f32[8192,2048]{1,0:T(8,128)}), f32[256,2048]{1,0:T(8,128)}) %reduce-scatter.38.cloned.1.call-update) | async-done | bytes 2097168 | tf_op jit(solution)/shard_map/reduce_scatter | solution.py:279
  (480 shorter events, 169.2 us)
Async XLA Ops:
  7.2 94.8 %copy-start.3 = (bf16[1,128,2048]{2,1,0:T(8,128)(2,1)S(1)}, bf16[1,128,2048]{2,1,0:T(8,128)(2,1)}, u32[]{:S(2)}) copy-start(bf16[1,128,2048]{2,1,0:T(8,128)(2,1)} %param.30) | copy-start | bytes 1572868
  7.2 91.8 %all-gather.14.cloned.1.call-start = ((), (), s32[]{:S(2)}) async-start(), calls=%async_computation.14 | async-start | bytes 2162688 | tf_op jit(solution)/shard_map/all_gather | solution.py:83
  8.9 120.3 %all-gather.20.cloned.1.call-start = ((), (), s32[]{:S(2)}) async-start(), calls=%async_computation.17 | async-start | bytes 2162688 | tf_op jit(solution)/shard_map/all_gather | solution.py:84
  10.5 223.5 %all-gather.16.cloned.1.call-start = ((), (), s32[]{:S(2)}) async-start(), calls=%async_computation.15 | async-start | bytes 1179648 | tf_op jit(solution)/shard_map/all_gather | solution.py:153
  97.5 91.7 %copy-start.76 = (f32[128]{0:T(128)}, f32[128]{0:T(128)S(1)}, u32[]{:S(2)}) copy-start(f32[128]{0:T(128)S(1)} %fusion.127) | copy-start | bytes 1540
  104.6 132.3 %all-gather.22.cloned.1.call-start = ((), (), s32[]{:S(2)}) async-start(), calls=%async_computation.18 | async-start | bytes 1179648 | tf_op jit(solution)/shard_map/all_gather | solution.py:154
  137.3 154.6 %all-gather.18.cloned.1.call-start = ((), (), s32[]{:S(2)}) async-start(), calls=%async_computation.16 | async-start | bytes 8650752 | tf_op jit(solution)/shard_map/all_gather | solution.py:82
  138.2 233.1 %all-gather.24.cloned.1.call-start = ((), (), s32[]{:S(2)}) async-start(), calls=%async_computation.19 | async-start | bytes 8650752 | tf_op jit(solution)/shard_map/all_gather | solution.py:85
  140.0 428.1 %all-gather.26.cloned.1.call-start = ((), (), s32[]{:S(2)}) async-start(), calls=%async_computation.20 | async-start | bytes 34603008 | tf_op jit(solution)/shard_map/all_gather | solution.py:228
  141.2 623.3 %all-gather.28.cloned.1.call-start = ((), (), s32[]{:S(2)}) async-start(), calls=%async_computation.21 | async-start | bytes 34603008 | tf_op jit(solution)/shard_map/all_gather | solution.py:229
  144.1 88.7 %copy-start.66 = (f32[1,2048]{1,0:T(1,128)S(1)}, f32[1,2048]{1,0:T(1,128)}, u32[]{:S(2)}) copy-start(f32[1,2048]{1,0:T(1,128)} %get-tuple-element.659) | copy-start | bytes 24580
  144.1 89.3 %copy-start.68 = (f32[1,2048]{1,0:T(1,128)S(1)}, f32[1,2048]{1,0:T(1,128)}, u32[]{:S(2)}) copy-start(f32[1,2048]{1,0:T(1,128)} %get-tuple-element.660) | copy-start | bytes 24580
  144.1 816.2 %all-gather.30.cloned.1.call-start = ((), (), s32[]{:S(2)}) async-start(), calls=%async_computation.22 | async-start | bytes 34603008 | tf_op jit(solution)/shard_map/all_gather | solution.py:237
  145.3 870.2 %all-gather.32.cloned.1.call-start = ((), (), s32[]{:S(2)}) async-start(), calls=%async_computation.23 | async-start | bytes 1081344 | tf_op jit(solution)/shard_map/all_gather | solution.py:90
  146.1 925.6 %all-gather.34.cloned.1.call-start = ((), (), s32[]{:S(2)}) async-start(), calls=%async_computation.24 | async-start | bytes 1081344 | tf_op jit(solution)/shard_map/all_gather | solution.py:91
  146.8 1087.4 %reduce-scatter.20.cloned.1.call-start = ((), (), s32[]{:S(2)}) async-start(), calls=%async_computation.25 | async-start | bytes 1179648 | tf_op jit(solution)/shard_map/reduce_scatter | solution.py:357
  190.4 48.4 %copy-start.70 = (bf16[128,64]{0,1:T(8,128)(2,1)}, bf16[128,64]{0,1:T(8,128)(2,1)S(1)}, u32[]{:S(2)}) copy-start(bf16[128,64]{0,1:T(8,128)(2,1)S(1)} %convolution_convert_fusion.2) | copy-start | bytes 49156
  326.3 50.0 %copy-start.22 = (f32[128,2,4,256]{3,0,2,1:T(8,128)}, f32[128,2,4,256]{3,0,2,1:T(8,128)S(1)}, u32[]{:S(2)}) copy-start(f32[128,2,4,256]{3,0,2,1:T(8,128)S(1)} %get-tuple-element.375) | copy-start | bytes 3145732
  326.3 50.0 %copy-start.105 = (f32[2,4,128]{2,1,0:T(4,128)}, f32[2,4,128]{2,1,0:T(4,128)S(1)}, u32[]{:S(2)}) copy-start(f32[2,4,128]{2,1,0:T(4,128)S(1)} %get-tuple-element.1143) | copy-start | bytes 12292
  376.3 209.6 %copy-start.109 = (f32[128]{0:T(128)}, f32[128]{0:T(128)S(1)}, u32[]{:S(2)}) copy-start(f32[128]{0:T(128)S(1)} %get-tuple-element.676) | copy-start | bytes 1540
  376.3 209.6 %copy-start.101 = (f32[128]{0:T(128)}, f32[128]{0:T(128)S(1)}, u32[]{:S(2)}) copy-start(f32[128]{0:T(128)S(1)} %fusion.128) | copy-start | bytes 1540
  377.9 208.0 %copy-start.119 = (f32[128]{0:T(128)}, f32[128]{0:T(128)S(1)}, u32[]{:S(2)}) copy-start(f32[128]{0:T(128)S(1)} %get-tuple-element.628) | copy-start | bytes 1540
  378.4 207.5 %copy-start.111 = (f32[128]{0:T(128)}, f32[128]{0:T(128)S(1)}, u32[]{:S(2)}) copy-start(f32[128]{0:T(128)S(1)} %get-tuple-element.667) | copy-start | bytes 1540
  974.5 99.1 %copy-start.121 = (f32[128]{0:T(128)}, f32[128]{0:T(128)S(1)}, u32[]{:S(2)}) copy-start(f32[128]{0:T(128)S(1)} %get-tuple-element.680) | copy-start | bytes 1540
  974.5 97.2 %copy-start.51 = (bf16[1,128,256]{2,1,0:T(8,128)(2,1)S(1)}, bf16[1,128,256]{2,1,0:T(8,128)(2,1)}, u32[]{:S(2)}) copy-start(bf16[1,128,256]{2,1,0:T(8,128)(2,1)} %param.31) | copy-start | bytes 196612
  974.5 99.1 %copy-start.63 = (f32[1,2048]{1,0:T(1,128)S(1)}, f32[1,2048]{1,0:T(1,128)}, u32[]{:S(2)}) copy-start(f32[1,2048]{1,0:T(1,128)} %get-tuple-element.656) | copy-start | bytes 24580
  974.5 101.3 %copy-start.97 = (f32[128]{0:T(128)}, f32[128]{0:T(128)S(1)}, u32[]{:S(2)}) copy-start(f32[128]{0:T(128)S(1)} %fusion.131) | copy-start | bytes 1540
  1017.4 60.6 %copy-start.44 = (f32[128,256]{1,0:T(8,128)}, f32[128,256]{1,0:T(8,128)S(1)}, u32[]{:S(2)}) copy-start(f32[128,256]{1,0:T(8,128)S(1)} %fusion.97) | copy-start | bytes 393220
  1173.6 126.9 %reduce-scatter.22.cloned.1.call-start = ((), (), s32[]{:S(2)}) async-start(), calls=%async_computation.26 | async-start | bytes 1179648 | tf_op jit(solution)/shard_map/reduce_scatter | solution.py:363
  1177.5 255.3 %reduce-scatter.44.cloned.1.call-start = ((), (), s32[]{:S(2)}) async-start(), calls=%async_computation.37 | async-start | bytes 1081344
  1188.6 53.3 %copy-start.35 = (f32[128,2,256]{2,0,1:T(8,128)S(1)}, f32[128,2,256]{2,0,1:T(8,128)}, u32[]{:S(2)}) copy-start(f32[128,2,256]{2,0,1:T(8,128)} %copy-done.34) | copy-start | bytes 786436
  1188.6 53.3 %copy-start.92 = (f32[128,2]{0,1:T(2,128)S(1)}, f32[128,2]{0,1:T(2,128)}, u32[]{:S(2)}) copy-start(f32[128,2]{0,1:T(2,128)} %copy-done.91) | copy-start | bytes 3076
  1189.9 117.9 %copy-start.24 = (bf16[2048,512]{1,0:T(8,128)(2,1)S(1)}, bf16[2048,512]{1,0:T(8,128)(2,1)}, u32[]{:S(2)}) copy-start(bf16[2048,512]{1,0:T(8,128)(2,1)} %all-gather.14.cloned.1.call-done) | copy-start | bytes 6291460
  1190.0 375.8 %reduce-scatter.46.cloned.1.call-start = ((), (), s32[]{:S(2)}) async-start(), calls=%async_computation.38 | async-start | bytes 1081344
  1241.9 68.2 %copy-start.79 = (f32[128]{0:T(128)S(1)}, f32[128]{0:T(128)}, u32[]{:S(2)}) copy-start(f32[128]{0:T(128)} %copy-done.76) | copy-start | bytes 1540
  1313.6 385.7 %reduce-scatter.32.cloned.1.call-start = ((), (), s32[]{:S(2)}) async-start(), calls=%async_computation.31 | async-start | bytes 1081344 | tf_op jit(solution)/shard_map/reduce_scatter | solution.py:401
  1315.1 519.6 %reduce-scatter.40.cloned.1.call-start = ((), (), s32[]{:S(2)}) async-start(), calls=%async_computation.35 | async-start | bytes 2162688 | tf_op jit(solution)/shard_map/reduce_scatter | solution.py:405
  1316.9 653.0 %reduce-scatter.42.cloned.1.call-start = ((), (), s32[]{:S(2)}) async-start(), calls=%async_computation.36 | async-start | bytes 2162688 | tf_op jit(solution)/shard_map/reduce_scatter | solution.py:406
  1318.9 790.7 %reduce-scatter.26.cloned.1.call-start = ((), (), s32[]{:S(2)}) async-start(), calls=%async_computation.28 | async-start | bytes 4325376 | tf_op jit(solution)/shard_map/reduce_scatter | solution.py:398
  1321.8 927.5 %reduce-scatter.28.cloned.1.call-start = ((), (), s32[]{:S(2)}) async-start(), calls=%async_computation.29 | async-start | bytes 4325376 | tf_op jit(solution)/shard_map/reduce_scatter | solution.py:399
  1324.7 1112.1 %reduce-scatter.24.cloned.1.call-start = ((), (), s32[]{:S(2)}) async-start(), calls=%async_computation.27 | async-start | bytes 17301504 | tf_op jit(solution)/shard_map/reduce_scatter | solution.py:397
  1333.3 1290.9 %reduce-scatter.30.cloned.1.call-start = ((), (), s32[]{:S(2)}) async-start(), calls=%async_computation.30 | async-start | bytes 17301504 | tf_op jit(solution)/shard_map/reduce_scatter | solution.py:400
  1342.7 1994.0 %reduce-scatter.34.cloned.1.call-start = ((), (), s32[]{:S(2)}) async-start(), calls=%async_computation.32 | async-start | bytes 69206016 | tf_op jit(solution)/shard_map/reduce_scatter | solution.py:286
  1367.7 2682.2 %reduce-scatter.36.cloned.1.call-start = ((), (), s32[]{:S(2)}) async-start(), calls=%async_computation.33 | async-start | bytes 69206016 | tf_op jit(solution)/shard_map/reduce_scatter | solution.py:289
  1392.5 3370.7 %reduce-scatter.38.cloned.1.call-start = ((), (), s32[]{:S(2)}) async-start(), calls=%async_computation.34 | async-start | bytes 69206016 | tf_op jit(solution)/shard_map/reduce_scatter | solution.py:279
  1417.4 58.9 %copy-start.117 = (f32[128]{0:T(128)S(1)}, f32[128]{0:T(128)}, u32[]{:S(2)}) copy-start(f32[128]{0:T(128)} %copy-done.116) | copy-start | bytes 1540
  1417.4 58.9 %copy-start.9 = (f32[128,2048]{1,0:T(8,128)S(1)}, f32[128,2048]{1,0:T(8,128)}, u32[]{:S(2)}) copy-start(f32[128,2048]{1,0:T(8,128)} %copy-done.7) | copy-start | bytes 3145732
  1417.4 58.9 %copy-start.33 = (f32[128,2048]{1,0:T(8,128)S(1)}, f32[128,2048]{1,0:T(8,128)}, u32[]{:S(2)}) copy-start(f32[128,2048]{1,0:T(8,128)} %get-tuple-element.686) | copy-start | bytes 3145732
  (103 other events, 665.9 us)
Sparse Core Ops, SparseCore 0:
  11.5 58.9 all-gather.13
  73.9 55.2 all-gather.19
  131.8 37.1 all-gather.15
  171.4 40.1 all-gather.21
  214.9 76.9 all-gather.17
  295.2 76.0 all-gather.23
  374.7 193.3 all-gather.25
  571.5 192.9 all-gather.27
  767.4 192.9 all-gather.29
  963.7 51.8 all-gather.31
  1019.0 52.6 all-gather.33
  1173.7 60.3 reduce-scatter.19
  1238.0 62.4 reduce-scatter.21
  1302.6 130.1 reduce-scatter.43
  1434.9 130.8 reduce-scatter.45
  1568.5 130.7 reduce-scatter.31
  1702.0 132.5 reduce-scatter.39
  1837.3 132.5 reduce-scatter.41
  1972.9 136.5 reduce-scatter.25
  2112.3 136.8 reduce-scatter.27
  2252.2 184.4 reduce-scatter.23
  2439.7 184.4 reduce-scatter.29
  2627.3 709.3 reduce-scatter.33
  3339.6 710.2 reduce-scatter.35
  4053.0 710.2 reduce-scatter.37
where the time goes:
time: 4780 us; the launch traced here: 4770 us
  waiting for transfers between devices  4160 us (87%)
  matrix products  261 us (5%)
  blocking collectives  201 us (4%)
  local copies, waits for them, and re-layouts  77.2 us (2%)
  other arithmetic  52.7 us (1%)
    reduce_scatter x1, waiting for transfers between devices, local(): lax.psum_scatter(contract_rows(hidden, d_down_low), ('ctx', 'fsdp'), scat...  713 us
    reduce_scatter x1, waiting for transfers between devices, local(): lax.psum_scatter(contract_rows(ff_in, d_up_low), ('ctx', 'fsdp'), scatter...  713 us
    reduce_scatter x1, waiting for transfers between devices, local(): lax.psum_scatter(contract_rows(ff_in, d_gate_low), ('ctx', 'fsdp'), scatt...  712 us
    all_gather x1, waiting for transfers between devices, local(): lax.all_gather(gate_low_shard, ('ctx', 'fsdp'), axis=0, tiled=True)  189 us
    reduce_scatter x1, waiting for transfers between devices, local(): lax.psum_scatter(grad_query, ('ctx', 'fsdp'), scatter_dimension=0, tiled=...  187 us
    reduce_scatter x1, waiting for transfers between devices, local(): lax.psum_scatter(grad_out, ('ctx', 'fsdp'), scatter_dimension=0, tiled=True)  187 us
    all_gather x1, waiting for transfers between devices, local(): lax.all_gather(up_low_shard, ('ctx', 'fsdp'), axis=0, tiled=True)  179 us
    all_gather x1, waiting for transfers between devices, local(): lax.all_gather(down_low_shard, ('ctx', 'fsdp'), axis=0, tiled=True)  177 us
  transfers between devices with their start and end apart: 25, of which 22 were waited for; matrix products, arithmetic and copies ran while one was open for 6% of the time, Pallas kernels for 0%

commit v1 on v0

v1 whole, which is shorter than its diff:
```python
import jax
import jax.numpy as jnp
from jax import lax
from jax.experimental import pallas as pl
from jax.experimental.pallas import tpu as pltpu
from jax.sharding import Mesh, PartitionSpec as P

H = 8
KVH = 2
HD = 256
Z = 4
X = 2
C = 2

EPSILON = 1e-06
ROPE_BASE = 1000000.0
HALF_ROOT = 0.7071067811865476
MASKED = -1e30
BF = jnp.bfloat16
F32 = jnp.float32
EVERY = ("z", "y", "x", "c")


def rms_norm(values_in, gain_in):
    return (
        values_in
        * lax.rsqrt(jnp.mean(values_in * values_in, axis=-1, keepdims=True) + EPSILON)
        * gain_in
    )


def unit_norm(values_in):
    return values_in * lax.rsqrt(
        jnp.mean(values_in * values_in, axis=-1, keepdims=True) + EPSILON
    )


def gelu_tanh(values_in):
    return jax.nn.gelu(values_in, approximate=True)


def glu_piece(gate_in, up_in):
    return gelu_tanh(gate_in) * up_in


def rotate(values_in, cos_tab, sine_tab):
    half_width = values_in.shape[-1] // 2
    first_half = values_in[..., :half_width]
    second_half = values_in[..., half_width:]
    return jnp.concatenate(
        [
            first_half * cos_tab - second_half * sine_tab,
            second_half * cos_tab + first_half * sine_tab,
        ],
        axis=-1,
    )


def times(left_in, right_in):
    return jnp.einsum("...a,ab->...b", left_in, right_in, preferred_element_type=F32)


def times_t(left_in, right_in):
    return jnp.einsum("...a,ba->...b", left_in, right_in, preferred_element_type=F32)


def over_rows(left_in, right_in):
    return jnp.einsum("ra,rb->ab", left_in, right_in, preferred_element_type=F32)


def give_to(value, axis, size, step):
    return lax.ppermute(value, axis, [(i, (i + step) % size) for i in range(size)])


def swap_core(value):
    return lax.ppermute(value, "c", [(0, 1), (1, 0)])


def after(value, *others):
    return lax.optimization_barrier((value, *others))[0]


def pick(value, index, axis):
    return lax.dynamic_index_in_dim(value, index, axis, keepdims=False)


def stage(*values):
    return lax.optimization_barrier(values)


def start_of(spec):
    return spec[0] * spec[1] if isinstance(spec, tuple) else spec


def shuffle(arrays, outs, copies):
    dtype = arrays[0].dtype
    aligned = True
    for _, r_in, c_in, _, r_out, c_out, height, wide in copies:
        for spec, tile in ((r_in, 16), (r_out, 16), (c_in, 128), (c_out, 128)):
            size = spec[1] if isinstance(spec, tuple) else spec
            aligned = aligned and size % tile == 0
        aligned = aligned and height % 16 == 0 and wide % 128 == 0
    if not aligned:
        made = [jnp.zeros(shape, dtype) for shape in outs]
        for a, r_in, c_in, o, r_out, c_out, height, wide in copies:
            piece = lax.dynamic_slice(
                arrays[a], (start_of(r_in), start_of(c_in)), (height, wide)
            )
            made[o] = lax.dynamic_update_slice(made[o], piece, (start_of(r_out), start_of(c_out)))
        return made
    numbers = []

    def known(spec):
        if not isinstance(spec, tuple):
            return spec
        numbers.append(spec[0])
        return (len(numbers) - 1, spec[1])

    plan = [
        (a, known(r_in), known(c_in), o, known(r_out), known(c_out), height, wide)
        for a, r_in, c_in, o, r_out, c_out, height, wide in copies
    ]
    table = jnp.stack([jnp.asarray(n, jnp.int32) for n in numbers] or [jnp.int32(0)])
    count = len(arrays)

    def kernel(table_ref, *refs):
        ins, made = refs[:count], refs[count:]

        def at(spec):
            if isinstance(spec, tuple):
                return pl.multiple_of(table_ref[spec[0]] * spec[1], spec[1])
            return spec

        for a, r_in, c_in, o, r_out, c_out, height, wide in plan:
            from_row, from_column, to_row, to_column = at(r_in), at(c_in), at(r_out), at(c_out)
            step = 16 if height % 32 else 32

            @pl.loop(0, height // step)
            def _(i):
                low = pl.multiple_of(i * step, step)
                made[o][pl.ds(to_row + low, step), pl.ds(to_column, wide)] = ins[a][
                    pl.ds(from_row + low, step), pl.ds(from_column, wide)
                ]

    moved = sum(height * wide for *_, height, wide in plan) * dtype.itemsize
    return pl.pallas_call(
        kernel,
        out_shape=[jax.ShapeDtypeStruct(shape, dtype) for shape in outs],
        grid_spec=pltpu.PrefetchScalarGridSpec(
            num_scalar_prefetch=1,
            grid=(1,),
            in_specs=[pl.BlockSpec(memory_space=pltpu.VMEM)] * count,
            out_specs=[pl.BlockSpec(memory_space=pltpu.VMEM)] * len(outs),
        ),
        cost_estimate=pl.CostEstimate(flops=0, bytes_accessed=2 * moved, transcendentals=0),
    )(table, *arrays)


def stack_rows(pieces):
    if len(pieces) == 1:
        return pieces[0]
    copies = []
    low = 0
    for i, piece in enumerate(pieces):
        copies.append((i, 0, 0, 0, low, 0, *piece.shape))
        low += piece.shape[0]
    return shuffle(pieces, [(low, pieces[0].shape[1])], copies)[0]


def z_take(block):
    return [block if k == 0 else give_to(block, "z", Z, -k) for k in range(Z)]


def flat_step(step_y, step_x, y_count):
    return [
        (y * X + x, ((y + step_y) % y_count) * X + (x + step_x) % X)
        for y in range(y_count)
        for x in range(X)
    ]


def all_steps(y_count):
    return [(p // X, p % X) for p in range(1, y_count * X)]


def gather_first(block, y_count):
    if y_count == 2:
        return [give_to(block, "x", X, 1), give_to(block, "y", 2, 1)]
    return [
        lax.ppermute(block, ("y", "x"), flat_step(-dy, -dx, y_count)) for dy, dx in all_steps(y_count)
    ]


def gather_second(block, got, y_count):
    if y_count == 2:
        half = block.shape[0] // 2
        return got + [give_to(got[0][:half], "y", 2, 1), give_to(got[1][half:], "x", X, 1)]
    return got


def gather_parts(block, got, y_count):
    arrays = [block] + list(got)
    rows = block.shape[0]
    parts = [[(i, 0, rows)] for i in range(len(arrays))]
    if y_count == 2:
        parts = parts[:3] + [[(3, 0, rows // 2), (4, 0, rows // 2)]]
    return arrays, parts


def sum_first(pieces, y_count):
    if y_count == 2:
        half = pieces[3].shape[0] // 2
        return [give_to(pieces[3][:half], "x", X, 1), give_to(pieces[3][half:], "y", 2, 1)]
    return [
        lax.ppermute(pieces[dy * X + dx], ("y", "x"), flat_step(dy, dx, y_count))
        for dy, dx in all_steps(y_count)
    ]


def add_low(first_in, second_in):
    return (first_in.astype(F32) + second_in.astype(F32)).astype(BF)


def sum_second(pieces, got, y_count):
    if y_count == 2:
        half = pieces[3].shape[0] // 2
        to_y = jnp.concatenate([add_low(pieces[2][:half], got[0]), pieces[2][half:]], axis=0)
        to_x = jnp.concatenate([pieces[1][:half], add_low(pieces[1][half:], got[1])], axis=0)
        return [give_to(to_y, "y", 2, 1), give_to(to_x, "x", X, 1)]
    return got


def sum_total(pieces, got):
    total = pieces[0].astype(F32)
    for piece in got:
        total = total + piece.astype(F32)
    return total


def reduce_start(own, other):
    return own + swap_core(other.astype(BF)).astype(F32)


def reduce_end(total):
    rows = total.shape[0] // Z
    out = total[:rows]
    for k in (2, 1, 3):
        piece = total[k * rows : (k + 1) * rows].astype(BF)
        out = out + give_to(piece, "z", Z, k).astype(F32)
    return out


def write_rows(pieces, starts):
    rows, width = pieces[0].shape
    whole = jnp.zeros((rows * len(pieces), width), pieces[0].dtype)
    for piece, start in zip(pieces, starts):
        whole = lax.dynamic_update_slice_in_dim(whole, piece, start, 0)
    return whole


def z_send(sends):
    return [sends(k) if k == 0 else give_to(sends(k), "z", Z, k) for k in range(Z)]


def z_place(arrived, zi):
    rows, width = arrived[0].shape
    copies = [(k, 0, 0, 0, ((zi - k) % Z, rows), 0, rows, width) for k in range(Z)]
    return shuffle(arrived, [(Z * rows, width)], copies)[0]


def order_cores(own, other, first, axis):
    return jnp.concatenate(
        [jnp.where(first, own, other), jnp.where(first, other, own)], axis=axis
    )


def places(pair_of, lengths, ctx_ids, row_count):
    blocks_last = 2 * pair_of.shape[0] - 1
    half_rows = row_count // 2
    pair = pair_of[ctx_ids][:, None]
    row = jnp.arange(row_count, dtype=jnp.int32)[None, :]
    block = jnp.where(row < half_rows, pair, blocks_last - pair)
    position = (block * half_rows + row % half_rows).reshape(-1)
    ends = jnp.cumsum(lengths, dtype=jnp.int32)
    before = ends[None, :] <= position[:, None]
    segment = jnp.sum(before.astype(jnp.int32), axis=1, dtype=jnp.int32)
    start = jnp.sum(jnp.where(before, lengths[None, :], 0), axis=1, dtype=jnp.int32)
    return position, segment, position - start


def local(
    tokens,
    layer_input,
    cotangent,
    doc_lengths,
    pair_of,
    w_query,
    w_key,
    w_value,
    w_out,
    w_left,
    w_right,
    norm_gains,
    qk_gain,
    w_gate,
    w_up,
    w_down,
    w_pgate,
    w_pproj,
):
    rows = tokens.shape[1]
    width = tokens.shape[2]
    y_count = lax.axis_size("y")
    zi, yi, xi, ci = (lax.axis_index(name) for name in EVERY)
    first = ci == 0
    shard = w_query.shape[0]
    ff_shard = w_down.shape[0]
    yx = y_count * X
    unit = C * shard
    places_yx = [((yi + p // X) % y_count) * X + (xi + p % X) % X for p in range(yx)]
    tall = Z * unit

    def place_parts(block, got, cuts):
        arrays, parts = gather_parts(block, got, y_count)
        copies = []
        for p in range(yx):
            z = 0
            for i, _, height in parts[p]:
                for low in range(0, height, unit):
                    to = (z * yx + places_yx[p], unit)
                    for o, (left_edge, right_edge) in enumerate(cuts):
                        copies.append(
                            (i, low, left_edge, o, to, 0, unit, right_edge - left_edge)
                        )
                    z += 1
        outs = [(Z * yx * unit, high - low) for low, high in cuts]
        return shuffle(arrays, outs, copies)

    def place_blocks(block, got, height):
        arrays, parts = gather_parts(block, got, y_count)
        copies = []
        for p in range(yx):
            low = 0
            for i, _, part in parts[p]:
                to = (places_yx[p] * (height // part) + low // part, part)
                copies.append((i, 0, 0, 0, to, 0, part, block.shape[1]))
                low += part
        return shuffle(arrays, [(yx * height, block.shape[1])], copies)[0]

    def row_pieces(value):
        value = value.reshape(Z, yx, unit, -1)
        return [pick(value, places_yx[p], 1).reshape(tall, -1) for p in range(yx)]

    def column_pieces(halves):
        copies = []
        for p in range(yx):
            for h in range(C):
                for z in range(Z):
                    column = (z * yx + places_yx[p], unit)
                    copies.append(
                        (h, 0, column, p * C + h, 0, z * unit, halves[h].shape[0], unit)
                    )
        made = shuffle(list(halves), [(halves[0].shape[0], tall)] * (C * yx), copies)
        return [made[p * C : p * C + C] for p in range(yx)]

    def pair_cores(own, height):
        other = swap_core(own)
        last = own.shape[1]
        cores = [jnp.where(first, own, other), jnp.where(first, other, own)]
        return jnp.concatenate([core.reshape(-1, 1, height, last) for core in cores], axis=1)

    left_rank = w_left.shape[1]
    ple = w_pgate.shape[1]
    gain_count = norm_gains.shape[0]
    qk_shard = qk_gain.shape[1]
    ff_own = yx * ff_shard
    lanes = 2 * left_rank
    span = 3 * HD

    group_rows = Z * rows

    def z_block(value, k, height, axis=0):
        return lax.dynamic_slice_in_dim(value, (zi + k) % Z * height, height, axis=axis)

    qkv_low = jnp.concatenate([w_query, w_key, w_value], axis=1).astype(BF)
    qkv_got = swap_core(qkv_low)
    gain_pack = jnp.concatenate(
        [
            jnp.pad(norm_gains, ((0, 0), (0, lanes - shard))),
            jnp.pad(qk_gain, ((0, 0), (0, lanes - qk_shard))),
            jnp.zeros((shard - gain_count - 2, lanes), F32),
        ],
        axis=0,
    )
    misc = jnp.concatenate(
        [
            jnp.concatenate([w_left, w_right.T, w_pgate], axis=1),
            jnp.concatenate([gain_pack, w_pproj.T], axis=1),
        ],
        axis=0,
    ).astype(BF)

    copies = []
    for k in range(Z):
        z_to = (zi + k) % Z
        head = z_to * KVH // Z
        columns = [z_to * C + ci, H + head, H + KVH + head]
        for a, c_from in ((0, ci), (1, 1 - ci)):
            for j, column in enumerate(columns):
                copies.append((a, 0, (column, HD), k, (c_from, shard), j * HD, shard, HD))
        copies.append((2, 0, 0, k, 0, span, unit, misc.shape[1]))
    first_sends = shuffle(
        [qkv_low, qkv_got, misc], [(unit, span + misc.shape[1])] * Z, copies
    )
    first_arrived = z_send(lambda k: first_sends[k])
    gate_late, up_late, _ = stage(w_gate, w_up, qkv_got)
    ff_low = [gate_late.astype(BF), up_late.astype(BF)]
    ff_got = [swap_core(mat) for mat in ff_low]
    own_tokens, pair_of, first_arrived, ff_low, ff_got = stage(
        tokens[0], pair_of, first_arrived, ff_low, ff_got
    )

    token_take = z_take(own_tokens)
    first_rows = z_place(first_arrived, zi)
    first_got = gather_second(first_rows, gather_first(first_rows, y_count), y_count)
    copies = []
    for m in range(2):
        for k in range(Z):
            for a in range(yx):
                column = (((zi + k) % Z * yx + a) * C + ci, ff_shard)
                to = (m * Z + k, a * ff_shard)
                for source, c_from in ((m, ci), (2 + m, 1 - ci)):
                    copies.append(
                        (source, 0, column, to[0], (c_from, shard), to[1], shard, ff_shard)
                    )
    ff_sends = shuffle(list(ff_low) + list(ff_got), [(unit, ff_own)] * (2 * Z), copies)
    ff_sends = [ff_sends[:Z], ff_sends[Z:]]

    lengths = [doc_lengths[0], swap_core(doc_lengths)[0]]
    z_ids = (zi + jnp.arange(Z)) % Z
    own_ids = z_ids * y_count + yi
    key_ids = (z_ids[None, :] * y_count + ((yi + jnp.arange(y_count)) % y_count)[:, None]).reshape(-1)
    visible = []
    relative = []
    for lens in lengths:
        q_pos, q_seg, q_rel = places(pair_of, lens, own_ids, rows)
        k_pos, k_seg, _ = places(pair_of, lens, key_ids, rows)
        seen = (k_seg[None, :] == q_seg[:, None]) & (k_pos[None, :] <= q_pos[:, None])
        visible.append(seen.astype(F32))
        relative.append(q_rel)
    visible = jnp.stack(visible)
    relative = jnp.concatenate(relative)
    frequency = ROPE_BASE ** (-2.0 * jnp.arange(HD // 2, dtype=F32) / HD)
    angles = relative.astype(F32)[:, None] * frequency[None, :]
    cos_tab, sine_tab = jnp.cos(angles), jnp.sin(angles)
    token_take, first_rows, first_got, ff_sends, visible, cos_tab, sine_tab, w_out = stage(
        token_take, first_rows, first_got, ff_sends, visible, cos_tab, sine_tab, w_out
    )
    visible = visible > 0.5

    def rotated(raw_in, gain_in):
        return rotate(rms_norm(raw_in, gain_in), cos_tab, sine_tab)

    def rotated_own(raw_in, gain_in):
        return rotate(rms_norm(raw_in, gain_in), cos_tab[:group_rows], sine_tab[:group_rows])

    token_own = stack_rows(token_take)
    token_other = swap_core(token_own)
    gate_arrived = z_send(lambda k: ff_sends[0][k])
    qkv_mat, misc_all, small_late = place_parts(
        first_rows,
        first_got,
        [(0, span), (span, span + lanes), (span + lanes, span + lanes + ple)],
    )
    misc_all = pair_cores(misc_all, unit)
    gain_all = misc_all[:, :, shard : shard + gain_count + 2, :shard]
    gain_all = gain_all.reshape(-1, gain_count + 2, shard).transpose(1, 0, 2)
    gains = gain_all[:gain_count].reshape(gain_count, -1).astype(F32)
    qk = gain_all[gain_count:, :, :qk_shard].reshape(2, -1).astype(F32)
    unit_own = unit_norm(token_own.astype(F32))
    unit_other = unit_norm(token_other.astype(F32))
    normed_own = (unit_own * gains[0]).astype(BF)
    normed_other = (unit_other * gains[0]).astype(BF)
    qkv = jnp.concatenate([times(normed_own, qkv_mat), times(normed_other, qkv_mat)], axis=0)
    q_raw, k_raw, v_raw = qkv[:, :HD], qkv[:, HD : 2 * HD], qkv[:, 2 * HD :]
    query = rotated(q_raw, qk[0]).astype(BF).reshape(C, group_rows, HD)
    key = rotated(k_raw, qk[1]).astype(BF)
    value = unit_norm(v_raw).astype(BF)
    kv = jnp.concatenate([key, value], axis=-1).reshape(C, group_rows, 2 * HD)
    out_low = w_out.astype(BF)
    out_got = gather_first(out_low, y_count)
    kv, query, gate_arrived, out_low, out_got, misc_all, small_late = stage(
        kv,
        query,
        gate_arrived,
        out_low,
        out_got,
        misc_all,
        small_late,
    )

    up_arrived = z_send(lambda k: ff_sends[1][k])
    kv_own, kv_other = [kv[0]], [kv[1]]
    for k in range(1, y_count):
        piece = give_to(kv[0], "y", y_count, -k)
        kv_own.append(piece)
        kv_other.append(swap_core(piece))
    kv_all = jnp.stack([jnp.concatenate(kv_own), jnp.concatenate(kv_other)])
    key_all, value_all = kv_all[..., :HD], kv_all[..., HD:]
    out_rows = place_blocks(out_low, gather_second(out_low, out_got, y_count), shard)
    out_half = yx // 2 * shard
    out_got = swap_core(lax.dynamic_slice_in_dim(out_rows, (1 - ci) * out_half, out_half))
    copies = []
    for a in range(yx // 2):
        copies.append((0, (ci * (yx // 2) + a, shard), 0, 0, (a * C + ci, shard), 0, shard, width))
        copies.append((1, a * shard, 0, 0, (a * C + 1 - ci, shard), 0, shard, width))
    out_mat = shuffle([out_rows, out_got], [(HD, width)], copies)[0]
    scores = jnp.einsum("sqd,skd->sqk", query, key_all, preferred_element_type=F32)
    scores = jnp.where(visible, scores, MASKED)
    top = jnp.max(scores, axis=-1, keepdims=True)
    log_total = top + jnp.log(jnp.sum(jnp.exp(scores - top), axis=-1, keepdims=True))
    probs = jnp.exp(scores - log_total)
    probs_low = probs.astype(BF)
    head_out = jnp.einsum("sqk,skd->sqd", probs_low, value_all, preferred_element_type=F32)
    heads_low = head_out.astype(BF).reshape(C * group_rows, HD)
    heads_share = times(heads_low[group_rows:], out_mat)
    projected = reduce_start(times(heads_low[:group_rows], out_mat), heads_share)
    copies = [
        (m * Z + k, 0, 0, 0, ((zi - k) % Z, unit), m * ff_own, unit, ff_own)
        for m in range(2)
        for k in range(Z)
    ]
    gu_rows = shuffle(list(gate_arrived) + up_arrived, [(tall, 2 * ff_own)], copies)[0]
    projected, gu_rows, heads_low, misc_all, own_tokens, small_late = stage(
        projected, gu_rows, heads_low, misc_all, own_tokens, small_late
    )

    projected = reduce_end(projected)
    gu_got = gather_first(gu_rows, y_count)
    lr_mat = misc_all[:, :, :shard].reshape(-1, lanes)
    left_mat, right_mat = lr_mat[:, :left_rank], lr_mat[:, left_rank:]
    token_vals = own_tokens.astype(F32)
    normed = rms_norm(token_vals, gains[0])
    normed_low = normed.astype(BF)
    left_low = times(normed_low, left_mat).astype(BF)
    right_out = times_t(left_low, right_mat)
    laurel = normed + rms_norm(right_out, gains[2])
    projected, gu_rows, gu_got, laurel, down_late = stage(
        projected, gu_rows, gu_got, laurel, w_down
    )

    gated_sum = token_vals + rms_norm(projected, gains[1])
    joined = (gated_sum + laurel) * HALF_ROOT
    ff_in = rms_norm(joined, gains[3]).astype(BF)
    ff_take = z_take(ff_in)
    gu_got = gather_second(gu_rows, gu_got, y_count)
    down_low = after(down_late, gu_got[-1]).astype(BF)
    down_got = gather_first(down_low, y_count)
    ff_take, gu_rows, gu_got, down_low, down_got = stage(
        ff_take, gu_rows, gu_got, down_low, down_got
    )

    ff_rows = stack_rows(ff_take)
    ff_halves = [ff_rows, swap_core(ff_rows)]
    gu_mat = place_parts(gu_rows, gu_got, [(0, 2 * ff_own)])[0]
    down_got = gather_second(down_low, down_got, y_count)
    gate_proj, up_proj, hidden = [], [], []
    for half in ff_halves:
        gate_up = times(half, gu_mat)
        gate_proj.append(gate_up[:, :ff_own])
        up_proj.append(gate_up[:, ff_own:])
        hidden.append(glu_piece(gate_proj[-1], up_proj[-1]).astype(BF))
    down_mat = place_blocks(down_low, down_got, ff_shard)
    down_share = times(hidden[1], down_mat)
    down_proj = reduce_start(times(hidden[0], down_mat), down_share)
    down_proj, small_late = stage(down_proj, small_late)

    down_proj = reduce_end(down_proj)
    ple_rows = small_late.reshape(-1, C, shard, ple)
    ple_rows = jnp.concatenate([ple_rows[:, 0], ple_rows[:, 1]], axis=-1).reshape(-1, 2 * ple)
    ple_mat = pair_cores(ple_rows, shard).reshape(-1, 2 * ple)
    down_proj, ple_mat = stage(down_proj, ple_mat)
    pgate_mat, pproj_mat = ple_mat[:, :ple], ple_mat[:, ple:]

    extra_vals = layer_input[0].astype(F32)
    after_ff = joined + rms_norm(down_proj, gains[4])
    after_low = after_ff.astype(BF)
    per_gate = times(after_low, pgate_mat)
    per_mix = glu_piece(per_gate, extra_vals).astype(BF)
    per_out = times_t(per_mix, pproj_mat)
    d_output = cotangent[0].astype(F32)
    _, norm_pull = jax.vjp(rms_norm, per_out, gains[5])
    d_per_out, d_gain_ple = norm_pull(d_output)
    d_per_low = d_per_out.astype(BF)
    d_per_mix = times(d_per_low, pproj_mat)
    _, glu_pull = jax.vjp(glu_piece, per_gate, extra_vals)
    d_per_gate, d_extra = glu_pull(d_per_mix)
    d_pgate_low = d_per_gate.astype(BF)
    d_after = d_output + times_t(d_pgate_low, pgate_mat)
    _, norm_pull = jax.vjp(rms_norm, down_proj, gains[4])
    d_down, d_gain_post_ff = norm_pull(d_after)
    d_down_low = d_down.astype(BF)
    (
        d_down_low, after_late, d_pgate_late, d_per_late, per_mix_late, after_ff, per_out, d_gain_ple,
        d_gain_post_ff, d_extra,
    ) = stage(
        d_down_low, after_low, d_pgate_low, d_per_low, per_mix, after_ff, per_out, d_gain_ple,
        d_gain_post_ff, d_extra,
    )

    d_down_take = z_take(d_down_low)
    output = after_ff + rms_norm(per_out, gains[5])
    ple_grads = row_pieces(
        jnp.concatenate(
            [over_rows(after_late, d_pgate_late), over_rows(d_per_late, per_mix_late)], axis=1
        ).astype(BF)
    )
    ple_got = sum_second(ple_grads, sum_first(ple_grads, y_count), y_count)
    ple_sum = sum_total(ple_grads, ple_got).astype(BF)
    d_down_take, ple_sum = stage(d_down_take, ple_sum)

    d_down_rows = stack_rows(d_down_take)
    d_down_halves = [d_down_rows, swap_core(d_down_rows)]
    ple_arrived = z_send(lambda k: z_block(ple_sum, k, unit))
    d_gu_low = []
    for half in range(C):
        d_hidden = times_t(d_down_halves[half], down_mat)
        _, glu_pull = jax.vjp(glu_piece, gate_proj[half], up_proj[half])
        d_gate, d_up = glu_pull(d_hidden)
        d_gu_low.append(jnp.concatenate([d_gate.astype(BF), d_up.astype(BF)], axis=-1))
    term_share = times_t(d_gu_low[1], gu_mat)
    term = reduce_start(times_t(d_gu_low[0], gu_mat), term_share)
    term, d_gu_low, ple_arrived, ff_halves, hidden, d_down_halves = stage(
        term, d_gu_low, ple_arrived, ff_halves, hidden, d_down_halves
    )

    term = reduce_end(term)

    def own_core(total):
        keep = jnp.where(first, total[:shard], total[shard:])
        send = jnp.where(first, total[shard:], total[:shard])
        return keep + swap_core(send.astype(BF)).astype(F32)

    def both_rows(lefts, rights):
        return (over_rows(lefts[0], rights[0]) + over_rows(lefts[1], rights[1])).astype(BF)

    gu_grads = [None] * yx
    down_grads = [None] * yx
    ff_pieces = column_pieces(ff_halves)
    for p in reversed(range(yx)):
        gu_grads[p] = both_rows(ff_pieces[p], d_gu_low)
    gu_got = sum_first(gu_grads, y_count)
    for p in reversed(range(yx)):
        down_grads[p] = both_rows(
            [
                lax.dynamic_slice_in_dim(half, places_yx[p] * ff_shard, ff_shard, axis=1)
                for half in hidden
            ],
            d_down_halves,
        )
    if y_count == 2:
        down_grads[3] = after(down_grads[3], gu_got[0])
    down_got = sum_first(down_grads, y_count)
    term, gu_got, down_got, gu_grads, down_grads, ple_arrived = stage(
        term, gu_got, down_got, gu_grads, down_grads, ple_arrived
    )

    _, norm_pull = jax.vjp(rms_norm, joined, gains[3])
    d_joined_norm, d_gain_pre_ff = norm_pull(term)
    d_branch = (d_after + d_joined_norm) * HALF_ROOT
    _, norm_pull = jax.vjp(rms_norm, projected, gains[1])
    d_projected, d_gain_post_attn = norm_pull(d_branch)
    d_proj_low = d_projected.astype(BF)
    d_proj_low, d_branch, d_gain_pre_ff, d_gain_post_attn, right_out, normed_own, normed_other = stage(
        d_proj_low, d_branch, d_gain_pre_ff, d_gain_post_attn, right_out, normed_own, normed_other
    )

    d_proj_take = z_take(d_proj_low)
    gu_got = sum_second(gu_grads, gu_got, y_count)
    ple_total = own_core(sum(piece.astype(F32) for piece in ple_arrived))
    _, norm_pull = jax.vjp(rms_norm, right_out, gains[2])
    d_right, d_gain_laurel = norm_pull(d_branch)
    d_right_low = d_right.astype(BF)
    d_left_low = times(d_right_low, right_mat).astype(BF)
    d_normed_own = d_branch + times_t(d_left_low, left_mat)
    left_grads = jnp.concatenate(
        [over_rows(d_left_low, normed_low), over_rows(left_low, d_right_low)], axis=0
    ).astype(BF)
    normed_pieces = column_pieces((normed_own, normed_other))
    d_proj_take, gu_got, left_grads, normed_pieces, d_normed_own, ple_total = stage(
        d_proj_take, gu_got, left_grads, normed_pieces, d_normed_own, ple_total
    )

    def by_core(rows_in, blocks):
        even = jnp.concatenate(
            [rows_in[2 * j * shard : (2 * j + 1) * shard] for j in range(blocks)], axis=0
        )
        odd = jnp.concatenate(
            [rows_in[(2 * j + 1) * shard : (2 * j + 2) * shard] for j in range(blocks)], axis=0
        )
        return jnp.where(first, even, odd), swap_core(jnp.where(first, odd, even))

    d_proj_rows = stack_rows(d_proj_take)
    d_proj_halves = [d_proj_rows, swap_core(d_proj_rows)]
    gu_sum = sum_total(gu_grads, gu_got).astype(BF)
    gu_pair = by_core(gu_sum, Z)
    gu_cores = [jnp.where(first, *gu_pair), jnp.where(first, *gu_pair[::-1])]
    gu_arrived = [z_send(lambda k: z_block(gu_cores[0], k, shard))]
    down_got = sum_second(down_grads, down_got, y_count)
    d_heads = jnp.concatenate([times_t(half, out_mat) for half in d_proj_halves], axis=0)
    d_heads = d_heads.astype(BF).reshape(C, group_rows, HD)
    delta = jnp.sum(d_heads.astype(F32) * head_out, axis=-1, keepdims=True)
    d_probs = jnp.einsum("sqd,skd->sqk", d_heads, value_all, preferred_element_type=F32)
    d_scores = (probs * (d_probs - delta)).astype(BF)
    d_query = jnp.einsum("sqk,skd->sqd", d_scores, key_all, preferred_element_type=F32)
    d_key = jnp.einsum("sqk,sqd->skd", d_scores, query, preferred_element_type=F32)
    d_value = jnp.einsum("sqk,sqd->skd", probs_low, d_heads, preferred_element_type=F32)
    d_key = d_key.reshape(C, y_count, group_rows, HD)
    d_value = d_value.reshape(C, y_count, group_rows, HD)

    def kv_share(stream, k):
        return jnp.concatenate([d_key[stream, k], d_value[stream, k]], axis=-1)

    kv_give = [swap_core(kv_share(1, k).astype(BF)) for k in range(y_count)]
    kv_sum = [kv_share(0, k) + kv_give[k].astype(F32) for k in range(y_count)]
    kv_sum, d_query, gu_arrived, gu_last, d_proj_halves, heads_low, down_got = stage(
        kv_sum, d_query, gu_arrived, gu_cores[1], d_proj_halves, heads_low, down_got
    )

    gu_arrived = gu_arrived + [z_send(lambda k: z_block(gu_last, k, shard))]
    own_kv = kv_sum[0]
    for k in range(1, y_count):
        own_kv = own_kv + give_to(kv_sum[k].astype(BF), "y", y_count, k).astype(F32)
    _, rot_pull = jax.vjp(rotated, q_raw, qk[0])
    d_q_raw, d_gain_query = rot_pull(d_query.reshape(C * group_rows, HD))
    _, rot_pull = jax.vjp(rotated_own, k_raw[:group_rows], qk[1])
    d_k_raw, d_gain_key = rot_pull(own_kv[:, :HD])
    _, unit_pull = jax.vjp(unit_norm, v_raw[:group_rows])
    (d_v_raw,) = unit_pull(own_kv[:, HD:])
    d_q_low = d_q_raw.astype(BF)
    d_kv_low = jnp.concatenate([d_k_raw.astype(BF), d_v_raw.astype(BF)], axis=-1)
    d_own_low = jnp.concatenate([d_q_low[:group_rows], d_kv_low], axis=-1)
    part_other = times_t(d_q_low[group_rows:], qkv_mat[:, :HD])
    part_own = times_t(d_own_low, qkv_mat)
    d_normed = reduce_start(part_own, part_other)
    d_normed, part_own, part_other, d_q_low, d_kv_low, gu_arrived, down_grads, d_proj_halves = stage(
        d_normed, part_own, part_other, d_q_low, d_kv_low, gu_arrived, down_grads, d_proj_halves
    )

    d_normed = d_normed_own + reduce_end(d_normed)
    d_gain_input = (
        jnp.sum(part_own * unit_own, axis=0)
        + jnp.sum(part_other * unit_other, axis=0)
        + jnp.sum(d_normed_own * unit_norm(token_vals), axis=0)
    )
    d_qk = jnp.stack([d_gain_query, d_gain_key]).reshape(2, -1, qk_shard)
    d_qk = jnp.pad(d_qk, ((0, 0), (0, 0), (0, shard - qk_shard))).reshape(2, -1)
    gain_grads = jnp.stack(
        [d_gain_input, d_gain_post_attn, d_gain_laurel, d_gain_pre_ff, d_gain_post_ff, d_gain_ple]
    )
    gain_grads = jnp.concatenate([gain_grads, d_qk], axis=0)
    gain_grads = jnp.pad(gain_grads, ((0, 16 - gain_count - 2), (0, 0))).astype(BF)
    row_grads = jnp.concatenate([left_grads, gain_grads], axis=0)
    row_count = row_grads.shape[0]
    last_grads = []
    for p in range(yx):
        query_part = both_rows(normed_pieces[p], (d_q_low[:group_rows], d_q_low[group_rows:]))
        kv_part = over_rows(normed_pieces[p][0], d_kv_low).astype(BF)
        last_grads.append((query_part, kv_part))
    copies = []
    for p in range(yx):
        copies.append((C * p, 0, 0, p, 0, 0, tall, HD))
        copies.append((C * p + 1, 0, 0, p, 0, HD, tall, 2 * HD))
        for z in range(Z):
            column = (z * yx + places_yx[p], unit)
            copies.append((C * yx, 0, column, p, tall, z * unit, row_count, unit))
        copies.append((C * yx + 1, 0, 0, p, tall, tall, row_count, span - tall))
    last_grads = shuffle(
        [part for pair in last_grads for part in pair]
        + [row_grads, jnp.zeros((row_count, span - tall), BF)],
        [(tall + row_count, span)] * yx,
        copies,
    )
    last_got = sum_first(last_grads, y_count)
    last_got, last_grads, heads_low, d_proj_halves = stage(
        last_got, last_grads, heads_low, d_proj_halves
    )
    last_got = sum_second(last_grads, last_got, y_count)
    out_grad = both_rows((heads_low[:group_rows], heads_low[group_rows:]), d_proj_halves)
    out_both = order_cores(*by_core(out_grad, yx // 2), first, 0)
    out_grads = [
        lax.dynamic_slice_in_dim(out_both, places_yx[p] * shard, shard) for p in range(yx)
    ]
    grad_down = sum_total(down_grads, down_got)
    d_normed, last_got, last_grads, out_grads, gu_arrived = stage(
        d_normed, last_got, last_grads, out_grads, gu_arrived
    )

    last_low = sum_total(last_grads, last_got).astype(BF)
    qkv_pair = by_core(last_low[:tall], Z)
    qkv_cores = order_cores(*qkv_pair, first, 1)
    last_arrived = z_send(lambda k: z_block(qkv_cores, k, shard))
    by_row = last_low[tall:, :tall]
    row_arrived = z_send(lambda k: z_block(by_row, k, unit, axis=1))
    grad_out = sum_total(out_grads, sum_second(out_grads, sum_first(out_grads, y_count), y_count))
    _, norm_pull = jax.vjp(rms_norm, token_vals, gains[0])
    d_tokens_norm, _ = norm_pull(d_normed)
    d_tokens = d_branch + d_tokens_norm
    copies = []
    for k in range(Z):
        for c in range(C):
            for m in range(2):
                for a in range(yx):
                    column = (((zi - k) % Z * yx + a) * C + c, ff_shard)
                    copies.append(
                        (
                            c * Z + k, 0, m * ff_own + a * ff_shard,
                            m, 0, column, shard, ff_shard,
                        )
                    )
    grad_gu = shuffle(
        list(gu_arrived[0]) + list(gu_arrived[1]), [(shard, Z * yx * C * ff_shard)] * 2, copies
    )
    grad_gu = [grad.astype(F32) for grad in grad_gu]
    qkv_parts = z_place(last_arrived, zi).astype(F32)
    row_total = sum(piece.astype(F32) for piece in row_arrived)
    row_keep = jnp.where(first, row_total[:, :shard], row_total[:, shard:])
    row_send = jnp.where(first, row_total[:, shard:], row_total[:, :shard])
    row_total = row_keep + swap_core(row_send.astype(BF)).astype(F32)

    def qkv_part(z, c, m):
        return qkv_parts[z * shard : (z + 1) * shard, (3 * c + m) * HD : (3 * c + m + 1) * HD]

    grad_query = jnp.concatenate([qkv_part(z, c, 0) for z in range(Z) for c in range(C)], axis=1)
    grad_kv = [
        jnp.concatenate(
            [
                sum(
                    qkv_part(z, c, m)
                    for z in range(h * Z // KVH, (h + 1) * Z // KVH)
                    for c in range(C)
                )
                for h in range(KVH)
            ],
            axis=1,
        )
        for m in (1, 2)
    ]
    grad_gains = row_total[lanes : lanes + gain_count]
    grad_qk = row_total[lanes + gain_count : lanes + gain_count + 2, :qk_shard]
    return (
        output.astype(BF)[None],
        d_tokens.astype(BF)[None],
        d_extra.astype(BF)[None],
        grad_query,
        grad_kv[0],
        grad_kv[1],
        grad_out,
        row_total[:left_rank].T,
        row_total[left_rank:lanes],
        grad_gains,
        grad_qk,
        grad_gu[0],
        grad_gu[1],
        grad_down,
        ple_total[:, :ple],
        ple_total[:, ple:].T,
    )


def solution(mesh):
    fine = Mesh(mesh.devices.reshape(Z, -1, X, C), EVERY)
    rows = P(EVERY, None)
    cols = P(None, EVERY)
    stream = P(("x", "c"), ("z", "y"), None)
    return jax.shard_map(
        local,
        mesh=fine,
        in_specs=(
            stream, stream, stream, P(("x", "c"), None), P(),
            rows, rows, rows, rows, rows, cols, cols, cols, rows, rows, rows, rows, cols,
        ),
        out_specs=(
            stream, stream, stream,
            rows, rows, rows, rows, rows, cols, cols, cols, rows, rows, rows, rows, cols,
        ),
        check_vma=False,
    )
```

time: 4780 us -> 899 us (0.19)
  waiting for transfers between devices: 4160 us -> 368 us
  blocking collectives: 201 us -> 0 us
  matrix products: 261 us -> 110 us
  starting transfers between devices: 1.5 us -> 150 us
  Pallas kernels: 0 us -> 83.8 us
  other arithmetic: 52.7 us -> 102 us
    reduce_scatter x12 -> x0, waiting for transfers between devices: 3290 us -> none  [the longest x1 713 us: local(): lax.psum_scatter(contract_rows(hidden, d_down_low), ('ctx', 'fsdp'), scat...]
    all_gather x11 -> x0, waiting for transfers between devices: 757 us -> none  [the longest x1 189 us: local(): lax.all_gather(gate_low_shard, ('ctx', 'fsdp'), axis=0, tiled=True)]
    ppermute x0 -> x109, waiting for transfers between devices: none -> 368 us  [the longest x86 363 us: give_to(): lax.ppermute(value, axis, [(i, (i + step) % size) for i in range(size)])]
    all_gather x4 -> x0, blocking collectives: 160 us -> none  [the longest x1 43.3 us: fetch_small(): lax.all_gather(norm_gains.astype(jnp.bfloat16), ('ctx', 'fsdp'), axis=1,...]
    dot_general x46 -> x64, matrix products: 260 us -> 110 us  [the longest x12 38.7 us: times_t(): jnp.einsum('...a,ba->...b', left_in, right_in, preferred_element_type=F32)]
    ppermute x0 -> x109, starting transfers between devices: none -> 150 us  [the longest x86 111 us: give_to(): lax.ppermute(value, axis, [(i, (i + step) % size) for i in range(size)])]
    unnamed x27 -> x0, waiting for transfers between devices: 104 us -> none
    pallas_call x0 -> x18, Pallas kernels: none -> 83.8 us  [shuffle(): pl.pallas_call(kernel, out_shape=[jax.ShapeDtypeStruct(shape, dtype) for...]
  transfers between devices with their start and end apart: 25 -> 109, of which waited for: 22 -> 48; matrix products, arithmetic and copies ran while one was open for 6% -> 21% of each run, Pallas kernels for 0% -> 7%
where the time goes in v1:
time: 899 us; the launch traced here: 882 us
  waiting for transfers between devices  368 us (41%)
  starting transfers between devices  150 us (17%)
  matrix products  110 us (12%)
  other arithmetic  102 us (11%)
  Pallas kernels  83.8 us (9%)
  local copies, waits for them, and re-layouts  64.9 us (7%)
    ppermute x86, waiting for transfers between devices, give_to(): lax.ppermute(value, axis, [(i, (i + step) % size) for i in range(size)])  363 us
    ppermute x86, starting transfers between devices, give_to(): lax.ppermute(value, axis, [(i, (i + step) % size) for i in range(size)])  111 us
    pallas_call x18, Pallas kernels, shuffle(): pl.pallas_call(kernel, out_shape=[jax.ShapeDtypeStruct(shape, dtype) for...  83.8 us
    dot_general x12, matrix products, times_t(): jnp.einsum('...a,ba->...b', left_in, right_in, preferred_element_type=F32)  38.7 us
    ppermute x23, starting transfers between devices, swap_core(): return lax.ppermute(value, 'c', [(0, 1), (1, 0)])  38.4 us
    dot_general x34, matrix products, over_rows(): jnp.einsum('ra,rb->ab', left_in, right_in, preferred_element_type=F32)  34.7 us
    unnamed x434, local copies, waits for them, and re-layouts  31 us
    dot_general x12, matrix products, times(): jnp.einsum('...a,ab->...b', left_in, right_in, preferred_element_type=F32)  26.8 us
  transfers between devices with their start and end apart: 109, of which 48 were waited for; matrix products, arithmetic and copies ran while one was open for 21% of the time, Pallas kernels for 7%

profile of v1, /device:TPU:1, one launch (start us, length us, event | category | flops | bytes accessed | tf_op | source)
XLA Modules:
  0.0 881.7 jit_solution(17324705017372900415)
XLA Ops:
  32.4 13.0 %collective-permute-done.2.refs_2_ = bf16[128,1152]{1,0:T(8,128)(2,1)S(1)} collective-permute-done((bf16[128,1152]{1,0:T(8,128)(2,1)}, bf16[128,1152]{1,0:T(8,128)(2,1)S(1)}, u32[]{:S(2)}, u32[]{:S(2)}) %collective-permute-start.2) | collective-permute-done | bytes 294944 | tf_op jit(solution)/shard_map/ppermute | solution.py:72
  45.4 7.0 collective-permute-start.6
  62.1 20.7 %collective-permute-done.9.refs_1_ = bf16[512,1152]{1,0:T(8,128)(2,1)} collective-permute-done((bf16[512,1152]{1,0:T(8,128)(2,1)}, bf16[512,1152]{1,0:T(8,128)(2,1)}, u32[]{:S(2)}, u32[]{:S(2)}) %collective-permute-start.9) | collective-permute-done | bytes 1179680 | tf_op jit(solution)/shard_map/ppermute | solution.py:72
  88.2 5.2 shard_map.299
  106.6 6.7 shard_map.300
  144.3 10.1 %collective-permute-done.23.refs_3_ = bf16[32,2048]{1,0:T(8,128)(2,1)S(1)} collective-permute-done((bf16[32,2048]{1,0:T(8,128)(2,1)S(1)}, bf16[32,2048]{1,0:T(8,128)(2,1)S(1)}, u32[]{:S(2)}, u32[]{:S(2)}) %collective-permute-start.23) | collective-permute-done | bytes 131104 | tf_op jit(solution)/shard_map/ppermute | solution.py:72
  188.1 11.6 %collective-permute-done.28.refs_6_ = bf16[128,1024]{1,0:T(8,128)(2,1)S(1)} collective-permute-done((bf16[128,1024]{1,0:T(8,128)(2,1)S(1)}, bf16[128,1024]{1,0:T(8,128)(2,1)S(1)}, u32[]{:S(2)}, u32[]{:S(2)}) %collective-permute-start.28) | collective-permute-done | bytes 262176 | tf_op jit(solution)/shard_map/ppermute | solution.py:72
  209.4 8.5 collective-permute-start.32
  220.7 7.2 collective-permute-done.32
  227.9 12.2 %collective-permute-done.31 = bf16[128,2048]{1,0:T(8,128)(2,1)S(1)} collective-permute-done((bf16[128,2048]{1,0:T(8,128)(2,1)S(1)}, bf16[128,2048]{1,0:T(8,128)(2,1)S(1)}, u32[]{:S(2)}, u32[]{:S(2)}) %collective-permute-start.31) | collective-permute-done | bytes 524320 | tf_op jit(solution)/shard_map/ppermute | solution.py:72
  240.1 20.5 %collective-permute-done.30 = bf16[128,2048]{1,0:T(8,128)(2,1)S(1)} collective-permute-done((bf16[128,2048]{1,0:T(8,128)(2,1)S(1)}, bf16[128,2048]{1,0:T(8,128)(2,1)S(1)}, u32[]{:S(2)}, u32[]{:S(2)}) %collective-permute-start.30) | collective-permute-done | bytes 524320 | tf_op jit(solution)/shard_map/ppermute | solution.py:72
  265.8 18.0 %collective-permute-done.39.refs_4_ = bf16[256,2048]{1,0:T(8,128)(2,1)S(1)} collective-permute-done((bf16[256,2048]{1,0:T(8,128)(2,1)S(1)}, bf16[256,2048]{1,0:T(8,128)(2,1)S(1)}, u32[]{:S(2)}, u32[]{:S(2)}) %collective-permute-start.39) | collective-permute-done | bytes 1048608 | tf_op jit(solution)/shard_map/ppermute | solution.py:72
  287.8 34.5 %collective-permute-done.36.refs_2_ = bf16[128,2048]{1,0:T(8,128)(2,1)S(1)} collective-permute-done((bf16[128,2048]{1,0:T(8,128)(2,1)S(1)}, bf16[128,2048]{1,0:T(8,128)(2,1)S(1)}, u32[]{:S(2)}, u32[]{:S(2)}) %collective-permute-start.36) | collective-permute-done | bytes 524320 | tf_op jit(solution)/shard_map/ppermute | solution.py:72
  331.5 8.1 shard_map.306
  344.6 5.1 shard_map.307
  349.8 7.7 fusion.220
  364.0 4.6 fusion.219
  382.4 8.6 collective-permute-done.48
  391.0 10.2 %collective-permute-done.47 = bf16[128,2048]{1,0:T(8,128)(2,1)} collective-permute-done((bf16[128,2048]{1,0:T(8,128)(2,1)}, bf16[128,2048]{1,0:T(8,128)(2,1)}, u32[]{:S(2)}, u32[]{:S(2)}) %collective-permute-start.47) | collective-permute-done | bytes 524320 | tf_op jit(solution)/shard_map/ppermute | solution.py:72
  401.1 21.6 %collective-permute-done.46 = bf16[128,2048]{1,0:T(8,128)(2,1)} collective-permute-done((bf16[128,2048]{1,0:T(8,128)(2,1)}, bf16[128,2048]{1,0:T(8,128)(2,1)}, u32[]{:S(2)}, u32[]{:S(2)}) %collective-permute-start.46) | collective-permute-done | bytes 524320 | tf_op jit(solution)/shard_map/ppermute | solution.py:72
  432.4 5.5 collective-permute-done.55
  439.4 5.3 collective-permute-start.50
  454.2 32.6 %collective-permute-done.51.refs_2_ = bf16[128,2048]{1,0:T(8,128)(2,1)S(1)} collective-permute-done((bf16[128,2048]{1,0:T(8,128)(2,1)S(1)}, bf16[128,2048]{1,0:T(8,128)(2,1)S(1)}, u32[]{:S(2)}, u32[]{:S(2)}) %collective-permute-start.51) | collective-permute-done | bytes 524320 | tf_op jit(solution)/shard_map/ppermute | solution.py:72
  498.3 7.5 fusion.29
  505.8 5.8 convolution_convert_fusion.2
  521.2 5.9 fusion.22
  530.6 6.8 convert_add_fusion.1
  542.3 8.0 shard_map.309
  580.3 6.3 collective-permute-done.62
  605.1 4.8 collective-permute-start.74
  613.0 8.0 shard_map.310
  623.2 16.7 %collective-permute-done.70.refs_2_ = bf16[128,2048]{1,0:T(8,128)(2,1)} collective-permute-done((bf16[128,2048]{1,0:T(8,128)(2,1)}, bf16[128,2048]{1,0:T(8,128)(2,1)}, u32[]{:S(2)}, u32[]{:S(2)}) %collective-permute-start.70) | collective-permute-done | bytes 524320 | tf_op jit(solution)/shard_map/ppermute | solution.py:72
  648.6 6.9 collective-permute-start.75
  655.6 4.1 add_convert_fusion
  681.4 5.5 collective-permute-done.83
  686.9 4.3 collective-permute-done.80.refs_2_
  693.5 4.7 fusion.216
  703.2 4.9 collective-permute-start.86
  720.8 7.7 collective-permute-done.87.refs_6_
  729.0 5.7 collective-permute-start.91
  750.5 7.4 collective-permute-done.90
  757.9 23.4 %collective-permute-done.89 = bf16[128,2048]{1,0:T(8,128)(2,1)S(1)} collective-permute-done((bf16[128,2048]{1,0:T(8,128)(2,1)S(1)}, bf16[128,2048]{1,0:T(8,128)(2,1)S(1)}, u32[]{:S(2)}, u32[]{:S(2)}) %collective-permute-start.89) | collective-permute-done | bytes 524320 | tf_op jit(solution)/shard_map/ppermute | solution.py:72
  784.5 6.9 shard_map.312
  796.1 8.5 collective-permute-done.92
  816.4 10.6 %collective-permute-done.94 = bf16[656,768]{1,0:T(8,128)(2,1)S(1)} collective-permute-done((bf16[656,768]{1,0:T(8,128)(2,1)S(1)}, bf16[656,768]{1,0:T(8,128)(2,1)S(1)}, u32[]{:S(2)}, u32[]{:S(2)}) %collective-permute-start.94) | collective-permute-done | bytes 1007648 | tf_op jit(solution)/shard_map/ppermute | solution.py:72
  830.9 4.4 collective-permute-start.107
  845.5 4.2 shard_map.314
  866.8 8.1 collective-permute-done.99.refs_2_
  (960 shorter events, 406.0 us)
Async XLA Ops:
  9.5 35.9 %collective-permute-start.4 = (bf16[64,8192]{1,0:T(8,128)(2,1)S(1)}, bf16[64,8192]{1,0:T(8,128)(2,1)}, u32[]{:S(2)}, u32[]{:S(2)}) collective-permute-start(bf16[64,8192]{1,0:T(8,128)(2,1)S(1)} %convert_element_type.525.refs_0_), channel_id=1, source_target_pairs={{0,1},{1,0},{2,3},{3,2},{4,5},{5,4},{6,7},{7,6},{8,9},{9,8},{10,11... | collective-permute-start | bytes 3145736 | tf_op jit(solution)/shard_map/ppermute | solution.py:76
  9.7 35.7 %collective-permute-start.5 = (bf16[64,8192]{1,0:T(8,128)(2,1)S(1)}, bf16[64,8192]{1,0:T(8,128)(2,1)}, u32[]{:S(2)}, u32[]{:S(2)}) collective-permute-start(bf16[64,8192]{1,0:T(8,128)(2,1)S(1)} %convert_element_type.526.refs_1_), channel_id=1, source_target_pairs={{0,1},{1,0},{2,3},{3,2},{4,5},{5,4},{6,7},{7,6},{8,9},{9,8},{10,11... | collective-permute-start | bytes 3145736 | tf_op jit(solution)/shard_map/ppermute | solution.py:76
  23.0 22.4 %collective-permute-start.2 = (bf16[128,1152]{1,0:T(8,128)(2,1)}, bf16[128,1152]{1,0:T(8,128)(2,1)S(1)}, u32[]{:S(2)}, u32[]{:S(2)}) collective-permute-start(bf16[128,1152]{1,0:T(8,128)(2,1)} %get-tuple-element.249), channel_id=1, source_target_pairs={{0,16},{8,24},{16,0},{24,8},{1,17},{9,25},{17,1},{25,9},{2,18},{10... | collective-permute-start | bytes 884744 | tf_op jit(solution)/shard_map/ppermute | solution.py:72
  45.4 52.4 %collective-permute-start.6 = (bf16[128,2048]{1,0:T(8,128)(2,1)S(1)}, bf16[128,2048]{1,0:T(8,128)(2,1)}, u32[]{:S(2)}, u32[]{:S(2)}) collective-permute-start(bf16[128,2048]{1,0:T(8,128)(2,1)S(1)} %bitcast.290), channel_id=1, source_target_pairs={{0,24},{8,0},{16,8},{24,16},{1,25},{9,1},{17,9},{25,17},{2,26},{10... | collective-permute-start | bytes 1572872 | tf_op jit(solution)/shard_map/ppermute | solution.py:72
  52.4 46.2 %collective-permute-start.7 = (bf16[128,2048]{1,0:T(8,128)(2,1)S(1)}, bf16[128,2048]{1,0:T(8,128)(2,1)}, u32[]{:S(2)}, u32[]{:S(2)}) collective-permute-start(bf16[128,2048]{1,0:T(8,128)(2,1)S(1)} %bitcast.291), channel_id=1, source_target_pairs={{0,16},{8,24},{16,0},{24,8},{1,17},{9,25},{17,1},{25,9},{2,18},{10... | collective-permute-start | bytes 1572872 | tf_op jit(solution)/shard_map/ppermute | solution.py:72
  53.2 45.3 %collective-permute-start.8 = (bf16[128,2048]{1,0:T(8,128)(2,1)S(1)}, bf16[128,2048]{1,0:T(8,128)(2,1)}, u32[]{:S(2)}, u32[]{:S(2)}) collective-permute-start(bf16[128,2048]{1,0:T(8,128)(2,1)S(1)} %bitcast.292), channel_id=1, source_target_pairs={{0,8},{8,16},{16,24},{24,0},{1,9},{9,17},{17,25},{25,1},{2,10},{10... | collective-permute-start | bytes 1572872 | tf_op jit(solution)/shard_map/ppermute | solution.py:72
  56.3 26.5 %collective-permute-start.9 = (bf16[512,1152]{1,0:T(8,128)(2,1)}, bf16[512,1152]{1,0:T(8,128)(2,1)}, u32[]{:S(2)}, u32[]{:S(2)}) collective-permute-start(bf16[512,1152]{1,0:T(8,128)(2,1)} %shard_map.298.refs_0_), channel_id=1, source_target_pairs={{0,2},{2,0},{1,3},{3,1},{4,6},{6,4},{5,7},{7,5},{8,10},{10,8},{9,1... | collective-permute-start | bytes 3538952 | tf_op jit(solution)/shard_map/ppermute | solution.py:72
  57.5 28.5 %collective-permute-start.10 = (bf16[512,1152]{1,0:T(8,128)(2,1)}, bf16[512,1152]{1,0:T(8,128)(2,1)S(1)}, u32[]{:S(2)}, u32[]{:S(2)}) collective-permute-start(bf16[512,1152]{1,0:T(8,128)(2,1)} %shard_map.298.refs_0_), channel_id=1, source_target_pairs={{0,4},{4,0},{1,5},{5,1},{2,6},{6,2},{3,7},{7,3},{8,12},{12,8},{9,1... | collective-permute-start | bytes 3538952 | tf_op jit(solution)/shard_map/ppermute | solution.py:72
  102.6 23.9 %collective-permute-start.15 = (bf16[512,2048]{1,0:T(8,128)(2,1)}, bf16[512,2048]{1,0:T(8,128)(2,1)}, u32[]{:S(2)}, u32[]{:S(2)}) collective-permute-start(bf16[512,2048]{1,0:T(8,128)(2,1)} %shard_map.301), channel_id=1, source_target_pairs={{0,1},{1,0},{2,3},{3,2},{4,5},{5,4},{6,7},{7,6},{8,9},{9,8},{10,11... | collective-permute-start | bytes 6291464 | tf_op jit(solution)/shard_map/ppermute | solution.py:76
  114.4 24.9 %collective-permute-start.19 = (bf16[64,2048]{1,0:T(8,128)(2,1)S(1)}, bf16[64,2048]{1,0:T(8,128)(2,1)}, u32[]{:S(2)}, u32[]{:S(2)}) collective-permute-start(bf16[64,2048]{1,0:T(8,128)(2,1)S(1)} %convert_element_type.539.refs_0_), channel_id=1, source_target_pairs={{0,2},{2,0},{1,3},{3,1},{4,6},{6,4},{5,7},{7,5},{8,10},{10,8},{9,1... | collective-permute-start | bytes 786440 | tf_op jit(solution)/shard_map/ppermute | solution.py:72
  115.7 23.6 %collective-permute-start.20 = (bf16[64,2048]{1,0:T(8,128)(2,1)S(1)}, bf16[64,2048]{1,0:T(8,128)(2,1)}, u32[]{:S(2)}, u32[]{:S(2)}) collective-permute-start(bf16[64,2048]{1,0:T(8,128)(2,1)S(1)} %convert_element_type.539.refs_0_), channel_id=1, source_target_pairs={{0,4},{4,0},{1,5},{5,1},{2,6},{6,2},{3,7},{7,3},{8,12},{12,8},{9,1... | collective-permute-start | bytes 786440 | tf_op jit(solution)/shard_map/ppermute | solution.py:72
  115.9 22.0 %collective-permute-start.16 = (bf16[128,1024]{1,0:T(8,128)(2,1)}, bf16[128,1024]{1,0:T(8,128)(2,1)}, u32[]{:S(2)}, u32[]{:S(2)}) collective-permute-start(bf16[128,1024]{1,0:T(8,128)(2,1)} %get-tuple-element.286), channel_id=1, source_target_pairs={{0,8},{8,16},{16,24},{24,0},{1,9},{9,17},{17,25},{25,1},{2,10},{10... | collective-permute-start | bytes 786440 | tf_op jit(solution)/shard_map/ppermute | solution.py:72
  140.0 22.5 %collective-permute-start.21 = (bf16[512,512]{1,0:T(8,128)(2,1)S(1)}, bf16[512,512]{1,0:T(8,128)(2,1)}, u32[]{:S(2)}, u32[]{:S(2)}) collective-permute-start(bf16[512,512]{1,0:T(8,128)(2,1)S(1)} %get-tuple-element.670), channel_id=1, source_target_pairs={{0,4},{4,0},{1,5},{5,1},{2,6},{6,2},{3,7},{7,3},{8,12},{12,8},{9,1... | collective-permute-start | bytes 1572872 | tf_op jit(solution)/shard_map/ppermute | solution.py:72
  177.9 26.9 %collective-permute-start.26 = (bf16[512,2048]{1,0:T(8,128)(2,1)}, bf16[512,2048]{1,0:T(8,128)(2,1)}, u32[]{:S(2)}, u32[]{:S(2)}) collective-permute-start(bf16[512,2048]{1,0:T(8,128)(2,1)} %convolution_convert_fusion.1), channel_id=1, source_target_pairs={{0,1},{1,0},{2,3},{3,2},{4,5},{5,4},{6,7},{7,6},{8,9},{9,8},{10,11... | collective-permute-start | bytes 6291464 | tf_op jit(solution)/shard_map/ppermute | solution.py:76
  207.3 53.6 %collective-permute-start.33 = (bf16[512,2048]{1,0:T(8,128)(2,1)S(1)}, bf16[512,2048]{1,0:T(8,128)(2,1)S(1)}, u32[]{:S(2)}, u32[]{:S(2)}) collective-permute-start(bf16[512,2048]{1,0:T(8,128)(2,1)S(1)} %copy-done.38), channel_id=1, source_target_pairs={{0,2},{2,0},{1,3},{3,1},{4,6},{6,4},{5,7},{7,5},{8,10},{10,8},{9,1... | collective-permute-start | bytes 6291464 | tf_op jit(solution)/shard_map/ppermute | solution.py:72
  207.7 53.3 %collective-permute-start.34 = (bf16[512,2048]{1,0:T(8,128)(2,1)S(1)}, bf16[512,2048]{1,0:T(8,128)(2,1)S(1)}, u32[]{:S(2)}, u32[]{:S(2)}) collective-permute-start(bf16[512,2048]{1,0:T(8,128)(2,1)S(1)} %copy-done.38), channel_id=1, source_target_pairs={{0,4},{4,0},{1,5},{5,1},{2,6},{6,2},{3,7},{7,3},{8,12},{12,8},{9,1... | collective-permute-start | bytes 6291464 | tf_op jit(solution)/shard_map/ppermute | solution.py:72
  217.8 22.3 %collective-permute-start.31 = (bf16[128,2048]{1,0:T(8,128)(2,1)S(1)}, bf16[128,2048]{1,0:T(8,128)(2,1)S(1)}, u32[]{:S(2)}, u32[]{:S(2)}) collective-permute-start(bf16[128,2048]{1,0:T(8,128)(2,1)S(1)} %get-tuple-element.627), channel_id=1, source_target_pairs={{0,8},{8,16},{16,24},{24,0},{1,9},{9,17},{17,25},{25,1},{2,10},{10... | collective-permute-start | bytes 1572872 | tf_op jit(solution)/shard_map/ppermute | solution.py:72
  217.8 42.8 %collective-permute-start.30 = (bf16[128,2048]{1,0:T(8,128)(2,1)S(1)}, bf16[128,2048]{1,0:T(8,128)(2,1)S(1)}, u32[]{:S(2)}, u32[]{:S(2)}) collective-permute-start(bf16[128,2048]{1,0:T(8,128)(2,1)S(1)} %get-tuple-element.625), channel_id=1, source_target_pairs={{0,16},{8,24},{16,0},{24,8},{1,17},{9,25},{17,1},{25,9},{2,18},{10... | collective-permute-start | bytes 1572872 | tf_op jit(solution)/shard_map/ppermute | solution.py:72
  261.2 22.6 %collective-permute-start.39 = (bf16[256,2048]{1,0:T(8,128)(2,1)S(1)}, bf16[256,2048]{1,0:T(8,128)(2,1)S(1)}, u32[]{:S(2)}, u32[]{:S(2)}) collective-permute-start(bf16[256,2048]{1,0:T(8,128)(2,1)S(1)} %slice.610), channel_id=1, source_target_pairs={{0,2},{2,0},{1,3},{3,1},{4,6},{6,4},{5,7},{7,5},{8,10},{10,8},{9,1... | collective-permute-start | bytes 3145736 | tf_op jit(solution)/shard_map/ppermute | solution.py:72
  263.2 22.2 %collective-permute-start.35 = (bf16[128,2048]{1,0:T(8,128)(2,1)S(1)}, bf16[128,2048]{1,0:T(8,128)(2,1)S(1)}, u32[]{:S(2)}, u32[]{:S(2)}) collective-permute-start(bf16[128,2048]{1,0:T(8,128)(2,1)S(1)} %multiply_convert_fusion.5.refs_0_), channel_id=1, source_target_pairs={{0,24},{8,0},{16,8},{24,16},{1,25},{9,1},{17,9},{25,17},{2,26},{10... | collective-permute-start | bytes 1572872 | tf_op jit(solution)/shard_map/ppermute | solution.py:72
  265.4 56.9 %collective-permute-start.38 = (bf16[256,2048]{1,0:T(8,128)(2,1)S(1)}, bf16[256,2048]{1,0:T(8,128)(2,1)S(1)}, u32[]{:S(2)}, u32[]{:S(2)}) collective-permute-start(bf16[256,2048]{1,0:T(8,128)(2,1)S(1)} %slice.609), channel_id=1, source_target_pairs={{0,4},{4,0},{1,5},{5,1},{2,6},{6,2},{3,7},{7,3},{8,12},{12,8},{9,1... | collective-permute-start | bytes 3145736 | tf_op jit(solution)/shard_map/ppermute | solution.py:72
  283.9 38.4 %collective-permute-start.40 = (bf16[256,2048]{1,0:T(8,128)(2,1)S(1)}, bf16[256,2048]{1,0:T(8,128)(2,1)S(1)}, u32[]{:S(2)}, u32[]{:S(2)}) collective-permute-start(bf16[256,2048]{1,0:T(8,128)(2,1)S(1)} %convert_element_type.551.refs_0_), channel_id=1, source_target_pairs={{0,2},{2,0},{1,3},{3,1},{4,6},{6,4},{5,7},{7,5},{8,10},{10,8},{9,1... | collective-permute-start | bytes 3145736 | tf_op jit(solution)/shard_map/ppermute | solution.py:72
  285.2 38.4 %collective-permute-start.41 = (bf16[256,2048]{1,0:T(8,128)(2,1)S(1)}, bf16[256,2048]{1,0:T(8,128)(2,1)}, u32[]{:S(2)}, u32[]{:S(2)}) collective-permute-start(bf16[256,2048]{1,0:T(8,128)(2,1)S(1)} %convert_element_type.551.refs_0_), channel_id=1, source_target_pairs={{0,4},{4,0},{1,5},{5,1},{2,6},{6,2},{3,7},{7,3},{8,12},{12,8},{9,1... | collective-permute-start | bytes 3145736 | tf_op jit(solution)/shard_map/ppermute | solution.py:72
  285.4 36.9 %collective-permute-start.36 = (bf16[128,2048]{1,0:T(8,128)(2,1)S(1)}, bf16[128,2048]{1,0:T(8,128)(2,1)S(1)}, u32[]{:S(2)}, u32[]{:S(2)}) collective-permute-start(bf16[128,2048]{1,0:T(8,128)(2,1)S(1)} %multiply_convert_fusion.5.refs_0_), channel_id=1, source_target_pairs={{0,16},{8,24},{16,0},{24,8},{1,17},{9,25},{17,1},{25,9},{2,18},{10... | collective-permute-start | bytes 1572872 | tf_op jit(solution)/shard_map/ppermute | solution.py:72
  285.4 36.9 %collective-permute-start.37 = (bf16[128,2048]{1,0:T(8,128)(2,1)S(1)}, bf16[128,2048]{1,0:T(8,128)(2,1)S(1)}, u32[]{:S(2)}, u32[]{:S(2)}) collective-permute-start(bf16[128,2048]{1,0:T(8,128)(2,1)S(1)} %multiply_convert_fusion.5.refs_0_), channel_id=1, source_target_pairs={{0,8},{8,16},{16,24},{24,0},{1,9},{9,17},{17,25},{25,1},{2,10},{10... | collective-permute-start | bytes 1572872 | tf_op jit(solution)/shard_map/ppermute | solution.py:72
  327.1 22.7 %collective-permute-start.44 = (bf16[512,2048]{1,0:T(8,128)(2,1)}, bf16[512,2048]{1,0:T(8,128)(2,1)}, u32[]{:S(2)}, u32[]{:S(2)}) collective-permute-start(bf16[512,2048]{1,0:T(8,128)(2,1)} %shard_map.305.refs_0_), channel_id=1, source_target_pairs={{0,1},{1,0},{2,3},{3,2},{4,5},{5,4},{6,7},{7,6},{8,9},{9,8},{10,11... | collective-permute-start | bytes 6291464 | tf_op jit(solution)/shard_map/ppermute | solution.py:76
  377.1 24.0 %collective-permute-start.47 = (bf16[128,2048]{1,0:T(8,128)(2,1)}, bf16[128,2048]{1,0:T(8,128)(2,1)}, u32[]{:S(2)}, u32[]{:S(2)}) collective-permute-start(bf16[128,2048]{1,0:T(8,128)(2,1)} %get-tuple-element.624), channel_id=1, source_target_pairs={{0,8},{8,16},{16,24},{24,0},{1,9},{9,17},{17,25},{25,1},{2,10},{10... | collective-permute-start | bytes 1572872 | tf_op jit(solution)/shard_map/ppermute | solution.py:72
  378.7 43.9 %collective-permute-start.46 = (bf16[128,2048]{1,0:T(8,128)(2,1)}, bf16[128,2048]{1,0:T(8,128)(2,1)}, u32[]{:S(2)}, u32[]{:S(2)}) collective-permute-start(bf16[128,2048]{1,0:T(8,128)(2,1)} %get-tuple-element.622), channel_id=1, source_target_pairs={{0,16},{8,24},{16,0},{24,8},{1,17},{9,25},{17,1},{25,9},{2,18},{10... | collective-permute-start | bytes 1572872 | tf_op jit(solution)/shard_map/ppermute | solution.py:72
  380.3 44.4 %collective-permute-start.49 = (bf16[1024,512]{1,0:T(8,128)(2,1)}, bf16[1024,512]{1,0:T(8,128)(2,1)S(1)}, u32[]{:S(2)}, u32[]{:S(2)}) collective-permute-start(bf16[1024,512]{1,0:T(8,128)(2,1)} %pad_maximum_fusion.9), channel_id=1, source_target_pairs={{0,1},{1,0},{2,3},{3,2},{4,5},{5,4},{6,7},{7,6},{8,9},{9,8},{10,11... | collective-permute-start | bytes 3145736 | tf_op jit(solution)/shard_map/ppermute | solution.py:76
  444.8 42.1 %collective-permute-start.51 = (bf16[128,2048]{1,0:T(8,128)(2,1)S(1)}, bf16[128,2048]{1,0:T(8,128)(2,1)S(1)}, u32[]{:S(2)}, u32[]{:S(2)}) collective-permute-start(bf16[128,2048]{1,0:T(8,128)(2,1)S(1)} %fusion.44.refs_0_), channel_id=1, source_target_pairs={{0,16},{8,24},{16,0},{24,8},{1,17},{9,25},{17,1},{25,9},{2,18},{10... | collective-permute-start | bytes 1572872 | tf_op jit(solution)/shard_map/ppermute | solution.py:72
  444.8 42.1 %collective-permute-start.52 = (bf16[128,2048]{1,0:T(8,128)(2,1)S(1)}, bf16[128,2048]{1,0:T(8,128)(2,1)S(1)}, u32[]{:S(2)}, u32[]{:S(2)}) collective-permute-start(bf16[128,2048]{1,0:T(8,128)(2,1)S(1)} %fusion.44.refs_0_), channel_id=1, source_target_pairs={{0,8},{8,16},{16,24},{24,0},{1,9},{9,17},{17,25},{25,1},{2,10},{10... | collective-permute-start | bytes 1572872 | tf_op jit(solution)/shard_map/ppermute | solution.py:72
  540.8 38.4 %collective-permute-start.64 = (bf16[128,2048]{1,0:T(8,128)(2,1)}, bf16[128,2048]{1,0:T(8,128)(2,1)}, u32[]{:S(2)}, u32[]{:S(2)}) collective-permute-start(bf16[128,2048]{1,0:T(8,128)(2,1)} %get-tuple-element.614), channel_id=1, source_target_pairs={{0,24},{8,0},{16,8},{24,16},{1,25},{9,1},{17,9},{25,17},{2,26},{10... | collective-permute-start | bytes 1572872 | tf_op jit(solution)/shard_map/ppermute | solution.py:72
  540.8 39.4 %collective-permute-start.63 = (bf16[128,2048]{1,0:T(8,128)(2,1)}, bf16[128,2048]{1,0:T(8,128)(2,1)}, u32[]{:S(2)}, u32[]{:S(2)}) collective-permute-start(bf16[128,2048]{1,0:T(8,128)(2,1)} %get-tuple-element.615), channel_id=1, source_target_pairs={{0,8},{8,16},{16,24},{24,0},{1,9},{9,17},{17,25},{25,1},{2,10},{10... | collective-permute-start | bytes 1572872 | tf_op jit(solution)/shard_map/ppermute | solution.py:72
  542.3 44.3 %collective-permute-start.62 = (bf16[128,2048]{1,0:T(8,128)(2,1)}, bf16[128,2048]{1,0:T(8,128)(2,1)}, u32[]{:S(2)}, u32[]{:S(2)}) collective-permute-start(bf16[128,2048]{1,0:T(8,128)(2,1)} %get-tuple-element.613), channel_id=1, source_target_pairs={{0,16},{8,24},{16,0},{24,8},{1,17},{9,25},{17,1},{25,9},{2,18},{10... | collective-permute-start | bytes 1572872 | tf_op jit(solution)/shard_map/ppermute | solution.py:72
  555.1 23.1 %collective-permute-start.65 = (bf16[256,2048]{1,0:T(8,128)(2,1)S(1)}, bf16[256,2048]{1,0:T(8,128)(2,1)S(1)}, u32[]{:S(2)}, u32[]{:S(2)}) collective-permute-start(bf16[256,2048]{1,0:T(8,128)(2,1)S(1)} %get-tuple-element.612), channel_id=1, source_target_pairs={{0,2},{2,0},{1,3},{3,1},{4,6},{6,4},{5,7},{7,5},{8,10},{10,8},{9,1... | collective-permute-start | bytes 3145736 | tf_op jit(solution)/shard_map/ppermute | solution.py:72
  556.0 32.6 %collective-permute-start.66 = (bf16[256,2048]{1,0:T(8,128)(2,1)S(1)}, bf16[256,2048]{1,0:T(8,128)(2,1)S(1)}, u32[]{:S(2)}, u32[]{:S(2)}) collective-permute-start(bf16[256,2048]{1,0:T(8,128)(2,1)S(1)} %get-tuple-element.611), channel_id=1, source_target_pairs={{0,4},{4,0},{1,5},{5,1},{2,6},{6,2},{3,7},{7,3},{8,12},{12,8},{9,1... | collective-permute-start | bytes 3145736 | tf_op jit(solution)/shard_map/ppermute | solution.py:72
  593.9 28.5 %collective-permute-start.69 = (bf16[128,2048]{1,0:T(8,128)(2,1)}, bf16[128,2048]{1,0:T(8,128)(2,1)}, u32[]{:S(2)}, u32[]{:S(2)}) collective-permute-start(bf16[128,2048]{1,0:T(8,128)(2,1)} %fusion.46.refs_0_), channel_id=1, source_target_pairs={{0,24},{8,0},{16,8},{24,16},{1,25},{9,1},{17,9},{25,17},{2,26},{10... | collective-permute-start | bytes 1572872 | tf_op jit(solution)/shard_map/ppermute | solution.py:72
  596.7 43.2 %collective-permute-start.70 = (bf16[128,2048]{1,0:T(8,128)(2,1)}, bf16[128,2048]{1,0:T(8,128)(2,1)}, u32[]{:S(2)}, u32[]{:S(2)}) collective-permute-start(bf16[128,2048]{1,0:T(8,128)(2,1)} %fusion.46.refs_0_), channel_id=1, source_target_pairs={{0,16},{8,24},{16,0},{24,8},{1,17},{9,25},{17,1},{25,9},{2,18},{10... | collective-permute-start | bytes 1572872 | tf_op jit(solution)/shard_map/ppermute | solution.py:72
  599.5 43.3 %collective-permute-start.72 = (bf16[512,2048]{1,0:T(8,128)(2,1)}, bf16[512,2048]{1,0:T(8,128)(2,1)}, u32[]{:S(2)}, u32[]{:S(2)}) collective-permute-start(bf16[512,2048]{1,0:T(8,128)(2,1)} %pad_maximum_fusion.3), channel_id=1, source_target_pairs={{0,4},{4,0},{1,5},{5,1},{2,6},{6,2},{3,7},{7,3},{8,12},{12,8},{9,1... | collective-permute-start | bytes 6291464 | tf_op jit(solution)/shard_map/ppermute | solution.py:72
  602.6 43.0 %collective-permute-start.73 = (bf16[512,2048]{1,0:T(8,128)(2,1)}, bf16[512,2048]{1,0:T(8,128)(2,1)}, u32[]{:S(2)}, u32[]{:S(2)}) collective-permute-start(bf16[512,2048]{1,0:T(8,128)(2,1)} %pad_maximum_fusion.4), channel_id=1, source_target_pairs={{0,2},{2,0},{1,3},{3,1},{4,6},{6,4},{5,7},{7,5},{8,10},{10,8},{9,1... | collective-permute-start | bytes 6291464 | tf_op jit(solution)/shard_map/ppermute | solution.py:72
  611.8 28.1 %collective-permute-start.71 = (bf16[128,2048]{1,0:T(8,128)(2,1)}, bf16[128,2048]{1,0:T(8,128)(2,1)}, u32[]{:S(2)}, u32[]{:S(2)}) collective-permute-start(bf16[128,2048]{1,0:T(8,128)(2,1)} %fusion.46.refs_0_), channel_id=1, source_target_pairs={{0,8},{8,16},{16,24},{24,0},{1,9},{9,17},{17,25},{25,1},{2,10},{10... | collective-permute-start | bytes 1572872 | tf_op jit(solution)/shard_map/ppermute | solution.py:72
  622.4 59.0 %collective-permute-start.82 = (bf16[256,2048]{1,0:T(8,128)(2,1)}, bf16[256,2048]{1,0:T(8,128)(2,1)}, u32[]{:S(2)}, u32[]{:S(2)}) collective-permute-start(bf16[256,2048]{1,0:T(8,128)(2,1)} %pad_maximum_fusion.12), channel_id=1, source_target_pairs={{0,4},{4,0},{1,5},{5,1},{2,6},{6,2},{3,7},{7,3},{8,12},{12,8},{9,1... | collective-permute-start | bytes 3145736 | tf_op jit(solution)/shard_map/ppermute | solution.py:72
  662.1 24.9 %collective-permute-start.83 = (bf16[256,2048]{1,0:T(8,128)(2,1)S(1)}, bf16[256,2048]{1,0:T(8,128)(2,1)S(1)}, u32[]{:S(2)}, u32[]{:S(2)}) collective-permute-start(bf16[256,2048]{1,0:T(8,128)(2,1)S(1)} %pad_maximum_fusion.13), channel_id=1, source_target_pairs={{0,2},{2,0},{1,3},{3,1},{4,6},{6,4},{5,7},{7,5},{8,10},{10,8},{9,1... | collective-permute-start | bytes 3145736 | tf_op jit(solution)/shard_map/ppermute | solution.py:72
  665.1 21.8 %collective-permute-start.79 = (bf16[64,2048]{1,0:T(8,128)(2,1)S(1)}, bf16[64,2048]{1,0:T(8,128)(2,1)S(1)}, u32[]{:S(2)}, u32[]{:S(2)}) collective-permute-start(bf16[64,2048]{1,0:T(8,128)(2,1)S(1)} %get-tuple-element.659), channel_id=1, source_target_pairs={{0,8},{8,16},{16,24},{24,0},{1,9},{9,17},{17,25},{25,1},{2,10},{10... | collective-permute-start | bytes 786440 | tf_op jit(solution)/shard_map/ppermute | solution.py:72
  729.0 21.6 %collective-permute-start.91 = (bf16[128,2048]{1,0:T(8,128)(2,1)S(1)}, bf16[128,2048]{1,0:T(8,128)(2,1)S(1)}, u32[]{:S(2)}, u32[]{:S(2)}) collective-permute-start(bf16[128,2048]{1,0:T(8,128)(2,1)S(1)} %get-tuple-element.593), channel_id=1, source_target_pairs={{0,24},{8,0},{16,8},{24,16},{1,25},{9,1},{17,9},{25,17},{2,26},{10... | collective-permute-start | bytes 1572872 | tf_op jit(solution)/shard_map/ppermute | solution.py:72
  734.7 23.3 %collective-permute-start.90 = (bf16[128,2048]{1,0:T(8,128)(2,1)S(1)}, bf16[128,2048]{1,0:T(8,128)(2,1)S(1)}, u32[]{:S(2)}, u32[]{:S(2)}) collective-permute-start(bf16[128,2048]{1,0:T(8,128)(2,1)S(1)} %get-tuple-element.594), channel_id=1, source_target_pairs={{0,8},{8,16},{16,24},{24,0},{1,9},{9,17},{17,25},{25,1},{2,10},{10... | collective-permute-start | bytes 1572872 | tf_op jit(solution)/shard_map/ppermute | solution.py:72
  735.2 46.2 %collective-permute-start.89 = (bf16[128,2048]{1,0:T(8,128)(2,1)S(1)}, bf16[128,2048]{1,0:T(8,128)(2,1)S(1)}, u32[]{:S(2)}, u32[]{:S(2)}) collective-permute-start(bf16[128,2048]{1,0:T(8,128)(2,1)S(1)} %get-tuple-element.592), channel_id=1, source_target_pairs={{0,16},{8,24},{16,0},{24,8},{1,17},{9,25},{17,1},{25,9},{2,18},{10... | collective-permute-start | bytes 1572872 | tf_op jit(solution)/shard_map/ppermute | solution.py:72
  835.9 22.8 %collective-permute-start.97 = (bf16[256,768]{1,0:T(8,128)(2,1)S(1)}, bf16[256,768]{1,0:T(8,128)(2,1)S(1)}, u32[]{:S(2)}, u32[]{:S(2)}) collective-permute-start(bf16[256,768]{1,0:T(8,128)(2,1)S(1)} %broadcast_select_fusion.14), channel_id=1, source_target_pairs={{0,1},{1,0},{2,3},{3,2},{4,5},{5,4},{6,7},{7,6},{8,9},{9,8},{10,11... | collective-permute-start | bytes 1179656 | tf_op jit(solution)/shard_map/ppermute | solution.py:76
  (275 other events, 2695.6 us)

commit v2 on v1

--- a/solution.py
+++ b/solution.py
@@ -133,14 +133,25 @@
 
         for a, r_in, c_in, o, r_out, c_out, height, wide in plan:
             from_row, from_column, to_row, to_column = at(r_in), at(c_in), at(r_out), at(c_out)
-            step = 16 if height % 32 else 32
-
-            @pl.loop(0, height // step)
-            def _(i):
-                low = pl.multiple_of(i * step, step)
+            step = 16
+            while height % (2 * step) == 0 and 2 * step * wide <= 65536:
+                step *= 2
+            chunks = height // step
+
+            def move(low):
                 made[o][pl.ds(to_row + low, step), pl.ds(to_column, wide)] = ins[a][
                     pl.ds(from_row + low, step), pl.ds(from_column, wide)
                 ]
+
+            if chunks % 4 or chunks <= 8:
+                for i in range(chunks):
+                    move(i * step)
+            else:
+
+                @pl.loop(0, chunks // 4)
+                def _(i):
+                    for j in range(4):
+                        move(pl.multiple_of(i * 4 * step, step) + j * step)
 
     moved = sum(height * wide for *_, height, wide in plan) * dtype.itemsize
     return pl.pallas_call(
@@ -231,23 +242,26 @@
 
 
 def sum_total(pieces, got):
+    return add_up([pieces[0]] + list(got))
+
+
+def core_sum(own, other):
+    total = own + swap_core(other.astype(BF)).astype(F32)
+    rows = total.shape[0] // Z
+    return [total[:rows]] + [
+        total[k * rows : (k + 1) * rows].astype(BF) for k in range(1, Z)
+    ]
+
+
+def z_shares(blocks):
+    return [blocks[0]] + [give_to(blocks[k], "z", Z, k) for k in range(1, Z)]
+
+
+def add_up(pieces):
     total = pieces[0].astype(F32)
-    for piece in got:
+    for piece in pieces[1:]:
         total = total + piece.astype(F32)
     return total
-
-
-def reduce_start(own, other):
-    return own + swap_core(other.astype(BF)).astype(F32)
-
-
-def reduce_end(total):
-    rows = total.shape[0] // Z
-    out = total[:rows]
-    for k in (2, 1, 3):
-        piece = total[k * rows : (k + 1) * rows].astype(BF)
-        out = out + give_to(piece, "z", Z, k).astype(F32)
-    return out
 
 
 def write_rows(pieces, starts):
@@ -382,24 +396,37 @@
     def z_block(value, k, height, axis=0):
         return lax.dynamic_slice_in_dim(value, (zi + k) % Z * height, height, axis=axis)
 
-    qkv_low = jnp.concatenate([w_query, w_key, w_value], axis=1).astype(BF)
-    qkv_got = swap_core(qkv_low)
     gain_pack = jnp.concatenate(
         [
             jnp.pad(norm_gains, ((0, 0), (0, lanes - shard))),
             jnp.pad(qk_gain, ((0, 0), (0, lanes - qk_shard))),
-            jnp.zeros((shard - gain_count - 2, lanes), F32),
         ],
         axis=0,
     )
+    gain_rows = gain_count + 2
+    qkv_low = jnp.concatenate(
+        [w_query, w_key, w_value, jnp.pad(gain_pack, ((0, shard - gain_rows), (0, 0)))], axis=1
+    ).astype(BF)
+    qkv_got = swap_core(qkv_low)
+    qkv_low, qkv_got, out_late = stage(qkv_low, qkv_got, w_out)
+
+    gain_low = (H + 2 * KVH) * HD
+    own_gain, other_gain = qkv_low[:gain_rows, gain_low:], qkv_got[:gain_rows, gain_low:]
+    gain_block = jnp.concatenate(
+        [
+            jnp.where(first, own_gain, other_gain),
+            jnp.where(first, other_gain, own_gain),
+            jnp.zeros((max(shard - C * gain_rows, 0), lanes), BF),
+        ],
+        axis=0,
+    )[:shard]
     misc = jnp.concatenate(
         [
-            jnp.concatenate([w_left, w_right.T, w_pgate], axis=1),
-            jnp.concatenate([gain_pack, w_pproj.T], axis=1),
+            jnp.concatenate([w_left, w_right.T, w_pgate], axis=1).astype(BF),
+            jnp.concatenate([gain_block, w_pproj.T.astype(BF)], axis=1),
         ],
         axis=0,
-    ).astype(BF)
-
+    )
     copies = []
     for k in range(Z):
         z_to = (zi + k) % Z
@@ -413,28 +440,35 @@
         [qkv_low, qkv_got, misc], [(unit, span + misc.shape[1])] * Z, copies
     )
     first_arrived = z_send(lambda k: first_sends[k])
-    gate_late, up_late, _ = stage(w_gate, w_up, qkv_got)
-    ff_low = [gate_late.astype(BF), up_late.astype(BF)]
-    ff_got = [swap_core(mat) for mat in ff_low]
-    own_tokens, pair_of, first_arrived, ff_low, ff_got = stage(
-        tokens[0], pair_of, first_arrived, ff_low, ff_got
+    gate_late, up_late, out_late, _ = stage(w_gate, w_up, out_late, first_sends)
+    ff_low = jnp.concatenate([gate_late, up_late], axis=1).astype(BF)
+    ff_got = swap_core(ff_low)
+    out_low = out_late.astype(BF)
+    out_x = give_to(out_low, "x", X, 1) if y_count == 2 else out_low
+    own_tokens, pair_of, first_arrived, ff_low, ff_got, out_low, out_x = stage(
+        tokens[0], pair_of, first_arrived, ff_low, ff_got, out_low, out_x
     )
 
     token_take = z_take(own_tokens)
     first_rows = z_place(first_arrived, zi)
-    first_got = gather_second(first_rows, gather_first(first_rows, y_count), y_count)
+    first_got = gather_first(first_rows, y_count)
     copies = []
     for m in range(2):
         for k in range(Z):
             for a in range(yx):
-                column = (((zi + k) % Z * yx + a) * C + ci, ff_shard)
-                to = (m * Z + k, a * ff_shard)
-                for source, c_from in ((m, ci), (2 + m, 1 - ci)):
+                column = (((m * Z + (zi + k) % Z) * yx + a) * C + ci, ff_shard)
+                for source, c_from in ((0, ci), (1, 1 - ci)):
                     copies.append(
-                        (source, 0, column, to[0], (c_from, shard), to[1], shard, ff_shard)
+                        (
+                            source, 0, column, m * Z + k, (c_from, shard), a * ff_shard,
+                            shard, ff_shard,
+                        )
                     )
-    ff_sends = shuffle(list(ff_low) + list(ff_got), [(unit, ff_own)] * (2 * Z), copies)
+    ff_sends = shuffle([ff_low, ff_got], [(unit, ff_own)] * (2 * Z), copies)
     ff_sends = [ff_sends[:Z], ff_sends[Z:]]
+    out_pair = stack_rows([out_low, out_x])
+    first_rows, first_got = stage(first_rows, first_got)
+    first_got = gather_second(first_rows, list(first_got), y_count)
 
     lengths = [doc_lengths[0], swap_core(doc_lengths)[0]]
     z_ids = (zi + jnp.arange(Z)) % Z
@@ -453,8 +487,10 @@
     frequency = ROPE_BASE ** (-2.0 * jnp.arange(HD // 2, dtype=F32) / HD)
     angles = relative.astype(F32)[:, None] * frequency[None, :]
     cos_tab, sine_tab = jnp.cos(angles), jnp.sin(angles)
-    token_take, first_rows, first_got, ff_sends, visible, cos_tab, sine_tab, w_out = stage(
-        token_take, first_rows, first_got, ff_sends, visible, cos_tab, sine_tab, w_out
+    (
+        token_take, first_rows, first_got, ff_sends, visible, cos_tab, sine_tab, out_pair
+    ) = stage(
+        token_take, first_rows, first_got, ff_sends, visible, cos_tab, sine_tab, out_pair
     )
     visible = visible > 0.5
 
@@ -472,11 +508,11 @@
         first_got,
         [(0, span), (span, span + lanes), (span + lanes, span + lanes + ple)],
     )
-    misc_all = pair_cores(misc_all, unit)
-    gain_all = misc_all[:, :, shard : shard + gain_count + 2, :shard]
-    gain_all = gain_all.reshape(-1, gain_count + 2, shard).transpose(1, 0, 2)
+    gain_all = misc_all.reshape(-1, unit, lanes)[:, shard : shard + C * gain_rows, :shard]
+    gain_all = gain_all.reshape(-1, gain_rows, shard).transpose(1, 0, 2)
     gains = gain_all[:gain_count].reshape(gain_count, -1).astype(F32)
     qk = gain_all[gain_count:, :, :qk_shard].reshape(2, -1).astype(F32)
+    lr_own = misc_all.reshape(-1, unit, lanes)[:, :shard].reshape(-1, lanes)
     unit_own = unit_norm(token_own.astype(F32))
     unit_other = unit_norm(token_other.astype(F32))
     normed_own = (unit_own * gains[0]).astype(BF)
@@ -487,34 +523,44 @@
     key = rotated(k_raw, qk[1]).astype(BF)
     value = unit_norm(v_raw).astype(BF)
     kv = jnp.concatenate([key, value], axis=-1).reshape(C, group_rows, 2 * HD)
-    out_low = w_out.astype(BF)
-    out_got = gather_first(out_low, y_count)
-    kv, query, gate_arrived, out_low, out_got, misc_all, small_late = stage(
-        kv,
-        query,
-        gate_arrived,
-        out_low,
-        out_got,
-        misc_all,
-        small_late,
-    )
-
+    out_y = give_to(out_pair, "y", 2, 1) if y_count == 2 else out_pair
+    kv, query, gate_arrived, out_pair, out_y, lr_own, small_own = stage(
+        kv, query, gate_arrived, out_pair, out_y, lr_own, small_late
+    )
+
+    kv_own = [kv[0]] + [give_to(kv[0], "y", y_count, -k) for k in range(1, y_count)]
+    lr_other = swap_core(lr_own)
+    small_other = swap_core(small_own)
+    if y_count == 2:
+        copies = []
+        for p in range(yx):
+            copies.append(
+                (p // X, p % X * shard, 0, 0, (places_yx[p], shard), 0, shard, width)
+            )
+        out_rows = shuffle([out_pair, out_y], [(yx * shard, width)], copies)[0]
+        out_half = yx // 2 * shard
+        out_got = swap_core(lax.dynamic_slice_in_dim(out_rows, (1 - ci) * out_half, out_half))
+    else:
+        out_rows = lax.all_gather(out_pair[:shard], ("y", "x", "c"), axis=0, tiled=True)
+        out_got = out_rows
+    kv_own, lr_other, small_other, out_rows, out_got = stage(
+        kv_own, lr_other, small_other, out_rows, out_got
+    )
+
+    if y_count == 2:
+        copies = []
+        for a in range(yx // 2):
+            copies.append(
+                (0, (ci * (yx // 2) + a, shard), 0, 0, (a * C + ci, shard), 0, shard, width)
+            )
+            copies.append((1, a * shard, 0, 0, (a * C + 1 - ci, shard), 0, shard, width))
+        out_mat = shuffle([out_rows, out_got], [(HD, width)], copies)[0]
+    else:
+        out_mat = lax.dynamic_slice_in_dim(out_rows, ci * HD, HD)
     up_arrived = z_send(lambda k: ff_sends[1][k])
-    kv_own, kv_other = [kv[0]], [kv[1]]
-    for k in range(1, y_count):
-        piece = give_to(kv[0], "y", y_count, -k)
-        kv_own.append(piece)
-        kv_other.append(swap_core(piece))
+    kv_other = [kv[1]] + [swap_core(piece) for piece in kv_own[1:]]
     kv_all = jnp.stack([jnp.concatenate(kv_own), jnp.concatenate(kv_other)])
     key_all, value_all = kv_all[..., :HD], kv_all[..., HD:]
-    out_rows = place_blocks(out_low, gather_second(out_low, out_got, y_count), shard)
-    out_half = yx // 2 * shard
-    out_got = swap_core(lax.dynamic_slice_in_dim(out_rows, (1 - ci) * out_half, out_half))
-    copies = []
-    for a in range(yx // 2):
-        copies.append((0, (ci * (yx // 2) + a, shard), 0, 0, (a * C + ci, shard), 0, shard, width))
-        copies.append((1, a * shard, 0, 0, (a * C + 1 - ci, shard), 0, shard, width))
-    out_mat = shuffle([out_rows, out_got], [(HD, width)], copies)[0]
     scores = jnp.einsum("sqd,skd->sqk", query, key_all, preferred_element_type=F32)
     scores = jnp.where(visible, scores, MASKED)
     top = jnp.max(scores, axis=-1, keepdims=True)
@@ -523,21 +569,30 @@
     probs_low = probs.astype(BF)
     head_out = jnp.einsum("sqk,skd->sqd", probs_low, value_all, preferred_element_type=F32)
     heads_low = head_out.astype(BF).reshape(C * group_rows, HD)
-    heads_share = times(heads_low[group_rows:], out_mat)
-    projected = reduce_start(times(heads_low[:group_rows], out_mat), heads_share)
+    heads_low, up_arrived, out_mat = stage(heads_low, up_arrived, out_mat)
+
     copies = [
         (m * Z + k, 0, 0, 0, ((zi - k) % Z, unit), m * ff_own, unit, ff_own)
         for m in range(2)
         for k in range(Z)
     ]
-    gu_rows = shuffle(list(gate_arrived) + up_arrived, [(tall, 2 * ff_own)], copies)[0]
-    projected, gu_rows, heads_low, misc_all, own_tokens, small_late = stage(
-        projected, gu_rows, heads_low, misc_all, own_tokens, small_late
-    )
-
-    projected = reduce_end(projected)
+    heads_share = times(heads_low[group_rows:], out_mat)
+    gu_rows = shuffle(list(gate_arrived) + list(up_arrived), [(tall, 2 * ff_own)], copies)[0]
+    blocks = core_sum(times(heads_low[:group_rows], out_mat), heads_share)
+    blocks, gu_rows, lr_own, lr_other, own_tokens, heads_low = stage(
+        blocks, gu_rows, lr_own, lr_other, own_tokens, heads_low
+    )
+    shares = z_shares(blocks)
     gu_got = gather_first(gu_rows, y_count)
-    lr_mat = misc_all[:, :, :shard].reshape(-1, lanes)
+
+    def core_rows(own, other):
+        last = own.shape[1]
+        cores = [jnp.where(first, own, other), jnp.where(first, other, own)]
+        return jnp.concatenate(
+            [core.reshape(-1, 1, shard, last) for core in cores], axis=1
+        ).reshape(-1, last)
+
+    lr_mat = core_rows(lr_own, lr_other)
     left_mat, right_mat = lr_mat[:, :left_rank], lr_mat[:, left_rank:]
     token_vals = own_tokens.astype(F32)
     normed = rms_norm(token_vals, gains[0])
@@ -545,42 +600,91 @@
     left_low = times(normed_low, left_mat).astype(BF)
     right_out = times_t(left_low, right_mat)
     laurel = normed + rms_norm(right_out, gains[2])
-    projected, gu_rows, gu_got, laurel, down_late = stage(
-        projected, gu_rows, gu_got, laurel, w_down
-    )
-
+    shares, gu_rows, gu_got, laurel, w_down = stage(shares, gu_rows, gu_got, laurel, w_down)
+
+    projected = add_up(shares)
     gated_sum = token_vals + rms_norm(projected, gains[1])
     joined = (gated_sum + laurel) * HALF_ROOT
     ff_in = rms_norm(joined, gains[3]).astype(BF)
+    ff_in, gu_got, gu_rows, w_down = stage(ff_in, gu_got, gu_rows, w_down)
     ff_take = z_take(ff_in)
-    gu_got = gather_second(gu_rows, gu_got, y_count)
-    down_low = after(down_late, gu_got[-1]).astype(BF)
-    down_got = gather_first(down_low, y_count)
-    ff_take, gu_rows, gu_got, down_low, down_got = stage(
-        ff_take, gu_rows, gu_got, down_low, down_got
-    )
+    down_low = w_down.astype(BF)
+    if y_count == 2:
+        half = tall // 2
+        pass_y = shuffle(
+            [gu_got[0], down_low],
+            [(half + down_low.shape[0], width)],
+            [(0, 0, 0, 0, 0, 0, half, width), (1, 0, 0, 0, half, 0, *down_low.shape)],
+        )[0]
+        pass_x = shuffle(
+            [gu_got[1], down_low],
+            [(half + down_low.shape[0], width)],
+            [(0, half, 0, 0, 0, 0, half, width), (1, 0, 0, 0, half, 0, *down_low.shape)],
+        )[0]
+        passed = [give_to(pass_y, "y", 2, 1), give_to(pass_x, "x", X, 1)]
+    else:
+        passed = gather_first(down_low, y_count)
+    ff_take, gu_rows, gu_got, down_low, passed = stage(ff_take, gu_rows, gu_got, down_low, passed)
 
     ff_rows = stack_rows(ff_take)
     ff_halves = [ff_rows, swap_core(ff_rows)]
-    gu_mat = place_parts(gu_rows, gu_got, [(0, 2 * ff_own)])[0]
-    down_got = gather_second(down_low, down_got, y_count)
+    if y_count == 2:
+        edge = down_low.shape[0] // 2
+        down_far = [
+            give_to(passed[1][half : half + edge], "y", 2, 1),
+            give_to(passed[0][half + edge :], "x", X, 1),
+        ]
+        copies = []
+        sources = [[(0, 0)], [(1, 0)], [(2, 0)], [(3, 0), (4, 0)]]
+        for p in range(yx):
+            for z in range(Z):
+                part, low = sources[p][0] if p < 3 else sources[p][z * 2 // Z]
+                low = z * unit if p < 3 else (z * unit) % half
+                copies.append(
+                    (part, low, 0, 0, (z * yx + places_yx[p], unit), 0, unit, width)
+                )
+        gu_mat = shuffle(
+            [gu_rows, gu_got[0], gu_got[1], passed[0], passed[1]], [(Z * yx * unit, width)], copies
+        )[0]
+    else:
+        down_far = passed
+        gu_mat = place_parts(gu_rows, gu_got, [(0, 2 * ff_own)])[0]
     gate_proj, up_proj, hidden = [], [], []
-    for half in ff_halves:
-        gate_up = times(half, gu_mat)
+    for part in ff_halves:
+        gate_up = times(part, gu_mat)
         gate_proj.append(gate_up[:, :ff_own])
         up_proj.append(gate_up[:, ff_own:])
         hidden.append(glu_piece(gate_proj[-1], up_proj[-1]).astype(BF))
-    down_mat = place_blocks(down_low, down_got, ff_shard)
+    hidden, down_far = stage(hidden, down_far)
+
+    if y_count == 2:
+        copies = [
+            (0, 0, 0, 0, (places_yx[0], ff_shard), 0, ff_shard, width),
+            (2, half, 0, 0, (places_yx[1], ff_shard), 0, ff_shard, width),
+            (1, half, 0, 0, (places_yx[2], ff_shard), 0, ff_shard, width),
+            (3, 0, 0, 0, (places_yx[3] * 2, edge), 0, edge, width),
+            (4, 0, 0, 0, (places_yx[3] * 2 + 1, edge), 0, edge, width),
+        ]
+        down_mat = shuffle(
+            [down_low, passed[0], passed[1], down_far[0], down_far[1]],
+            [(yx * ff_shard, width)],
+            copies,
+        )[0]
+    else:
+        down_mat = place_blocks(down_low, down_far, ff_shard)
     down_share = times(hidden[1], down_mat)
-    down_proj = reduce_start(times(hidden[0], down_mat), down_share)
-    down_proj, small_late = stage(down_proj, small_late)
-
-    down_proj = reduce_end(down_proj)
-    ple_rows = small_late.reshape(-1, C, shard, ple)
-    ple_rows = jnp.concatenate([ple_rows[:, 0], ple_rows[:, 1]], axis=-1).reshape(-1, 2 * ple)
-    ple_mat = pair_cores(ple_rows, shard).reshape(-1, 2 * ple)
-    down_proj, ple_mat = stage(down_proj, ple_mat)
+    blocks = core_sum(times(hidden[0], down_mat), down_share)
+    blocks, small_own, small_other = stage(blocks, small_own, small_other)
+    shares = z_shares(blocks)
+
+    def small_rows(value):
+        value = value.reshape(-1, C, shard, ple)
+        return jnp.concatenate([value[:, 0], value[:, 1]], axis=-1).reshape(-1, 2 * ple)
+
+    ple_mat = core_rows(small_rows(small_own), small_rows(small_other))
+    shares, ple_mat = stage(shares, ple_mat)
     pgate_mat, pproj_mat = ple_mat[:, :ple], ple_mat[:, ple:]
+    down_proj = add_up(shares)
 
     extra_vals = layer_input[0].astype(F32)
     after_ff = joined + rms_norm(down_proj, gains[4])
@@ -615,26 +719,26 @@
             [over_rows(after_late, d_pgate_late), over_rows(d_per_late, per_mix_late)], axis=1
         ).astype(BF)
     )
-    ple_got = sum_second(ple_grads, sum_first(ple_grads, y_count), y_count)
-    ple_sum = sum_total(ple_grads, ple_got).astype(BF)
-    d_down_take, ple_sum = stage(d_down_take, ple_sum)
+    ple_got = sum_first(ple_grads, y_count)
+    d_down_take, ple_grads, ple_got = stage(d_down_take, ple_grads, ple_got)
 
     d_down_rows = stack_rows(d_down_take)
     d_down_halves = [d_down_rows, swap_core(d_down_rows)]
-    ple_arrived = z_send(lambda k: z_block(ple_sum, k, unit))
+    ple_got = sum_second(ple_grads, list(ple_got), y_count)
     d_gu_low = []
-    for half in range(C):
-        d_hidden = times_t(d_down_halves[half], down_mat)
-        _, glu_pull = jax.vjp(glu_piece, gate_proj[half], up_proj[half])
+    for h in range(C):
+        d_hidden = times_t(d_down_halves[h], down_mat)
+        _, glu_pull = jax.vjp(glu_piece, gate_proj[h], up_proj[h])
         d_gate, d_up = glu_pull(d_hidden)
         d_gu_low.append(jnp.concatenate([d_gate.astype(BF), d_up.astype(BF)], axis=-1))
+    d_gu_low, ple_got = stage(d_gu_low, ple_got)
+
     term_share = times_t(d_gu_low[1], gu_mat)
-    term = reduce_start(times_t(d_gu_low[0], gu_mat), term_share)
-    term, d_gu_low, ple_arrived, ff_halves, hidden, d_down_halves = stage(
-        term, d_gu_low, ple_arrived, ff_halves, hidden, d_down_halves
-    )
-
-    term = reduce_end(term)
+    blocks = core_sum(times_t(d_gu_low[0], gu_mat), term_share)
+    blocks, d_gu_low, ff_halves, hidden, d_down_halves = stage(
+        blocks, d_gu_low, ff_halves, hidden, d_down_halves
+    )
+    share_mid = give_to(blocks[2], "z", Z, 2)
 
     def own_core(total):
         keep = jnp.where(first, total[:shard], total[shard:])
@@ -647,23 +751,53 @@
     gu_grads = [None] * yx
     down_grads = [None] * yx
     ff_pieces = column_pieces(ff_halves)
-    for p in reversed(range(yx)):
-        gu_grads[p] = both_rows(ff_pieces[p], d_gu_low)
-    gu_got = sum_first(gu_grads, y_count)
-    for p in reversed(range(yx)):
-        down_grads[p] = both_rows(
+
+    def down_grad(p):
+        return both_rows(
             [
-                lax.dynamic_slice_in_dim(half, places_yx[p] * ff_shard, ff_shard, axis=1)
-                for half in hidden
+                lax.dynamic_slice_in_dim(half_in, places_yx[p] * ff_shard, ff_shard, axis=1)
+                for half_in in hidden
             ],
             d_down_halves,
         )
-    if y_count == 2:
-        down_grads[3] = after(down_grads[3], gu_got[0])
-    down_got = sum_first(down_grads, y_count)
-    term, gu_got, down_got, gu_grads, down_grads, ple_arrived = stage(
-        term, gu_got, down_got, gu_grads, down_grads, ple_arrived
-    )
+
+    gu_grads[yx - 1] = both_rows(ff_pieces[yx - 1], d_gu_low)
+    down_grads[yx - 1] = down_grad(yx - 1)
+    merged = [jnp.zeros((16, 128), BF)]
+    if y_count == 2:
+        merged = [
+            shuffle(
+                [gu_grads[3], down_grads[3]],
+                [(half + edge, width)],
+                [
+                    (0, side * half, 0, 0, 0, 0, half, width),
+                    (1, side * edge, 0, 0, half, 0, edge, width),
+                ],
+            )[0]
+            for side in range(2)
+        ]
+    (
+        share_mid, merged, blocks, ff_pieces, d_gu_low, hidden, d_down_halves, gu_grads[yx - 1],
+        down_grads[yx - 1],
+    ) = stage(
+        share_mid, merged, blocks, ff_pieces, d_gu_low, hidden, d_down_halves, gu_grads[yx - 1],
+        down_grads[yx - 1],
+    )
+    shares = [blocks[0], give_to(blocks[1], "z", Z, 1), give_to(blocks[3], "z", Z, 3), share_mid]
+    if y_count == 2:
+        merged_got = [give_to(merged[0], "x", X, 1), give_to(merged[1], "y", 2, 1)]
+    for p in range(yx - 1):
+        gu_grads[p] = both_rows(ff_pieces[p], d_gu_low)
+        down_grads[p] = down_grad(p)
+    if y_count != 2:
+        merged_got = sum_first(gu_grads, y_count)
+    shares, merged_got, gu_grads, down_grads = stage(shares, merged_got, gu_grads, down_grads)
+    term = add_up(shares)
+    if y_count == 2:
+        gu_got = [got[:half] for got in merged_got]
+        down_got = [got[half:] for got in merged_got]
+    else:
+        gu_got = list(merged_got)
 
     _, norm_pull = jax.vjp(rms_norm, joined, gains[3])
     d_joined_norm, d_gain_pre_ff = norm_pull(term)
@@ -671,13 +805,14 @@
     _, norm_pull = jax.vjp(rms_norm, projected, gains[1])
     d_projected, d_gain_post_attn = norm_pull(d_branch)
     d_proj_low = d_projected.astype(BF)
-    d_proj_low, d_branch, d_gain_pre_ff, d_gain_post_attn, right_out, normed_own, normed_other = stage(
+    (
+        d_proj_low, d_branch, d_gain_pre_ff, d_gain_post_attn, right_out, normed_own, normed_other
+    ) = stage(
         d_proj_low, d_branch, d_gain_pre_ff, d_gain_post_attn, right_out, normed_own, normed_other
     )
 
     d_proj_take = z_take(d_proj_low)
     gu_got = sum_second(gu_grads, gu_got, y_count)
-    ple_total = own_core(sum(piece.astype(F32) for piece in ple_arrived))
     _, norm_pull = jax.vjp(rms_norm, right_out, gains[2])
     d_right, d_gain_laurel = norm_pull(d_branch)
     d_right_low = d_right.astype(BF)
@@ -687,8 +822,8 @@
         [over_rows(d_left_low, normed_low), over_rows(left_low, d_right_low)], axis=0
     ).astype(BF)
     normed_pieces = column_pieces((normed_own, normed_other))
-    d_proj_take, gu_got, left_grads, normed_pieces, d_normed_own, ple_total = stage(
-        d_proj_take, gu_got, left_grads, normed_pieces, d_normed_own, ple_total
+    d_proj_take, gu_got, left_grads, normed_pieces, d_normed_own = stage(
+        d_proj_take, gu_got, left_grads, normed_pieces, d_normed_own
     )
 
     def by_core(rows_in, blocks):
@@ -705,9 +840,16 @@
     gu_sum = sum_total(gu_grads, gu_got).astype(BF)
     gu_pair = by_core(gu_sum, Z)
     gu_cores = [jnp.where(first, *gu_pair), jnp.where(first, *gu_pair[::-1])]
+    ple_sum = sum_total(ple_grads, ple_got).astype(BF)
+    ple_arrived = z_send(lambda k: z_block(ple_sum, k, unit))
+    d_heads = jnp.concatenate([times_t(half_in, out_mat) for half_in in d_proj_halves], axis=0)
+    d_heads, gu_cores, ple_arrived, d_proj_halves, down_grads = stage(
+        d_heads, gu_cores, ple_arrived, d_proj_halves, down_grads
+    )
+    if y_count != 2:
+        down_got = sum_first(down_grads, y_count)
     gu_arrived = [z_send(lambda k: z_block(gu_cores[0], k, shard))]
     down_got = sum_second(down_grads, down_got, y_count)
-    d_heads = jnp.concatenate([times_t(half, out_mat) for half in d_proj_halves], axis=0)
     d_heads = d_heads.astype(BF).reshape(C, group_rows, HD)
     delta = jnp.sum(d_heads.astype(F32) * head_out, axis=-1, keepdims=True)
     d_probs = jnp.einsum("sqd,skd->sqk", d_heads, value_all, preferred_element_type=F32)
@@ -718,19 +860,23 @@
     d_key = d_key.reshape(C, y_count, group_rows, HD)
     d_value = d_value.reshape(C, y_count, group_rows, HD)
 
-    def kv_share(stream, k):
-        return jnp.concatenate([d_key[stream, k], d_value[stream, k]], axis=-1)
-
-    kv_give = [swap_core(kv_share(1, k).astype(BF)) for k in range(y_count)]
-    kv_sum = [kv_share(0, k) + kv_give[k].astype(F32) for k in range(y_count)]
-    kv_sum, d_query, gu_arrived, gu_last, d_proj_halves, heads_low, down_got = stage(
-        kv_sum, d_query, gu_arrived, gu_cores[1], d_proj_halves, heads_low, down_got
-    )
-
-    gu_arrived = gu_arrived + [z_send(lambda k: z_block(gu_last, k, shard))]
+    def kv_share(stream):
+        return jnp.concatenate([d_key[stream], d_value[stream]], axis=-1).reshape(-1, 2 * HD)
+
+    kv_share_own, kv_share_other = kv_share(0), kv_share(1).astype(BF)
+    (
+        kv_share_own, kv_share_other, d_query, gu_arrived, gu_last, d_proj_halves, heads_low, down_got
+    ) = stage(
+        kv_share_own, kv_share_other, d_query, gu_arrived, gu_cores[1], d_proj_halves, heads_low,
+        down_got,
+    )
+
+    kv_sum = kv_share_own + swap_core(kv_share_other).astype(F32)
+    kv_sum = kv_sum.reshape(y_count, group_rows, 2 * HD)
     own_kv = kv_sum[0]
     for k in range(1, y_count):
         own_kv = own_kv + give_to(kv_sum[k].astype(BF), "y", y_count, k).astype(F32)
+    gu_arrived = list(gu_arrived) + [z_send(lambda k: z_block(gu_last, k, shard))]
     _, rot_pull = jax.vjp(rotated, q_raw, qk[0])
     d_q_raw, d_gain_query = rot_pull(d_query.reshape(C * group_rows, HD))
     _, rot_pull = jax.vjp(rotated_own, k_raw[:group_rows], qk[1])
@@ -740,14 +886,17 @@
     d_q_low = d_q_raw.astype(BF)
     d_kv_low = jnp.concatenate([d_k_raw.astype(BF), d_v_raw.astype(BF)], axis=-1)
     d_own_low = jnp.concatenate([d_q_low[:group_rows], d_kv_low], axis=-1)
+    d_q_low, d_kv_low, d_own_low, gu_arrived, down_grads, d_proj_halves = stage(
+        d_q_low, d_kv_low, d_own_low, gu_arrived, down_grads, d_proj_halves
+    )
+
     part_other = times_t(d_q_low[group_rows:], qkv_mat[:, :HD])
     part_own = times_t(d_own_low, qkv_mat)
-    d_normed = reduce_start(part_own, part_other)
-    d_normed, part_own, part_other, d_q_low, d_kv_low, gu_arrived, down_grads, d_proj_halves = stage(
-        d_normed, part_own, part_other, d_q_low, d_kv_low, gu_arrived, down_grads, d_proj_halves
-    )
-
-    d_normed = d_normed_own + reduce_end(d_normed)
+    blocks = core_sum(part_own, part_other)
+    blocks, part_own, part_other, d_q_low, d_kv_low, normed_pieces, left_grads = stage(
+        blocks, part_own, part_other, d_q_low, d_kv_low, normed_pieces, left_grads
+    )
+    share_mid = give_to(blocks[2], "z", Z, 2)
     d_gain_input = (
         jnp.sum(part_own * unit_own, axis=0)
         + jnp.sum(part_other * unit_other, axis=0)
@@ -781,28 +930,49 @@
         [(tall + row_count, span)] * yx,
         copies,
     )
+    share_mid, last_grads, blocks, heads_low, d_proj_halves, down_got, down_grads = stage(
+        share_mid, last_grads, blocks, heads_low, d_proj_halves, down_got, down_grads
+    )
+    share_next = give_to(blocks[1], "z", Z, 1)
     last_got = sum_first(last_grads, y_count)
-    last_got, last_grads, heads_low, d_proj_halves = stage(
-        last_got, last_grads, heads_low, d_proj_halves
-    )
-    last_got = sum_second(last_grads, last_got, y_count)
     out_grad = both_rows((heads_low[:group_rows], heads_low[group_rows:]), d_proj_halves)
+    share_next, last_got, last_grads, out_grad, blocks, down_got, down_grads = stage(
+        share_next, last_got, last_grads, out_grad, blocks, down_got, down_grads
+    )
+    shares = [blocks[0], share_mid, share_next, give_to(blocks[3], "z", Z, 3)]
+    last_got = sum_second(last_grads, list(last_got), y_count)
     out_both = order_cores(*by_core(out_grad, yx // 2), first, 0)
+    grad_down = sum_total(down_grads, down_got)
+    shares, last_got, last_grads, out_both, gu_arrived, ple_arrived = stage(
+        shares, last_got, last_grads, out_both, gu_arrived, ple_arrived
+    )
+    d_normed = d_normed_own + add_up(shares)
+
+    last_low = sum_total(last_grads, last_got).astype(BF)
+    qkv_pair = by_core(last_low[:tall], Z)
+    qkv_cores = [jnp.where(first, *qkv_pair), jnp.where(first, *qkv_pair[::-1])]
+    heights = [min(shard, row_count - low) for low in range(0, row_count, shard)]
+    copies = []
+    for k in range(Z):
+        z_to = (zi + k) % Z
+        for c in range(C):
+            copies.append((c, (z_to, shard), 0, k, 0, c * span, shard, span))
+        for j, height in enumerate(heights):
+            copies.append(
+                (2, tall + j * shard, (z_to, unit), k, 0, C * span + j * unit, height, unit)
+            )
+    last_sends = shuffle(
+        qkv_cores + [last_low], [(shard, C * span + len(heights) * unit)] * Z, copies
+    )
+    last_sends, out_both, gu_arrived, ple_arrived, d_normed = stage(
+        last_sends, out_both, gu_arrived, ple_arrived, d_normed
+    )
+    last_arrived = z_send(lambda k: last_sends[k])
     out_grads = [
         lax.dynamic_slice_in_dim(out_both, places_yx[p] * shard, shard) for p in range(yx)
     ]
-    grad_down = sum_total(down_grads, down_got)
-    d_normed, last_got, last_grads, out_grads, gu_arrived = stage(
-        d_normed, last_got, last_grads, out_grads, gu_arrived
-    )
-
-    last_low = sum_total(last_grads, last_got).astype(BF)
-    qkv_pair = by_core(last_low[:tall], Z)
-    qkv_cores = order_cores(*qkv_pair, first, 1)
-    last_arrived = z_send(lambda k: z_block(qkv_cores, k, shard))
-    by_row = last_low[tall:, :tall]
-    row_arrived = z_send(lambda k: z_block(by_row, k, unit, axis=1))
     grad_out = sum_total(out_grads, sum_second(out_grads, sum_first(out_grads, y_count), y_count))
+    ple_total = own_core(sum(piece.astype(F32) for piece in ple_arrived))
     _, norm_pull = jax.vjp(rms_norm, token_vals, gains[0])
     d_tokens_norm, _ = norm_pull(d_normed)
     d_tokens = d_branch + d_tokens_norm
@@ -822,8 +992,11 @@
         list(gu_arrived[0]) + list(gu_arrived[1]), [(shard, Z * yx * C * ff_shard)] * 2, copies
     )
     grad_gu = [grad.astype(F32) for grad in grad_gu]
-    qkv_parts = z_place(last_arrived, zi).astype(F32)
-    row_total = sum(piece.astype(F32) for piece in row_arrived)
+    qkv_parts = z_place(last_arrived, zi)[:, : C * span].astype(F32)
+    row_total = sum(piece[:, C * span :].astype(F32) for piece in last_arrived)
+    row_total = jnp.concatenate(
+        [row_total[:height, j * unit : (j + 1) * unit] for j, height in enumerate(heights)], axis=0
+    )
     row_keep = jnp.where(first, row_total[:, :shard], row_total[:, shard:])
     row_send = jnp.where(first, row_total[:, shard:], row_total[:, :shard])
     row_total = row_keep + swap_core(row_send.astype(BF)).astype(F32)

time: 899 us -> 861 us (0.958); the launches traced: 882 us -> 853 us
  waiting for transfers between devices: 368 us -> 333 us
  matrix products: 110 us -> 129 us
  other arithmetic: 102 us -> 90.9 us
  Pallas kernels: 83.8 us -> 94.5 us
    ppermute x86 -> x77, waiting for transfers between devices: 363 us -> 321 us  [give_to(): lax.ppermute(value, axis, [(i, (i + step) % size) for i in range(size)])]
    pallas_call x18 -> x24, Pallas kernels: 83.8 us -> 94.5 us  [shuffle(): pl.pallas_call(kernel, out_shape=[jax.ShapeDtypeStruct(shape, dtype) for...]
    dot_general x34, matrix products: 34.7 us -> 45 us  [over_rows(): jnp.einsum('ra,rb->ab', left_in, right_in, preferred_element_type=F32)]
    unnamed x434 -> x422, local copies, waits for them, and re-layouts: 31 us -> 23 us
    ppermute x23 -> x21, starting transfers between devices: 38.4 us -> 30.5 us  [swap_core(): return lax.ppermute(value, 'c', [(0, 1), (1, 0)])]
    ppermute x86 -> x77, starting transfers between devices: 111 us -> 114 us  [give_to(): lax.ppermute(value, axis, [(i, (i + step) % size) for i in range(size)])]
  transfers between devices with their start and end apart: 109 -> 98, of which waited for: 48 -> 46; matrix products, arithmetic and copies ran while one was open for 21% -> 20% of each run, Pallas kernels for 7% -> 8%
where the time goes in v2:
time: 861 us; the launch traced here: 853 us
  waiting for transfers between devices  333 us (39%)
  starting transfers between devices  144 us (17%)
  matrix products  129 us (15%)
  Pallas kernels  94.5 us (11%)
  other arithmetic  90.9 us (11%)
  local copies, waits for them, and re-layouts  57.7 us (7%)
    ppermute x77, waiting for transfers between devices, give_to(): lax.ppermute(value, axis, [(i, (i + step) % size) for i in range(size)])  321 us
    ppermute x77, starting transfers between devices, give_to(): lax.ppermute(value, axis, [(i, (i + step) % size) for i in range(size)])  114 us
    pallas_call x24, Pallas kernels, shuffle(): pl.pallas_call(kernel, out_shape=[jax.ShapeDtypeStruct(shape, dtype) for...  94.5 us
    dot_general x34, matrix products, over_rows(): jnp.einsum('ra,rb->ab', left_in, right_in, preferred_element_type=F32)  45 us
    dot_general x12, matrix products, times_t(): jnp.einsum('...a,ba->...b', left_in, right_in, preferred_element_type=F32)  41.8 us
    dot_general x12, matrix products, times(): jnp.einsum('...a,ab->...b', left_in, right_in, preferred_element_type=F32)  34.4 us
    ppermute x21, starting transfers between devices, swap_core(): return lax.ppermute(value, 'c', [(0, 1), (1, 0)])  30.5 us
    unnamed x422, local copies, waits for them, and re-layouts  23 us
  transfers between devices with their start and end apart: 98, of which 46 were waited for; matrix products, arithmetic and copies ran while one was open for 20% of the time, Pallas kernels for 8%

profile of v2, /device:TPU:1, one launch (start us, length us, event | category | flops | bytes accessed | tf_op | source)
XLA Modules:
  0.0 853.1 jit_solution(9975390161787902448)
XLA Ops:
  22.7 4.5 collective-permute-done.5.refs_1_
  27.2 12.1 %collective-permute-done.2.refs_2_ = bf16[128,1152]{1,0:T(8,128)(2,1)} collective-permute-done((bf16[128,1152]{1,0:T(8,128)(2,1)}, bf16[128,1152]{1,0:T(8,128)(2,1)}, u32[]{:S(2)}, u32[]{:S(2)}) %collective-permute-start.2) | collective-permute-done | bytes 294944 | tf_op jit(solution)/shard_map/ppermute | solution.py:72
  39.3 7.2 collective-permute-start.6
  55.2 21.3 %collective-permute-done.9.refs_1_ = bf16[512,1152]{1,0:T(8,128)(2,1)} collective-permute-done((bf16[512,1152]{1,0:T(8,128)(2,1)}, bf16[512,1152]{1,0:T(8,128)(2,1)}, u32[]{:S(2)}, u32[]{:S(2)}) %collective-permute-start.9) | collective-permute-done | bytes 1179680 | tf_op jit(solution)/shard_map/ppermute | solution.py:72
  82.9 4.5 shard_map.299
  102.3 5.6 shard_map.301
  141.2 7.0 collective-permute-done.19
  149.7 5.8 collective-permute-start.24
  168.6 5.6 collective-permute-done.25.refs_6_
  185.9 5.8 collective-permute-start.28
  197.9 6.8 collective-permute-done.28
  204.7 23.3 %collective-permute-done.29 = bf16[128,2048]{1,0:T(8,128)(2,1)S(1)} collective-permute-done((bf16[128,2048]{1,0:T(8,128)(2,1)S(1)}, bf16[128,2048]{1,0:T(8,128)(2,1)S(1)}, u32[]{:S(2)}, u32[]{:S(2)}) %collective-permute-start.29) | collective-permute-done | bytes 524320 | tf_op jit(solution)/shard_map/ppermute | solution.py:72
  243.3 7.8 collective-permute-start.33
  253.3 9.9 %collective-permute-done.33.refs_1_ = bf16[128,2048]{1,0:T(8,128)(2,1)S(1)} collective-permute-done((bf16[128,2048]{1,0:T(8,128)(2,1)}, bf16[128,2048]{1,0:T(8,128)(2,1)S(1)}, u32[]{:S(2)}, u32[]{:S(2)}) %collective-permute-start.33) | collective-permute-done | bytes 524320 | tf_op jit(solution)/shard_map/ppermute | solution.py:72
  263.2 34.5 %collective-permute-done.34.refs_2_ = bf16[128,2048]{1,0:T(8,128)(2,1)S(1)} collective-permute-done((bf16[128,2048]{1,0:T(8,128)(2,1)}, bf16[128,2048]{1,0:T(8,128)(2,1)S(1)}, u32[]{:S(2)}, u32[]{:S(2)}) %collective-permute-start.34) | collective-permute-done | bytes 524320 | tf_op jit(solution)/shard_map/ppermute | solution.py:72
  309.4 8.6 %shard_map.309 = bf16[2048,2048]{1,0:T(8,128)(2,1)} custom-call(s32[16]{0:T(128)} %stack.350.table_ref, bf16[512,2048]{1,0:T(8,128)(2,1)} %shard_map.305.refs_0_, bf16[512,2048]{1,0:T(8,128)(2,1)} %collective-permute-done.31.refs_0_.refs_1_, bf16[512,2048]{1,0:T(8,128)(2,1)} %collective-permute-done.32.refs_0_.refs_2_, bf16[512,2048]{1,0:T(8,128)(2,1)} %copy-done.37, ...), custom_call_target="tpu_custom_call" | custom-call | bytes 16777216 | tf_op jit(solution)/shard_map/pallas_call | solution.py:157
  318.0 7.1 fusion.197
  327.1 6.6 fusion.198
  335.6 5.7 shard_map.310
  341.3 5.9 convolution_convert_fusion
  347.9 4.0 collective-permute-done.41
  351.9 5.2 fusion.192
  363.0 9.5 %collective-permute-done.42 = bf16[128,2048]{1,0:T(8,128)(2,1)S(1)} collective-permute-done((bf16[128,2048]{1,0:T(8,128)(2,1)S(1)}, bf16[128,2048]{1,0:T(8,128)(2,1)S(1)}, u32[]{:S(2)}, u32[]{:S(2)}) %collective-permute-start.42) | collective-permute-done | bytes 524320 | tf_op jit(solution)/shard_map/ppermute | solution.py:72
  372.5 21.6 %collective-permute-done.43 = bf16[128,2048]{1,0:T(8,128)(2,1)S(1)} collective-permute-done((bf16[128,2048]{1,0:T(8,128)(2,1)S(1)}, bf16[128,2048]{1,0:T(8,128)(2,1)S(1)}, u32[]{:S(2)}, u32[]{:S(2)}) %collective-permute-start.43) | collective-permute-done | bytes 524320 | tf_op jit(solution)/shard_map/ppermute | solution.py:72
  400.2 11.5 %collective-permute-start.45 = (bf16[128,2048]{1,0:T(8,128)(2,1)S(1)}, bf16[128,2048]{1,0:T(8,128)(2,1)S(1)}, u32[]{:S(2)}, u32[]{:S(2)}) collective-permute-start(bf16[128,2048]{1,0:T(8,128)(2,1)S(1)} %fusion.44.refs_0_), channel_id=1, source_target_pairs={{0,24},{8,0},{16,8},{24,16},{1,25},{9,1},{17,9},{25,17},{2,26},{10... | collective-permute-start | bytes 1572872 | tf_op jit(solution)/shard_map/ppermute | solution.py:72
  417.0 4.2 collective-permute-done.48
  422.8 34.6 %collective-permute-done.46.refs_2_ = bf16[128,2048]{1,0:T(8,128)(2,1)S(1)} collective-permute-done((bf16[128,2048]{1,0:T(8,128)(2,1)S(1)}, bf16[128,2048]{1,0:T(8,128)(2,1)S(1)}, u32[]{:S(2)}, u32[]{:S(2)}) %collective-permute-start.46) | collective-permute-done | bytes 524320 | tf_op jit(solution)/shard_map/ppermute | solution.py:72
  467.6 6.9 fusion.22
  480.8 5.9 convolution_convert_fusion.2
  491.5 9.1 %fusion.193 = (bf16[512,2048]{1,0:T(8,128)(2,1)S(1)}, f32[512,2048]{1,0:T(8,128)S(1)}) fusion(bf16[512,2048]{1,0:T(8,128)(2,1)} %collective-permute-done.53, bf16[512,2048]{1,0:T(8,128)(2,1)} %pad_maximum_fusion.2, bf16[2048,2048]{1,0:T(8,128)(2,1)} %shard_map.309), kind=kOutput, calls=%fused_computation.526 | convolution fusion | flops 4298113024 | bytes 18874368 | tf_op jit(solution)/shard_map/...a,ba->...b/dot_general | solution.py:64
  502.9 6.0 shard_map.312
  551.6 13.8 %collective-permute-done.57 = bf16[384,2048]{1,0:T(8,128)(2,1)S(1)} collective-permute-done((bf16[384,2048]{1,0:T(8,128)(2,1)}, bf16[384,2048]{1,0:T(8,128)(2,1)S(1)}, u32[]{:S(2)}, u32[]{:S(2)}) %collective-permute-start.57) | collective-permute-done | bytes 1572896 | tf_op jit(solution)/shard_map/ppermute | solution.py:72
  579.9 6.1 shard_map.315
  590.2 25.1 %collective-permute-done.60.refs_2_ = bf16[128,2048]{1,0:T(8,128)(2,1)} collective-permute-done((bf16[128,2048]{1,0:T(8,128)(2,1)}, bf16[128,2048]{1,0:T(8,128)(2,1)}, u32[]{:S(2)}, u32[]{:S(2)}) %collective-permute-start.60) | collective-permute-done | bytes 524320 | tf_op jit(solution)/shard_map/ppermute | solution.py:72
  615.3 4.8 collective-permute-done.62
  625.3 4.0 collective-permute-start.64
  629.3 4.1 add_convert_fusion
  668.1 12.6 %collective-permute-done.70.refs_2_ = bf16[64,2048]{1,0:T(8,128)(2,1)S(1)} collective-permute-done((bf16[64,2048]{1,0:T(8,128)(2,1)S(1)}, bf16[64,2048]{1,0:T(8,128)(2,1)S(1)}, u32[]{:S(2)}, u32[]{:S(2)}) %collective-permute-start.70) | collective-permute-done | bytes 262176 | tf_op jit(solution)/shard_map/ppermute | solution.py:72
  680.7 7.3 collective-permute-done.72
  699.2 7.9 collective-permute-done.75
  710.4 5.0 collective-permute-done.77.refs_6_
  715.5 4.9 fusion.194
  727.6 4.5 fusion.172
  739.9 3.9 collective-permute-start.80
  756.8 4.9 shard_map.317
  761.7 5.8 collective-permute-done.80
  774.2 7.6 collective-permute-done.82
  794.8 12.6 %collective-permute-done.85 = bf16[656,768]{1,0:T(8,128)(2,1)S(1)} collective-permute-done((bf16[656,768]{1,0:T(8,128)(2,1)S(1)}, bf16[656,768]{1,0:T(8,128)(2,1)S(1)}, u32[]{:S(2)}, u32[]{:S(2)}) %collective-permute-start.85) | collective-permute-done | bytes 1007648 | tf_op jit(solution)/shard_map/ppermute | solution.py:72
  (927 shorter events, 399.6 us)
Async XLA Ops:
  12.6 26.7 %collective-permute-start.4 = (bf16[64,16384]{1,0:T(8,128)(2,1)S(1)}, bf16[64,16384]{1,0:T(8,128)(2,1)}, u32[]{:S(2)}, u32[]{:S(2)}) collective-permute-start(bf16[64,16384]{1,0:T(8,128)(2,1)S(1)} %pad_maximum_fusion.refs_0_), channel_id=1, source_target_pairs={{0,1},{1,0},{2,3},{3,2},{4,5},{5,4},{6,7},{7,6},{8,9},{9,8},{10,11... | collective-permute-start | bytes 6291464 | tf_op jit(solution)/shard_map/ppermute | solution.py:76
  16.8 22.5 %collective-permute-start.2 = (bf16[128,1152]{1,0:T(8,128)(2,1)}, bf16[128,1152]{1,0:T(8,128)(2,1)}, u32[]{:S(2)}, u32[]{:S(2)}) collective-permute-start(bf16[128,1152]{1,0:T(8,128)(2,1)} %get-tuple-element.379), channel_id=1, source_target_pairs={{0,16},{8,24},{16,0},{24,8},{1,17},{9,25},{17,1},{25,9},{2,18},{10... | collective-permute-start | bytes 884744 | tf_op jit(solution)/shard_map/ppermute | solution.py:72
  19.1 20.2 %collective-permute-start.3 = (bf16[128,1152]{1,0:T(8,128)(2,1)}, bf16[128,1152]{1,0:T(8,128)(2,1)}, u32[]{:S(2)}, u32[]{:S(2)}) collective-permute-start(bf16[128,1152]{1,0:T(8,128)(2,1)} %get-tuple-element.380), channel_id=1, source_target_pairs={{0,24},{8,0},{16,8},{24,16},{1,25},{9,1},{17,9},{25,17},{2,26},{10... | collective-permute-start | bytes 884744 | tf_op jit(solution)/shard_map/ppermute | solution.py:72
  39.3 55.5 %collective-permute-start.6 = (bf16[128,2048]{1,0:T(8,128)(2,1)S(1)}, bf16[128,2048]{1,0:T(8,128)(2,1)}, u32[]{:S(2)}, u32[]{:S(2)}) collective-permute-start(bf16[128,2048]{1,0:T(8,128)(2,1)S(1)} %bitcast.283), channel_id=1, source_target_pairs={{0,24},{8,0},{16,8},{24,16},{1,25},{9,1},{17,9},{25,17},{2,26},{10... | collective-permute-start | bytes 1572872 | tf_op jit(solution)/shard_map/ppermute | solution.py:72
  46.5 48.3 %collective-permute-start.7 = (bf16[128,2048]{1,0:T(8,128)(2,1)S(1)}, bf16[128,2048]{1,0:T(8,128)(2,1)}, u32[]{:S(2)}, u32[]{:S(2)}) collective-permute-start(bf16[128,2048]{1,0:T(8,128)(2,1)S(1)} %bitcast.284), channel_id=1, source_target_pairs={{0,16},{8,24},{16,0},{24,8},{1,17},{9,25},{17,1},{25,9},{2,18},{10... | collective-permute-start | bytes 1572872 | tf_op jit(solution)/shard_map/ppermute | solution.py:72
  47.1 47.8 %collective-permute-start.8 = (bf16[128,2048]{1,0:T(8,128)(2,1)S(1)}, bf16[128,2048]{1,0:T(8,128)(2,1)}, u32[]{:S(2)}, u32[]{:S(2)}) collective-permute-start(bf16[128,2048]{1,0:T(8,128)(2,1)S(1)} %bitcast.285), channel_id=1, source_target_pairs={{0,8},{8,16},{16,24},{24,0},{1,9},{9,17},{17,25},{25,1},{2,10},{10... | collective-permute-start | bytes 1572872 | tf_op jit(solution)/shard_map/ppermute | solution.py:72
  50.1 26.5 %collective-permute-start.9 = (bf16[512,1152]{1,0:T(8,128)(2,1)}, bf16[512,1152]{1,0:T(8,128)(2,1)}, u32[]{:S(2)}, u32[]{:S(2)}) collective-permute-start(bf16[512,1152]{1,0:T(8,128)(2,1)} %shard_map.298.refs_0_), channel_id=1, source_target_pairs={{0,2},{2,0},{1,3},{3,1},{4,6},{6,4},{5,7},{7,5},{8,10},{10,8},{9,1... | collective-permute-start | bytes 3538952 | tf_op jit(solution)/shard_map/ppermute | solution.py:72
  51.3 26.2 %collective-permute-start.10 = (bf16[512,1152]{1,0:T(8,128)(2,1)}, bf16[512,1152]{1,0:T(8,128)(2,1)}, u32[]{:S(2)}, u32[]{:S(2)}) collective-permute-start(bf16[512,1152]{1,0:T(8,128)(2,1)} %shard_map.298.refs_0_), channel_id=1, source_target_pairs={{0,4},{4,0},{1,5},{5,1},{2,6},{6,2},{3,7},{7,3},{8,12},{12,8},{9,1... | collective-permute-start | bytes 3538952 | tf_op jit(solution)/shard_map/ppermute | solution.py:72
  111.7 18.9 %collective-permute-start.15 = (bf16[128,1024]{1,0:T(8,128)(2,1)}, bf16[128,1024]{1,0:T(8,128)(2,1)}, u32[]{:S(2)}, u32[]{:S(2)}) collective-permute-start(bf16[128,1024]{1,0:T(8,128)(2,1)} %get-tuple-element.421), channel_id=1, source_target_pairs={{0,8},{8,16},{16,24},{24,0},{1,9},{9,17},{17,25},{25,1},{2,10},{10... | collective-permute-start | bytes 786440 | tf_op jit(solution)/shard_map/ppermute | solution.py:72
  113.4 20.0 %collective-permute-start.16 = (bf16[128,1024]{1,0:T(8,128)(2,1)}, bf16[128,1024]{1,0:T(8,128)(2,1)}, u32[]{:S(2)}, u32[]{:S(2)}) collective-permute-start(bf16[128,1024]{1,0:T(8,128)(2,1)} %get-tuple-element.422), channel_id=1, source_target_pairs={{0,16},{8,24},{16,0},{24,8},{1,17},{9,25},{17,1},{25,9},{2,18},{10... | collective-permute-start | bytes 786440 | tf_op jit(solution)/shard_map/ppermute | solution.py:72
  149.7 18.9 %collective-permute-start.24 = (bf16[128,1024]{1,0:T(8,128)(2,1)}, bf16[128,1024]{1,0:T(8,128)(2,1)}, u32[]{:S(2)}, u32[]{:S(2)}) collective-permute-start(bf16[128,1024]{1,0:T(8,128)(2,1)} %get-tuple-element.435), channel_id=1, source_target_pairs={{0,8},{8,16},{16,24},{24,0},{1,9},{9,17},{17,25},{25,1},{2,10},{10... | collective-permute-start | bytes 786440 | tf_op jit(solution)/shard_map/ppermute | solution.py:72
  184.4 47.3 %collective-permute-start.31 = (bf16[512,2048]{1,0:T(8,128)(2,1)}, bf16[512,2048]{1,0:T(8,128)(2,1)}, u32[]{:S(2)}, u32[]{:S(2)}) collective-permute-start(bf16[512,2048]{1,0:T(8,128)(2,1)} %shard_map.305.refs_0_), channel_id=1, source_target_pairs={{0,2},{2,0},{1,3},{3,1},{4,6},{6,4},{5,7},{7,5},{8,10},{10,8},{9,1... | collective-permute-start | bytes 6291464 | tf_op jit(solution)/shard_map/ppermute | solution.py:72
  185.5 47.0 %collective-permute-start.32 = (bf16[512,2048]{1,0:T(8,128)(2,1)}, bf16[512,2048]{1,0:T(8,128)(2,1)}, u32[]{:S(2)}, u32[]{:S(2)}) collective-permute-start(bf16[512,2048]{1,0:T(8,128)(2,1)} %shard_map.305.refs_0_), channel_id=1, source_target_pairs={{0,4},{4,0},{1,5},{5,1},{2,6},{6,2},{3,7},{7,3},{8,12},{12,8},{9,1... | collective-permute-start | bytes 6291464 | tf_op jit(solution)/shard_map/ppermute | solution.py:72
  185.9 18.8 %collective-permute-start.28 = (bf16[128,2048]{1,0:T(8,128)(2,1)}, bf16[128,2048]{1,0:T(8,128)(2,1)S(1)}, u32[]{:S(2)}, u32[]{:S(2)}) collective-permute-start(bf16[128,2048]{1,0:T(8,128)(2,1)} %get-tuple-element.453), channel_id=1, source_target_pairs={{0,8},{8,16},{16,24},{24,0},{1,9},{9,17},{17,25},{25,1},{2,10},{10... | collective-permute-start | bytes 1572872 | tf_op jit(solution)/shard_map/ppermute | solution.py:72
  191.8 36.3 %collective-permute-start.29 = (bf16[128,2048]{1,0:T(8,128)(2,1)S(1)}, bf16[128,2048]{1,0:T(8,128)(2,1)S(1)}, u32[]{:S(2)}, u32[]{:S(2)}) collective-permute-start(bf16[128,2048]{1,0:T(8,128)(2,1)S(1)} %get-tuple-element.454), channel_id=1, source_target_pairs={{0,16},{8,24},{16,0},{24,8},{1,17},{9,25},{17,1},{25,9},{2,18},{10... | collective-permute-start | bytes 1572872 | tf_op jit(solution)/shard_map/ppermute | solution.py:72
  193.2 34.8 %collective-permute-start.30 = (bf16[128,2048]{1,0:T(8,128)(2,1)S(1)}, bf16[128,2048]{1,0:T(8,128)(2,1)S(1)}, u32[]{:S(2)}, u32[]{:S(2)}) collective-permute-start(bf16[128,2048]{1,0:T(8,128)(2,1)S(1)} %get-tuple-element.455), channel_id=1, source_target_pairs={{0,24},{8,0},{16,8},{24,16},{1,25},{9,1},{17,9},{25,17},{2,26},{10... | collective-permute-start | bytes 1572872 | tf_op jit(solution)/shard_map/ppermute | solution.py:72
  239.4 58.3 %collective-permute-start.36 = (bf16[512,2048]{1,0:T(8,128)(2,1)}, bf16[512,2048]{1,0:T(8,128)(2,1)S(1)}, u32[]{:S(2)}, u32[]{:S(2)}) collective-permute-start(bf16[512,2048]{1,0:T(8,128)(2,1)} %shard_map.306), channel_id=1, source_target_pairs={{0,4},{4,0},{1,5},{5,1},{2,6},{6,2},{3,7},{7,3},{8,12},{12,8},{9,1... | collective-permute-start | bytes 6291464 | tf_op jit(solution)/shard_map/ppermute | solution.py:72
  242.9 55.8 %collective-permute-start.37 = (bf16[512,2048]{1,0:T(8,128)(2,1)}, bf16[512,2048]{1,0:T(8,128)(2,1)}, u32[]{:S(2)}, u32[]{:S(2)}) collective-permute-start(bf16[512,2048]{1,0:T(8,128)(2,1)} %shard_map.307), channel_id=1, source_target_pairs={{0,2},{2,0},{1,3},{3,1},{4,6},{6,4},{5,7},{7,5},{8,10},{10,8},{9,1... | collective-permute-start | bytes 6291464 | tf_op jit(solution)/shard_map/ppermute | solution.py:72
  243.3 19.9 %collective-permute-start.33 = (bf16[128,2048]{1,0:T(8,128)(2,1)}, bf16[128,2048]{1,0:T(8,128)(2,1)S(1)}, u32[]{:S(2)}, u32[]{:S(2)}) collective-permute-start(bf16[128,2048]{1,0:T(8,128)(2,1)} %multiply_convert_fusion.5.refs_0_), channel_id=1, source_target_pairs={{0,24},{8,0},{16,8},{24,16},{1,25},{9,1},{17,9},{25,17},{2,26},{10... | collective-permute-start | bytes 1572872 | tf_op jit(solution)/shard_map/ppermute | solution.py:72
  251.1 46.6 %collective-permute-start.34 = (bf16[128,2048]{1,0:T(8,128)(2,1)}, bf16[128,2048]{1,0:T(8,128)(2,1)S(1)}, u32[]{:S(2)}, u32[]{:S(2)}) collective-permute-start(bf16[128,2048]{1,0:T(8,128)(2,1)} %multiply_convert_fusion.5.refs_0_), channel_id=1, source_target_pairs={{0,16},{8,24},{16,0},{24,8},{1,17},{9,25},{17,1},{25,9},{2,18},{10... | collective-permute-start | bytes 1572872 | tf_op jit(solution)/shard_map/ppermute | solution.py:72
  252.9 44.8 %collective-permute-start.35 = (bf16[128,2048]{1,0:T(8,128)(2,1)}, bf16[128,2048]{1,0:T(8,128)(2,1)S(1)}, u32[]{:S(2)}, u32[]{:S(2)}) collective-permute-start(bf16[128,2048]{1,0:T(8,128)(2,1)} %multiply_convert_fusion.5.refs_0_), channel_id=1, source_target_pairs={{0,8},{8,16},{16,24},{24,0},{1,9},{9,17},{17,25},{25,1},{2,10},{10... | collective-permute-start | bytes 1572872 | tf_op jit(solution)/shard_map/ppermute | solution.py:72
  302.4 24.7 %collective-permute-start.38 = (bf16[512,2048]{1,0:T(8,128)(2,1)}, bf16[512,2048]{1,0:T(8,128)(2,1)}, u32[]{:S(2)}, u32[]{:S(2)}) collective-permute-start(bf16[512,2048]{1,0:T(8,128)(2,1)} %shard_map.308.refs_0_), channel_id=1, source_target_pairs={{0,1},{1,0},{2,3},{3,2},{4,5},{5,4},{6,7},{7,6},{8,9},{9,8},{10,11... | collective-permute-start | bytes 6291464 | tf_op jit(solution)/shard_map/ppermute | solution.py:76
  307.5 28.1 %collective-permute-start.39 = (bf16[128,2048]{1,0:T(8,128)(2,1)}, bf16[128,2048]{1,0:T(8,128)(2,1)}, u32[]{:S(2)}, u32[]{:S(2)}) collective-permute-start(bf16[128,2048]{1,0:T(8,128)(2,1)} %slice.617), channel_id=1, source_target_pairs={{0,4},{4,0},{1,5},{5,1},{2,6},{6,2},{3,7},{7,3},{8,12},{12,8},{9,1... | collective-permute-start | bytes 1572872 | tf_op jit(solution)/shard_map/ppermute | solution.py:72
  308.6 27.0 %collective-permute-start.40 = (bf16[128,2048]{1,0:T(8,128)(2,1)}, bf16[128,2048]{1,0:T(8,128)(2,1)}, u32[]{:S(2)}, u32[]{:S(2)}) collective-permute-start(bf16[128,2048]{1,0:T(8,128)(2,1)} %slice.618), channel_id=1, source_target_pairs={{0,2},{2,0},{1,3},{3,1},{4,6},{6,4},{5,7},{7,5},{8,10},{10,8},{9,1... | collective-permute-start | bytes 1572872 | tf_op jit(solution)/shard_map/ppermute | solution.py:72
  357.5 36.6 %collective-permute-start.43 = (bf16[128,2048]{1,0:T(8,128)(2,1)S(1)}, bf16[128,2048]{1,0:T(8,128)(2,1)S(1)}, u32[]{:S(2)}, u32[]{:S(2)}) collective-permute-start(bf16[128,2048]{1,0:T(8,128)(2,1)S(1)} %get-tuple-element.490), channel_id=1, source_target_pairs={{0,16},{8,24},{16,0},{24,8},{1,17},{9,25},{17,1},{25,9},{2,18},{10... | collective-permute-start | bytes 1572872 | tf_op jit(solution)/shard_map/ppermute | solution.py:72
  357.9 36.3 %collective-permute-start.44 = (bf16[128,2048]{1,0:T(8,128)(2,1)S(1)}, bf16[128,2048]{1,0:T(8,128)(2,1)S(1)}, u32[]{:S(2)}, u32[]{:S(2)}) collective-permute-start(bf16[128,2048]{1,0:T(8,128)(2,1)S(1)} %get-tuple-element.491), channel_id=1, source_target_pairs={{0,24},{8,0},{16,8},{24,16},{1,25},{9,1},{17,9},{25,17},{2,26},{10... | collective-permute-start | bytes 1572872 | tf_op jit(solution)/shard_map/ppermute | solution.py:72
  400.2 22.6 %collective-permute-start.45 = (bf16[128,2048]{1,0:T(8,128)(2,1)S(1)}, bf16[128,2048]{1,0:T(8,128)(2,1)S(1)}, u32[]{:S(2)}, u32[]{:S(2)}) collective-permute-start(bf16[128,2048]{1,0:T(8,128)(2,1)S(1)} %fusion.44.refs_0_), channel_id=1, source_target_pairs={{0,24},{8,0},{16,8},{24,16},{1,25},{9,1},{17,9},{25,17},{2,26},{10... | collective-permute-start | bytes 1572872 | tf_op jit(solution)/shard_map/ppermute | solution.py:72
  411.6 45.7 %collective-permute-start.46 = (bf16[128,2048]{1,0:T(8,128)(2,1)S(1)}, bf16[128,2048]{1,0:T(8,128)(2,1)S(1)}, u32[]{:S(2)}, u32[]{:S(2)}) collective-permute-start(bf16[128,2048]{1,0:T(8,128)(2,1)S(1)} %fusion.44.refs_0_), channel_id=1, source_target_pairs={{0,16},{8,24},{16,0},{24,8},{1,17},{9,25},{17,1},{25,9},{2,18},{10... | collective-permute-start | bytes 1572872 | tf_op jit(solution)/shard_map/ppermute | solution.py:72
  412.9 44.5 %collective-permute-start.47 = (bf16[128,2048]{1,0:T(8,128)(2,1)S(1)}, bf16[128,2048]{1,0:T(8,128)(2,1)S(1)}, u32[]{:S(2)}, u32[]{:S(2)}) collective-permute-start(bf16[128,2048]{1,0:T(8,128)(2,1)S(1)} %fusion.44.refs_0_), channel_id=1, source_target_pairs={{0,8},{8,16},{16,24},{24,0},{1,9},{9,17},{17,25},{25,1},{2,10},{10... | collective-permute-start | bytes 1572872 | tf_op jit(solution)/shard_map/ppermute | solution.py:72
  502.9 23.8 %collective-permute-start.54 = (bf16[128,2048]{1,0:T(8,128)(2,1)}, bf16[128,2048]{1,0:T(8,128)(2,1)}, u32[]{:S(2)}, u32[]{:S(2)}) collective-permute-start(bf16[128,2048]{1,0:T(8,128)(2,1)} %get-tuple-element.516), channel_id=1, source_target_pairs={{0,16},{8,24},{16,0},{24,8},{1,17},{9,25},{17,1},{25,9},{2,18},{10... | collective-permute-start | bytes 1572872 | tf_op jit(solution)/shard_map/ppermute | solution.py:72
  526.7 24.9 %collective-permute-start.55 = (bf16[128,2048]{1,0:T(8,128)(2,1)}, bf16[128,2048]{1,0:T(8,128)(2,1)S(1)}, u32[]{:S(2)}, u32[]{:S(2)}) collective-permute-start(bf16[128,2048]{1,0:T(8,128)(2,1)} %get-tuple-element.537), channel_id=1, source_target_pairs={{0,8},{8,16},{16,24},{24,0},{1,9},{9,17},{17,25},{25,1},{2,10},{10... | collective-permute-start | bytes 1572872 | tf_op jit(solution)/shard_map/ppermute | solution.py:72
  526.7 24.9 %collective-permute-start.56 = (bf16[128,2048]{1,0:T(8,128)(2,1)}, bf16[128,2048]{1,0:T(8,128)(2,1)S(1)}, u32[]{:S(2)}, u32[]{:S(2)}) collective-permute-start(bf16[128,2048]{1,0:T(8,128)(2,1)} %get-tuple-element.538), channel_id=1, source_target_pairs={{0,24},{8,0},{16,8},{24,16},{1,25},{9,1},{17,9},{25,17},{2,26},{10... | collective-permute-start | bytes 1572872 | tf_op jit(solution)/shard_map/ppermute | solution.py:72
  530.3 35.1 %collective-permute-start.57 = (bf16[384,2048]{1,0:T(8,128)(2,1)}, bf16[384,2048]{1,0:T(8,128)(2,1)S(1)}, u32[]{:S(2)}, u32[]{:S(2)}) collective-permute-start(bf16[384,2048]{1,0:T(8,128)(2,1)} %shard_map.313), channel_id=1, source_target_pairs={{0,2},{2,0},{1,3},{3,1},{4,6},{6,4},{5,7},{7,5},{8,10},{10,8},{9,1... | collective-permute-start | bytes 4718600 | tf_op jit(solution)/shard_map/ppermute | solution.py:72
  531.1 34.8 %collective-permute-start.58 = (bf16[384,2048]{1,0:T(8,128)(2,1)}, bf16[384,2048]{1,0:T(8,128)(2,1)S(1)}, u32[]{:S(2)}, u32[]{:S(2)}) collective-permute-start(bf16[384,2048]{1,0:T(8,128)(2,1)} %shard_map.314), channel_id=1, source_target_pairs={{0,4},{4,0},{1,5},{5,1},{2,6},{6,2},{3,7},{7,3},{8,12},{12,8},{9,1... | collective-permute-start | bytes 4718600 | tf_op jit(solution)/shard_map/ppermute | solution.py:72
  572.1 43.2 %collective-permute-start.60 = (bf16[128,2048]{1,0:T(8,128)(2,1)}, bf16[128,2048]{1,0:T(8,128)(2,1)}, u32[]{:S(2)}, u32[]{:S(2)}) collective-permute-start(bf16[128,2048]{1,0:T(8,128)(2,1)} %fusion.46.refs_0_), channel_id=1, source_target_pairs={{0,16},{8,24},{16,0},{24,8},{1,17},{9,25},{17,1},{25,9},{2,18},{10... | collective-permute-start | bytes 1572872 | tf_op jit(solution)/shard_map/ppermute | solution.py:72
  572.1 43.2 %collective-permute-start.61 = (bf16[128,2048]{1,0:T(8,128)(2,1)}, bf16[128,2048]{1,0:T(8,128)(2,1)}, u32[]{:S(2)}, u32[]{:S(2)}) collective-permute-start(bf16[128,2048]{1,0:T(8,128)(2,1)} %fusion.46.refs_0_), channel_id=1, source_target_pairs={{0,8},{8,16},{16,24},{24,0},{1,9},{9,17},{17,25},{25,1},{2,10},{10... | collective-permute-start | bytes 1572872 | tf_op jit(solution)/shard_map/ppermute | solution.py:72
  575.4 44.7 %collective-permute-start.62 = (bf16[512,2048]{1,0:T(8,128)(2,1)}, bf16[512,2048]{1,0:T(8,128)(2,1)}, u32[]{:S(2)}, u32[]{:S(2)}) collective-permute-start(bf16[512,2048]{1,0:T(8,128)(2,1)} %pad_maximum_fusion.4), channel_id=1, source_target_pairs={{0,4},{4,0},{1,5},{5,1},{2,6},{6,2},{3,7},{7,3},{8,12},{12,8},{9,1... | collective-permute-start | bytes 6291464 | tf_op jit(solution)/shard_map/ppermute | solution.py:72
  578.0 44.4 %collective-permute-start.63 = (bf16[512,2048]{1,0:T(8,128)(2,1)}, bf16[512,2048]{1,0:T(8,128)(2,1)}, u32[]{:S(2)}, u32[]{:S(2)}) collective-permute-start(bf16[512,2048]{1,0:T(8,128)(2,1)} %pad_maximum_fusion.5), channel_id=1, source_target_pairs={{0,2},{2,0},{1,3},{3,1},{4,6},{6,4},{5,7},{7,5},{8,10},{10,8},{9,1... | collective-permute-start | bytes 6291464 | tf_op jit(solution)/shard_map/ppermute | solution.py:72
  625.3 19.8 %collective-permute-start.64 = (bf16[512,2048]{1,0:T(8,128)(2,1)}, bf16[512,2048]{1,0:T(8,128)(2,1)}, u32[]{:S(2)}, u32[]{:S(2)}) collective-permute-start(bf16[512,2048]{1,0:T(8,128)(2,1)} %shard_map.316), channel_id=1, source_target_pairs={{0,1},{1,0},{2,3},{3,2},{4,5},{5,4},{6,7},{7,6},{8,9},{9,8},{10,11... | collective-permute-start | bytes 6291464 | tf_op jit(solution)/shard_map/ppermute | solution.py:76
  664.3 23.7 %collective-permute-start.72 = (bf16[256,2048]{1,0:T(8,128)(2,1)S(1)}, bf16[256,2048]{1,0:T(8,128)(2,1)S(1)}, u32[]{:S(2)}, u32[]{:S(2)}) collective-permute-start(bf16[256,2048]{1,0:T(8,128)(2,1)S(1)} %pad_maximum_fusion.16), channel_id=1, source_target_pairs={{0,4},{4,0},{1,5},{5,1},{2,6},{6,2},{3,7},{7,3},{8,12},{12,8},{9,1... | collective-permute-start | bytes 3145736 | tf_op jit(solution)/shard_map/ppermute | solution.py:72
  665.5 23.4 %collective-permute-start.73 = (bf16[256,2048]{1,0:T(8,128)(2,1)S(1)}, bf16[256,2048]{1,0:T(8,128)(2,1)S(1)}, u32[]{:S(2)}, u32[]{:S(2)}) collective-permute-start(bf16[256,2048]{1,0:T(8,128)(2,1)S(1)} %pad_maximum_fusion.17), channel_id=1, source_target_pairs={{0,2},{2,0},{1,3},{3,1},{4,6},{6,4},{5,7},{7,5},{8,10},{10,8},{9,1... | collective-permute-start | bytes 3145736 | tf_op jit(solution)/shard_map/ppermute | solution.py:72
  695.8 19.6 %collective-permute-start.77 = (bf16[64,2048]{1,0:T(8,128)(2,1)S(1)}, bf16[64,2048]{1,0:T(8,128)(2,1)S(1)}, u32[]{:S(2)}, u32[]{:S(2)}) collective-permute-start(bf16[64,2048]{1,0:T(8,128)(2,1)S(1)} %get-tuple-element.927), channel_id=1, source_target_pairs={{0,16},{8,24},{16,0},{24,8},{1,17},{9,25},{17,1},{25,9},{2,18},{10... | collective-permute-start | bytes 786440 | tf_op jit(solution)/shard_map/ppermute | solution.py:72
  739.9 27.6 %collective-permute-start.80 = (bf16[128,2048]{1,0:T(8,128)(2,1)}, bf16[128,2048]{1,0:T(8,128)(2,1)}, u32[]{:S(2)}, u32[]{:S(2)}) collective-permute-start(bf16[128,2048]{1,0:T(8,128)(2,1)} %get-tuple-element.619), channel_id=1, source_target_pairs={{0,16},{8,24},{16,0},{24,8},{1,17},{9,25},{17,1},{25,9},{2,18},{10... | collective-permute-start | bytes 1572872 | tf_op jit(solution)/shard_map/ppermute | solution.py:72
  785.7 21.7 %collective-permute-start.85 = (bf16[656,768]{1,0:T(8,128)(2,1)S(1)}, bf16[656,768]{1,0:T(8,128)(2,1)S(1)}, u32[]{:S(2)}, u32[]{:S(2)}) collective-permute-start(bf16[656,768]{1,0:T(8,128)(2,1)S(1)} %pad_maximum_fusion.19), channel_id=1, source_target_pairs={{0,4},{4,0},{1,5},{5,1},{2,6},{6,2},{3,7},{7,3},{8,12},{12,8},{9,1... | collective-permute-start | bytes 3022856 | tf_op jit(solution)/shard_map/ppermute | solution.py:72
  786.8 21.4 %collective-permute-start.86 = (bf16[656,768]{1,0:T(8,128)(2,1)S(1)}, bf16[656,768]{1,0:T(8,128)(2,1)S(1)}, u32[]{:S(2)}, u32[]{:S(2)}) collective-permute-start(bf16[656,768]{1,0:T(8,128)(2,1)S(1)} %pad_maximum_fusion.20), channel_id=1, source_target_pairs={{0,2},{2,0},{1,3},{3,1},{4,6},{6,4},{5,7},{7,5},{8,10},{10,8},{9,1... | collective-permute-start | bytes 3022856 | tf_op jit(solution)/shard_map/ppermute | solution.py:72
  819.4 21.0 %collective-permute-start.89 = (bf16[64,1920]{1,0:T(8,128)(2,1)}, bf16[64,1920]{1,0:T(8,128)(2,1)S(1)}, u32[]{:S(2)}, u32[]{:S(2)}) collective-permute-start(bf16[64,1920]{1,0:T(8,128)(2,1)} %get-tuple-element.713), channel_id=1, source_target_pairs={{0,8},{8,16},{16,24},{24,0},{1,9},{9,17},{17,25},{25,1},{2,10},{10... | collective-permute-start | bytes 737288 | tf_op jit(solution)/shard_map/ppermute | solution.py:72
  819.5 21.0 %collective-permute-start.90 = (bf16[64,1920]{1,0:T(8,128)(2,1)}, bf16[64,1920]{1,0:T(8,128)(2,1)S(1)}, u32[]{:S(2)}, u32[]{:S(2)}) collective-permute-start(bf16[64,1920]{1,0:T(8,128)(2,1)} %get-tuple-element.714), channel_id=1, source_target_pairs={{0,16},{8,24},{16,0},{24,8},{1,17},{9,25},{17,1},{25,9},{2,18},{10... | collective-permute-start | bytes 737288 | tf_op jit(solution)/shard_map/ppermute | solution.py:72
  821.2 19.3 %collective-permute-start.91 = (bf16[64,1920]{1,0:T(8,128)(2,1)}, bf16[64,1920]{1,0:T(8,128)(2,1)S(1)}, u32[]{:S(2)}, u32[]{:S(2)}) collective-permute-start(bf16[64,1920]{1,0:T(8,128)(2,1)} %get-tuple-element.715), channel_id=1, source_target_pairs={{0,24},{8,0},{16,8},{24,16},{1,25},{9,1},{17,9},{25,17},{2,26},{10... | collective-permute-start | bytes 737288 | tf_op jit(solution)/shard_map/ppermute | solution.py:72
  (259 other events, 2370.6 us)

commit v3 on v2

--- a/solution.py
+++ b/solution.py
@@ -456,16 +456,17 @@
     for m in range(2):
         for k in range(Z):
             for a in range(yx):
-                column = (((m * Z + (zi + k) % Z) * yx + a) * C + ci, ff_shard)
+                part, low = divmod(a, yx // 2)
                 for source, c_from in ((0, ci), (1, 1 - ci)):
+                    column = (((m * Z + (zi + k) % Z) * yx + a) * C + ci, ff_shard)
                     copies.append(
                         (
-                            source, 0, column, m * Z + k, (c_from, shard), a * ff_shard,
-                            shard, ff_shard,
+                            source, 0, column, (2 * m + part) * Z + k, (c_from, shard),
+                            low * ff_shard, shard, ff_shard,
                         )
                     )
-    ff_sends = shuffle([ff_low, ff_got], [(unit, ff_own)] * (2 * Z), copies)
-    ff_sends = [ff_sends[:Z], ff_sends[Z:]]
+    ff_sends = shuffle([ff_low, ff_got], [(unit, ff_own // 2)] * (4 * Z), copies)
+    ff_sends = [ff_sends[j * Z : (j + 1) * Z] for j in range(4)]
     out_pair = stack_rows([out_low, out_x])
     first_rows, first_got = stage(first_rows, first_got)
     first_got = gather_second(first_rows, list(first_got), y_count)
@@ -502,7 +503,7 @@
 
     token_own = stack_rows(token_take)
     token_other = swap_core(token_own)
-    gate_arrived = z_send(lambda k: ff_sends[0][k])
+    ff_arrived = [z_send(lambda k: ff_sends[0][k])]
     qkv_mat, misc_all, small_late = place_parts(
         first_rows,
         first_got,
@@ -524,13 +525,12 @@
     value = unit_norm(v_raw).astype(BF)
     kv = jnp.concatenate([key, value], axis=-1).reshape(C, group_rows, 2 * HD)
     out_y = give_to(out_pair, "y", 2, 1) if y_count == 2 else out_pair
-    kv, query, gate_arrived, out_pair, out_y, lr_own, small_own = stage(
-        kv, query, gate_arrived, out_pair, out_y, lr_own, small_late
-    )
+    kv, query, ff_arrived, ff_sends, out_pair, out_y, lr_own, small_own = stage(
+        kv, query, ff_arrived, ff_sends, out_pair, out_y, lr_own, small_late
+    )
+    ff_arrived = list(ff_arrived) + [z_send(lambda k: ff_sends[1][k])]
 
     kv_own = [kv[0]] + [give_to(kv[0], "y", y_count, -k) for k in range(1, y_count)]
-    lr_other = swap_core(lr_own)
-    small_other = swap_core(small_own)
     if y_count == 2:
         copies = []
         for p in range(yx):
@@ -543,8 +543,8 @@
     else:
         out_rows = lax.all_gather(out_pair[:shard], ("y", "x", "c"), axis=0, tiled=True)
         out_got = out_rows
-    kv_own, lr_other, small_other, out_rows, out_got = stage(
-        kv_own, lr_other, small_other, out_rows, out_got
+    kv_own, ff_arrived, ff_sends, out_rows, out_got = stage(
+        kv_own, ff_arrived, ff_sends, out_rows, out_got
     )
 
     if y_count == 2:
@@ -557,7 +557,7 @@
         out_mat = shuffle([out_rows, out_got], [(HD, width)], copies)[0]
     else:
         out_mat = lax.dynamic_slice_in_dim(out_rows, ci * HD, HD)
-    up_arrived = z_send(lambda k: ff_sends[1][k])
+    ff_arrived = list(ff_arrived) + [z_send(lambda k: ff_sends[2][k])]
     kv_other = [kv[1]] + [swap_core(piece) for piece in kv_own[1:]]
     kv_all = jnp.stack([jnp.concatenate(kv_own), jnp.concatenate(kv_other)])
     key_all, value_all = kv_all[..., :HD], kv_all[..., HD:]
@@ -569,19 +569,25 @@
     probs_low = probs.astype(BF)
     head_out = jnp.einsum("sqk,skd->sqd", probs_low, value_all, preferred_element_type=F32)
     heads_low = head_out.astype(BF).reshape(C * group_rows, HD)
-    heads_low, up_arrived, out_mat = stage(heads_low, up_arrived, out_mat)
-
+    heads_low, ff_arrived, ff_sends, out_mat, lr_own = stage(
+        heads_low, ff_arrived, ff_sends, out_mat, lr_own
+    )
+
+    heads_share = times(heads_low[group_rows:], out_mat)
+    ff_arrived = list(ff_arrived) + [z_send(lambda k: ff_sends[3][k])]
+    lr_other = swap_core(lr_own)
+    blocks = core_sum(times(heads_low[:group_rows], out_mat), heads_share)
+    blocks, ff_arrived, lr_own, lr_other, own_tokens, heads_low = stage(
+        blocks, ff_arrived, lr_own, lr_other, own_tokens, heads_low
+    )
     copies = [
-        (m * Z + k, 0, 0, 0, ((zi - k) % Z, unit), m * ff_own, unit, ff_own)
-        for m in range(2)
+        (j * Z + k, 0, 0, 0, ((zi - k) % Z, unit), j * (ff_own // 2), unit, ff_own // 2)
+        for j in range(4)
         for k in range(Z)
     ]
-    heads_share = times(heads_low[group_rows:], out_mat)
-    gu_rows = shuffle(list(gate_arrived) + list(up_arrived), [(tall, 2 * ff_own)], copies)[0]
-    blocks = core_sum(times(heads_low[:group_rows], out_mat), heads_share)
-    blocks, gu_rows, lr_own, lr_other, own_tokens, heads_low = stage(
-        blocks, gu_rows, lr_own, lr_other, own_tokens, heads_low
-    )
+    gu_rows = shuffle(
+        [piece for pieces in ff_arrived for piece in pieces], [(tall, 2 * ff_own)], copies
+    )[0]
     shares = z_shares(blocks)
     gu_got = gather_first(gu_rows, y_count)
 
@@ -655,7 +661,7 @@
         gate_proj.append(gate_up[:, :ff_own])
         up_proj.append(gate_up[:, ff_own:])
         hidden.append(glu_piece(gate_proj[-1], up_proj[-1]).astype(BF))
-    hidden, down_far = stage(hidden, down_far)
+    hidden, down_far, small_own = stage(hidden, down_far, small_own)
 
     if y_count == 2:
         copies = [
@@ -673,6 +679,7 @@
     else:
         down_mat = place_blocks(down_low, down_far, ff_shard)
     down_share = times(hidden[1], down_mat)
+    small_other = swap_core(small_own)
     blocks = core_sum(times(hidden[0], down_mat), down_share)
     blocks, small_own, small_other = stage(blocks, small_own, small_other)
     shares = z_shares(blocks)
@@ -734,9 +741,11 @@
     d_gu_low, ple_got = stage(d_gu_low, ple_got)
 
     term_share = times_t(d_gu_low[1], gu_mat)
+    ple_sum = sum_total(ple_grads, ple_got).astype(BF)
+    ple_arrived = z_send(lambda k: z_block(ple_sum, k, unit))
     blocks = core_sum(times_t(d_gu_low[0], gu_mat), term_share)
-    blocks, d_gu_low, ff_halves, hidden, d_down_halves = stage(
-        blocks, d_gu_low, ff_halves, hidden, d_down_halves
+    blocks, d_gu_low, ff_halves, hidden, d_down_halves, ple_arrived = stage(
+        blocks, d_gu_low, ff_halves, hidden, d_down_halves, ple_arrived
     )
     share_mid = give_to(blocks[2], "z", Z, 2)
 
@@ -840,12 +849,7 @@
     gu_sum = sum_total(gu_grads, gu_got).astype(BF)
     gu_pair = by_core(gu_sum, Z)
     gu_cores = [jnp.where(first, *gu_pair), jnp.where(first, *gu_pair[::-1])]
-    ple_sum = sum_total(ple_grads, ple_got).astype(BF)
-    ple_arrived = z_send(lambda k: z_block(ple_sum, k, unit))
     d_heads = jnp.concatenate([times_t(half_in, out_mat) for half_in in d_proj_halves], axis=0)
-    d_heads, gu_cores, ple_arrived, d_proj_halves, down_grads = stage(
-        d_heads, gu_cores, ple_arrived, d_proj_halves, down_grads
-    )
     if y_count != 2:
         down_got = sum_first(down_grads, y_count)
     gu_arrived = [z_send(lambda k: z_block(gu_cores[0], k, shard))]
@@ -876,7 +880,7 @@
     own_kv = kv_sum[0]
     for k in range(1, y_count):
         own_kv = own_kv + give_to(kv_sum[k].astype(BF), "y", y_count, k).astype(F32)
-    gu_arrived = list(gu_arrived) + [z_send(lambda k: z_block(gu_last, k, shard))]
+    gu_next = z_send(lambda k: z_block(gu_last[:, :ff_own], k, shard))
     _, rot_pull = jax.vjp(rotated, q_raw, qk[0])
     d_q_raw, d_gain_query = rot_pull(d_query.reshape(C * group_rows, HD))
     _, rot_pull = jax.vjp(rotated_own, k_raw[:group_rows], qk[1])
@@ -886,16 +890,18 @@
     d_q_low = d_q_raw.astype(BF)
     d_kv_low = jnp.concatenate([d_k_raw.astype(BF), d_v_raw.astype(BF)], axis=-1)
     d_own_low = jnp.concatenate([d_q_low[:group_rows], d_kv_low], axis=-1)
-    d_q_low, d_kv_low, d_own_low, gu_arrived, down_grads, d_proj_halves = stage(
-        d_q_low, d_kv_low, d_own_low, gu_arrived, down_grads, d_proj_halves
+    d_q_low, d_kv_low, d_own_low, gu_next, gu_last, down_grads, d_proj_halves = stage(
+        d_q_low, d_kv_low, d_own_low, gu_next, gu_last[:, ff_own:], down_grads, d_proj_halves
     )
 
     part_other = times_t(d_q_low[group_rows:], qkv_mat[:, :HD])
     part_own = times_t(d_own_low, qkv_mat)
+    gu_final = z_send(lambda k: z_block(gu_last, k, shard))
     blocks = core_sum(part_own, part_other)
-    blocks, part_own, part_other, d_q_low, d_kv_low, normed_pieces, left_grads = stage(
-        blocks, part_own, part_other, d_q_low, d_kv_low, normed_pieces, left_grads
-    )
+    blocks, part_own, part_other, d_q_low, d_kv_low, normed_pieces, left_grads, gu_final = stage(
+        blocks, part_own, part_other, d_q_low, d_kv_low, normed_pieces, left_grads, gu_final
+    )
+    gu_arrived = list(gu_arrived[0]) + list(gu_next) + list(gu_final)
     share_mid = give_to(blocks[2], "z", Z, 2)
     d_gain_input = (
         jnp.sum(part_own * unit_own, axis=0)
@@ -982,15 +988,14 @@
             for m in range(2):
                 for a in range(yx):
                     column = (((zi - k) % Z * yx + a) * C + c, ff_shard)
+                    source = (k, m * ff_own) if c == 0 else ((1 + m) * Z + k, 0)
                     copies.append(
                         (
-                            c * Z + k, 0, m * ff_own + a * ff_shard,
+                            source[0], 0, source[1] + a * ff_shard,
                             m, 0, column, shard, ff_shard,
                         )
                     )
-    grad_gu = shuffle(
-        list(gu_arrived[0]) + list(gu_arrived[1]), [(shard, Z * yx * C * ff_shard)] * 2, copies
-    )
+    grad_gu = shuffle(list(gu_arrived), [(shard, Z * yx * C * ff_shard)] * 2, copies)
     grad_gu = [grad.astype(F32) for grad in grad_gu]
     qkv_parts = z_place(last_arrived, zi)[:, : C * span].astype(F32)
     row_total = sum(piece[:, C * span :].astype(F32) for piece in last_arrived)

time: 861 us -> 837 us (0.972)
  waiting for transfers between devices: 333 us -> 298 us
    ppermute x77 -> x86, waiting for transfers between devices: 321 us -> 290 us  [give_to(): lax.ppermute(value, axis, [(i, (i + step) % size) for i in range(size)])]
    ppermute x77 -> x86, starting transfers between devices: 114 us -> 121 us  [give_to(): lax.ppermute(value, axis, [(i, (i + step) % size) for i in range(size)])]
    unnamed x422 -> x418, local copies, waits for them, and re-layouts: 23 us -> 24.4 us
  transfers between devices with their start and end apart: 98 -> 107, of which waited for: 46 -> 41; matrix products, arithmetic and copies ran while one was open for 20% -> 26% of each run, Pallas kernels for 8% -> 8%
where the time goes in v3:
time: 837 us; the launch traced here: 829 us
  waiting for transfers between devices  298 us (36%)
  starting transfers between devices  151 us (18%)
  matrix products  126 us (15%)
  Pallas kernels  94.8 us (11%)
  other arithmetic  91 us (11%)
  local copies, waits for them, and re-layouts  64.2 us (8%)
    ppermute x86, waiting for transfers between devices, give_to(): lax.ppermute(value, axis, [(i, (i + step) % size) for i in range(size)])  290 us
    ppermute x86, starting transfers between devices, give_to(): lax.ppermute(value, axis, [(i, (i + step) % size) for i in range(size)])  121 us
    pallas_call x24, Pallas kernels, shuffle(): pl.pallas_call(kernel, out_shape=[jax.ShapeDtypeStruct(shape, dtype) for...  94.8 us
    dot_general x34, matrix products, over_rows(): jnp.einsum('ra,rb->ab', left_in, right_in, preferred_element_type=F32)  44.3 us
    dot_general x12, matrix products, times_t(): jnp.einsum('...a,ba->...b', left_in, right_in, preferred_element_type=F32)  39.1 us
    dot_general x12, matrix products, times(): jnp.einsum('...a,ab->...b', left_in, right_in, preferred_element_type=F32)  35.5 us
    ppermute x21, starting transfers between devices, swap_core(): return lax.ppermute(value, 'c', [(0, 1), (1, 0)])  30.4 us
    unnamed x418, local copies, waits for them, and re-layouts  24.4 us
  transfers between devices with their start and end apart: 107, of which 41 were waited for; matrix products, arithmetic and copies ran while one was open for 26% of the time, Pallas kernels for 8%

profile of v3, /device:TPU:1, one launch (start us, length us, event | category | flops | bytes accessed | tf_op | source)
XLA Modules:
  0.0 829.3 jit_solution(9407124978150589690)
XLA Ops:
  22.6 4.5 collective-permute-done.5.refs_1_
  27.1 12.1 %collective-permute-done.2.refs_2_ = bf16[128,1152]{1,0:T(8,128)(2,1)} collective-permute-done((bf16[128,1152]{1,0:T(8,128)(2,1)}, bf16[128,1152]{1,0:T(8,128)(2,1)}, u32[]{:S(2)}, u32[]{:S(2)}) %collective-permute-start.2) | collective-permute-done | bytes 294944 | tf_op jit(solution)/shard_map/ppermute | solution.py:72
  39.2 7.2 collective-permute-start.6
  55.2 21.3 %collective-permute-done.9.refs_1_ = bf16[512,1152]{1,0:T(8,128)(2,1)} collective-permute-done((bf16[512,1152]{1,0:T(8,128)(2,1)}, bf16[512,1152]{1,0:T(8,128)(2,1)}, u32[]{:S(2)}, u32[]{:S(2)}) %collective-permute-start.9) | collective-permute-done | bytes 1179680 | tf_op jit(solution)/shard_map/ppermute | solution.py:72
  82.9 4.5 shard_map.299
  102.8 5.6 shard_map.301
  139.4 3.8 collective-permute-done.20.refs_5_
  143.3 6.0 collective-permute-done.21.refs_6_
  177.9 4.6 collective-permute-done.30.refs_14_
  183.2 3.9 shard_map.305.refs_0_
  198.4 4.2 collective-permute-done.33
  202.6 25.0 %collective-permute-done.34 = bf16[128,2048]{1,0:T(8,128)(2,1)S(1)} collective-permute-done((bf16[128,2048]{1,0:T(8,128)(2,1)S(1)}, bf16[128,2048]{1,0:T(8,128)(2,1)S(1)}, u32[]{:S(2)}, u32[]{:S(2)}) %collective-permute-start.34) | collective-permute-done | bytes 524320 | tf_op jit(solution)/shard_map/ppermute | solution.py:72
  227.6 5.1 collective-permute-done.36.refs_0_.refs_1_
  245.1 5.1 collective-permute-start.38
  251.8 10.4 %collective-permute-done.38.refs_1_ = bf16[128,2048]{1,0:T(8,128)(2,1)S(1)} collective-permute-done((bf16[128,2048]{1,0:T(8,128)(2,1)}, bf16[128,2048]{1,0:T(8,128)(2,1)S(1)}, u32[]{:S(2)}, u32[]{:S(2)}) %collective-permute-start.38) | collective-permute-done | bytes 524320 | tf_op jit(solution)/shard_map/ppermute | solution.py:72
  262.2 34.5 %collective-permute-done.39.refs_2_ = bf16[128,2048]{1,0:T(8,128)(2,1)S(1)} collective-permute-done((bf16[128,2048]{1,0:T(8,128)(2,1)}, bf16[128,2048]{1,0:T(8,128)(2,1)S(1)}, u32[]{:S(2)}, u32[]{:S(2)}) %collective-permute-start.39) | collective-permute-done | bytes 524320 | tf_op jit(solution)/shard_map/ppermute | solution.py:72
  297.6 3.7 shard_map.308.refs_0_
  309.1 8.5 %shard_map.309 = bf16[2048,2048]{1,0:T(8,128)(2,1)} custom-call(s32[16]{0:T(128)} %stack.350.table_ref, bf16[512,2048]{1,0:T(8,128)(2,1)} %shard_map.305.refs_0_, bf16[512,2048]{1,0:T(8,128)(2,1)} %collective-permute-done.36.refs_0_.refs_1_, bf16[512,2048]{1,0:T(8,128)(2,1)} %collective-permute-done.37.refs_0_.refs_2_, bf16[512,2048]{1,0:T(8,128)(2,1)} %copy-done.37, ...), custom_call_target="tpu_custom_call" | custom-call | bytes 16777216 | tf_op jit(solution)/shard_map/pallas_call | solution.py:157
  317.7 7.1 fusion.198
  326.7 6.6 fusion.199
  335.3 5.7 shard_map.310
  341.0 5.9 convolution_convert_fusion
  347.6 5.5 collective-permute-done.46
  353.1 5.2 fusion.193
  363.0 10.6 %collective-permute-done.48 = bf16[128,2048]{1,0:T(8,128)(2,1)S(1)} collective-permute-done((bf16[128,2048]{1,0:T(8,128)(2,1)S(1)}, bf16[128,2048]{1,0:T(8,128)(2,1)S(1)}, u32[]{:S(2)}, u32[]{:S(2)}) %collective-permute-start.48) | collective-permute-done | bytes 524320 | tf_op jit(solution)/shard_map/ppermute | solution.py:72
  373.7 21.6 %collective-permute-done.49 = bf16[128,2048]{1,0:T(8,128)(2,1)S(1)} collective-permute-done((bf16[128,2048]{1,0:T(8,128)(2,1)S(1)}, bf16[128,2048]{1,0:T(8,128)(2,1)S(1)}, u32[]{:S(2)}, u32[]{:S(2)}) %collective-permute-start.49) | collective-permute-done | bytes 524320 | tf_op jit(solution)/shard_map/ppermute | solution.py:72
  401.3 11.4 %collective-permute-start.51 = (bf16[128,2048]{1,0:T(8,128)(2,1)S(1)}, bf16[128,2048]{1,0:T(8,128)(2,1)S(1)}, u32[]{:S(2)}, u32[]{:S(2)}) collective-permute-start(bf16[128,2048]{1,0:T(8,128)(2,1)S(1)} %fusion.44.refs_0_), channel_id=1, source_target_pairs={{0,24},{8,0},{16,8},{24,16},{1,25},{9,1},{17,9},{25,17},{2,26},{10... | collective-permute-start | bytes 1572872 | tf_op jit(solution)/shard_map/ppermute | solution.py:72
  417.1 5.3 collective-permute-done.54
  423.9 34.6 %collective-permute-done.52.refs_2_ = bf16[128,2048]{1,0:T(8,128)(2,1)S(1)} collective-permute-done((bf16[128,2048]{1,0:T(8,128)(2,1)S(1)}, bf16[128,2048]{1,0:T(8,128)(2,1)S(1)}, u32[]{:S(2)}, u32[]{:S(2)}) %collective-permute-start.52) | collective-permute-done | bytes 524320 | tf_op jit(solution)/shard_map/ppermute | solution.py:72
  467.5 6.9 fusion.22
  481.3 5.7 convolution_convert_fusion.2
  493.6 8.5 %fusion.194 = (bf16[512,2048]{1,0:T(8,128)(2,1)S(1)}, f32[512,2048]{1,0:T(8,128)S(1)}) fusion(bf16[512,2048]{1,0:T(8,128)(2,1)} %collective-permute-done.59, bf16[512,2048]{1,0:T(8,128)(2,1)S(1)} %copy-done.7, bf16[2048,2048]{1,0:T(8,128)(2,1)} %shard_map.309), kind=kOutput, calls=%fused_computation.533 | convolution fusion | flops 4298113024 | bytes 18874368 | tf_op jit(solution)/shard_map/...a,ba->...b/dot_general | solution.py:64
  505.8 6.0 shard_map.312
  554.7 13.8 %collective-permute-done.66 = bf16[384,2048]{1,0:T(8,128)(2,1)S(1)} collective-permute-done((bf16[384,2048]{1,0:T(8,128)(2,1)}, bf16[384,2048]{1,0:T(8,128)(2,1)S(1)}, u32[]{:S(2)}, u32[]{:S(2)}) %collective-permute-start.66) | collective-permute-done | bytes 1572896 | tf_op jit(solution)/shard_map/ppermute | solution.py:72
  584.2 6.2 shard_map.315
  599.0 19.3 %collective-permute-done.69.refs_2_ = bf16[128,2048]{1,0:T(8,128)(2,1)} collective-permute-done((bf16[128,2048]{1,0:T(8,128)(2,1)}, bf16[128,2048]{1,0:T(8,128)(2,1)}, u32[]{:S(2)}, u32[]{:S(2)}) %collective-permute-start.69) | collective-permute-done | bytes 524320 | tf_op jit(solution)/shard_map/ppermute | solution.py:72
  618.3 4.5 collective-permute-done.71
  628.3 5.3 collective-permute-start.73
  633.6 4.1 add_convert_fusion
  656.1 9.4 %collective-permute-done.79 = bf16[256,2048]{1,0:T(8,128)(2,1)S(1)} collective-permute-done((bf16[256,2048]{1,0:T(8,128)(2,1)S(1)}, bf16[256,2048]{1,0:T(8,128)(2,1)S(1)}, u32[]{:S(2)}, u32[]{:S(2)}) %collective-permute-start.79) | collective-permute-done | bytes 1048608 | tf_op jit(solution)/shard_map/ppermute | solution.py:72
  672.0 5.0 collective-permute-start.82
  688.1 4.8 fusion.195
  709.8 4.5 fusion.172
  737.6 4.9 shard_map.317
  750.1 7.1 collective-permute-done.91
  770.7 11.5 %collective-permute-done.94 = bf16[656,768]{1,0:T(8,128)(2,1)S(1)} collective-permute-done((bf16[656,768]{1,0:T(8,128)(2,1)S(1)}, bf16[656,768]{1,0:T(8,128)(2,1)S(1)}, u32[]{:S(2)}, u32[]{:S(2)}) %collective-permute-start.94) | collective-permute-done | bytes 1007648 | tf_op jit(solution)/shard_map/ppermute | solution.py:72
  783.7 3.9 collective-permute-start.97
  802.2 3.7 shard_map.320
  (943 shorter events, 400.3 us)
Async XLA Ops:
  12.6 26.6 %collective-permute-start.4 = (bf16[64,16384]{1,0:T(8,128)(2,1)S(1)}, bf16[64,16384]{1,0:T(8,128)(2,1)}, u32[]{:S(2)}, u32[]{:S(2)}) collective-permute-start(bf16[64,16384]{1,0:T(8,128)(2,1)S(1)} %pad_maximum_fusion.refs_0_), channel_id=1, source_target_pairs={{0,1},{1,0},{2,3},{3,2},{4,5},{5,4},{6,7},{7,6},{8,9},{9,8},{10,11... | collective-permute-start | bytes 6291464 | tf_op jit(solution)/shard_map/ppermute | solution.py:76
  16.7 22.5 %collective-permute-start.2 = (bf16[128,1152]{1,0:T(8,128)(2,1)}, bf16[128,1152]{1,0:T(8,128)(2,1)}, u32[]{:S(2)}, u32[]{:S(2)}) collective-permute-start(bf16[128,1152]{1,0:T(8,128)(2,1)} %get-tuple-element.451), channel_id=1, source_target_pairs={{0,16},{8,24},{16,0},{24,8},{1,17},{9,25},{17,1},{25,9},{2,18},{10... | collective-permute-start | bytes 884744 | tf_op jit(solution)/shard_map/ppermute | solution.py:72
  19.0 20.2 %collective-permute-start.3 = (bf16[128,1152]{1,0:T(8,128)(2,1)}, bf16[128,1152]{1,0:T(8,128)(2,1)}, u32[]{:S(2)}, u32[]{:S(2)}) collective-permute-start(bf16[128,1152]{1,0:T(8,128)(2,1)} %get-tuple-element.452), channel_id=1, source_target_pairs={{0,24},{8,0},{16,8},{24,16},{1,25},{9,1},{17,9},{25,17},{2,26},{10... | collective-permute-start | bytes 884744 | tf_op jit(solution)/shard_map/ppermute | solution.py:72
  39.2 55.5 %collective-permute-start.6 = (bf16[128,2048]{1,0:T(8,128)(2,1)S(1)}, bf16[128,2048]{1,0:T(8,128)(2,1)}, u32[]{:S(2)}, u32[]{:S(2)}) collective-permute-start(bf16[128,2048]{1,0:T(8,128)(2,1)S(1)} %bitcast.283), channel_id=1, source_target_pairs={{0,24},{8,0},{16,8},{24,16},{1,25},{9,1},{17,9},{25,17},{2,26},{10... | collective-permute-start | bytes 1572872 | tf_op jit(solution)/shard_map/ppermute | solution.py:72
  46.4 48.3 %collective-permute-start.7 = (bf16[128,2048]{1,0:T(8,128)(2,1)S(1)}, bf16[128,2048]{1,0:T(8,128)(2,1)}, u32[]{:S(2)}, u32[]{:S(2)}) collective-permute-start(bf16[128,2048]{1,0:T(8,128)(2,1)S(1)} %bitcast.284), channel_id=1, source_target_pairs={{0,16},{8,24},{16,0},{24,8},{1,17},{9,25},{17,1},{25,9},{2,18},{10... | collective-permute-start | bytes 1572872 | tf_op jit(solution)/shard_map/ppermute | solution.py:72
  47.0 47.7 %collective-permute-start.8 = (bf16[128,2048]{1,0:T(8,128)(2,1)S(1)}, bf16[128,2048]{1,0:T(8,128)(2,1)}, u32[]{:S(2)}, u32[]{:S(2)}) collective-permute-start(bf16[128,2048]{1,0:T(8,128)(2,1)S(1)} %bitcast.285), channel_id=1, source_target_pairs={{0,8},{8,16},{16,24},{24,0},{1,9},{9,17},{17,25},{25,1},{2,10},{10... | collective-permute-start | bytes 1572872 | tf_op jit(solution)/shard_map/ppermute | solution.py:72
  50.0 26.5 %collective-permute-start.9 = (bf16[512,1152]{1,0:T(8,128)(2,1)}, bf16[512,1152]{1,0:T(8,128)(2,1)}, u32[]{:S(2)}, u32[]{:S(2)}) collective-permute-start(bf16[512,1152]{1,0:T(8,128)(2,1)} %shard_map.298.refs_0_), channel_id=1, source_target_pairs={{0,2},{2,0},{1,3},{3,1},{4,6},{6,4},{5,7},{7,5},{8,10},{10,8},{9,1... | collective-permute-start | bytes 3538952 | tf_op jit(solution)/shard_map/ppermute | solution.py:72
  51.2 26.2 %collective-permute-start.10 = (bf16[512,1152]{1,0:T(8,128)(2,1)}, bf16[512,1152]{1,0:T(8,128)(2,1)}, u32[]{:S(2)}, u32[]{:S(2)}) collective-permute-start(bf16[512,1152]{1,0:T(8,128)(2,1)} %shard_map.298.refs_0_), channel_id=1, source_target_pairs={{0,4},{4,0},{1,5},{5,1},{2,6},{6,2},{3,7},{7,3},{8,12},{12,8},{9,1... | collective-permute-start | bytes 3538952 | tf_op jit(solution)/shard_map/ppermute | solution.py:72
  98.1 19.1 %collective-permute-start.14 = (bf16[512,2048]{1,0:T(8,128)(2,1)}, bf16[512,2048]{1,0:T(8,128)(2,1)}, u32[]{:S(2)}, u32[]{:S(2)}) collective-permute-start(bf16[512,2048]{1,0:T(8,128)(2,1)} %shard_map.302), channel_id=1, source_target_pairs={{0,1},{1,0},{2,3},{3,2},{4,5},{5,4},{6,7},{7,6},{8,9},{9,8},{10,11... | collective-permute-start | bytes 6291464 | tf_op jit(solution)/shard_map/ppermute | solution.py:76
  129.4 19.9 %collective-permute-start.19 = (bf16[512,512]{1,0:T(8,128)(2,1)S(1)}, bf16[512,512]{1,0:T(8,128)(2,1)S(1)}, u32[]{:S(2)}, u32[]{:S(2)}) collective-permute-start(bf16[512,512]{1,0:T(8,128)(2,1)S(1)} %get-tuple-element.538), channel_id=1, source_target_pairs={{0,4},{4,0},{1,5},{5,1},{2,6},{6,2},{3,7},{7,3},{8,12},{12,8},{9,1... | collective-permute-start | bytes 1572872 | tf_op jit(solution)/shard_map/ppermute | solution.py:72
  187.1 45.6 %collective-permute-start.36 = (bf16[512,2048]{1,0:T(8,128)(2,1)}, bf16[512,2048]{1,0:T(8,128)(2,1)}, u32[]{:S(2)}, u32[]{:S(2)}) collective-permute-start(bf16[512,2048]{1,0:T(8,128)(2,1)} %shard_map.305.refs_0_), channel_id=1, source_target_pairs={{0,2},{2,0},{1,3},{3,1},{4,6},{6,4},{5,7},{7,5},{8,10},{10,8},{9,1... | collective-permute-start | bytes 6291464 | tf_op jit(solution)/shard_map/ppermute | solution.py:72
  188.2 45.4 %collective-permute-start.37 = (bf16[512,2048]{1,0:T(8,128)(2,1)}, bf16[512,2048]{1,0:T(8,128)(2,1)}, u32[]{:S(2)}, u32[]{:S(2)}) collective-permute-start(bf16[512,2048]{1,0:T(8,128)(2,1)} %shard_map.305.refs_0_), channel_id=1, source_target_pairs={{0,4},{4,0},{1,5},{5,1},{2,6},{6,2},{3,7},{7,3},{8,12},{12,8},{9,1... | collective-permute-start | bytes 6291464 | tf_op jit(solution)/shard_map/ppermute | solution.py:72
  192.3 35.3 %collective-permute-start.34 = (bf16[128,2048]{1,0:T(8,128)(2,1)S(1)}, bf16[128,2048]{1,0:T(8,128)(2,1)S(1)}, u32[]{:S(2)}, u32[]{:S(2)}) collective-permute-start(bf16[128,2048]{1,0:T(8,128)(2,1)S(1)} %get-tuple-element.581), channel_id=1, source_target_pairs={{0,16},{8,24},{16,0},{24,8},{1,17},{9,25},{17,1},{25,9},{2,18},{10... | collective-permute-start | bytes 1572872 | tf_op jit(solution)/shard_map/ppermute | solution.py:72
  192.5 35.1 %collective-permute-start.35 = (bf16[128,2048]{1,0:T(8,128)(2,1)S(1)}, bf16[128,2048]{1,0:T(8,128)(2,1)S(1)}, u32[]{:S(2)}, u32[]{:S(2)}) collective-permute-start(bf16[128,2048]{1,0:T(8,128)(2,1)S(1)} %get-tuple-element.582), channel_id=1, source_target_pairs={{0,24},{8,0},{16,8},{24,16},{1,25},{9,1},{17,9},{25,17},{2,26},{10... | collective-permute-start | bytes 1572872 | tf_op jit(solution)/shard_map/ppermute | solution.py:72
  240.6 56.1 %collective-permute-start.41 = (bf16[512,2048]{1,0:T(8,128)(2,1)}, bf16[512,2048]{1,0:T(8,128)(2,1)S(1)}, u32[]{:S(2)}, u32[]{:S(2)}) collective-permute-start(bf16[512,2048]{1,0:T(8,128)(2,1)} %shard_map.306), channel_id=1, source_target_pairs={{0,4},{4,0},{1,5},{5,1},{2,6},{6,2},{3,7},{7,3},{8,12},{12,8},{9,1... | collective-permute-start | bytes 6291464 | tf_op jit(solution)/shard_map/ppermute | solution.py:72
  244.9 52.8 %collective-permute-start.42 = (bf16[512,2048]{1,0:T(8,128)(2,1)}, bf16[512,2048]{1,0:T(8,128)(2,1)}, u32[]{:S(2)}, u32[]{:S(2)}) collective-permute-start(bf16[512,2048]{1,0:T(8,128)(2,1)} %shard_map.307), channel_id=1, source_target_pairs={{0,2},{2,0},{1,3},{3,1},{4,6},{6,4},{5,7},{7,5},{8,10},{10,8},{9,1... | collective-permute-start | bytes 6291464 | tf_op jit(solution)/shard_map/ppermute | solution.py:72
  250.2 46.5 %collective-permute-start.39 = (bf16[128,2048]{1,0:T(8,128)(2,1)}, bf16[128,2048]{1,0:T(8,128)(2,1)S(1)}, u32[]{:S(2)}, u32[]{:S(2)}) collective-permute-start(bf16[128,2048]{1,0:T(8,128)(2,1)} %multiply_convert_fusion.5.refs_0_), channel_id=1, source_target_pairs={{0,16},{8,24},{16,0},{24,8},{1,17},{9,25},{17,1},{25,9},{2,18},{10... | collective-permute-start | bytes 1572872 | tf_op jit(solution)/shard_map/ppermute | solution.py:72
  251.8 44.9 %collective-permute-start.40 = (bf16[128,2048]{1,0:T(8,128)(2,1)}, bf16[128,2048]{1,0:T(8,128)(2,1)S(1)}, u32[]{:S(2)}, u32[]{:S(2)}) collective-permute-start(bf16[128,2048]{1,0:T(8,128)(2,1)} %multiply_convert_fusion.5.refs_0_), channel_id=1, source_target_pairs={{0,8},{8,16},{16,24},{24,0},{1,9},{9,17},{17,25},{25,1},{2,10},{10... | collective-permute-start | bytes 1572872 | tf_op jit(solution)/shard_map/ppermute | solution.py:72
  301.4 25.4 %collective-permute-start.43 = (bf16[512,2048]{1,0:T(8,128)(2,1)}, bf16[512,2048]{1,0:T(8,128)(2,1)}, u32[]{:S(2)}, u32[]{:S(2)}) collective-permute-start(bf16[512,2048]{1,0:T(8,128)(2,1)} %shard_map.308.refs_0_), channel_id=1, source_target_pairs={{0,1},{1,0},{2,3},{3,2},{4,5},{5,4},{6,7},{7,6},{8,9},{9,8},{10,11... | collective-permute-start | bytes 6291464 | tf_op jit(solution)/shard_map/ppermute | solution.py:76
  306.4 28.9 %collective-permute-start.44 = (bf16[128,2048]{1,0:T(8,128)(2,1)}, bf16[128,2048]{1,0:T(8,128)(2,1)}, u32[]{:S(2)}, u32[]{:S(2)}) collective-permute-start(bf16[128,2048]{1,0:T(8,128)(2,1)} %slice.626), channel_id=1, source_target_pairs={{0,4},{4,0},{1,5},{5,1},{2,6},{6,2},{3,7},{7,3},{8,12},{12,8},{9,1... | collective-permute-start | bytes 1572872 | tf_op jit(solution)/shard_map/ppermute | solution.py:72
  307.9 27.3 %collective-permute-start.45 = (bf16[128,2048]{1,0:T(8,128)(2,1)}, bf16[128,2048]{1,0:T(8,128)(2,1)}, u32[]{:S(2)}, u32[]{:S(2)}) collective-permute-start(bf16[128,2048]{1,0:T(8,128)(2,1)} %slice.627), channel_id=1, source_target_pairs={{0,2},{2,0},{1,3},{3,1},{4,6},{6,4},{5,7},{7,5},{8,10},{10,8},{9,1... | collective-permute-start | bytes 1572872 | tf_op jit(solution)/shard_map/ppermute | solution.py:72
  358.7 36.6 %collective-permute-start.49 = (bf16[128,2048]{1,0:T(8,128)(2,1)S(1)}, bf16[128,2048]{1,0:T(8,128)(2,1)S(1)}, u32[]{:S(2)}, u32[]{:S(2)}) collective-permute-start(bf16[128,2048]{1,0:T(8,128)(2,1)S(1)} %get-tuple-element.633), channel_id=1, source_target_pairs={{0,16},{8,24},{16,0},{24,8},{1,17},{9,25},{17,1},{25,9},{2,18},{10... | collective-permute-start | bytes 1572872 | tf_op jit(solution)/shard_map/ppermute | solution.py:72
  359.0 36.3 %collective-permute-start.50 = (bf16[128,2048]{1,0:T(8,128)(2,1)S(1)}, bf16[128,2048]{1,0:T(8,128)(2,1)S(1)}, u32[]{:S(2)}, u32[]{:S(2)}) collective-permute-start(bf16[128,2048]{1,0:T(8,128)(2,1)S(1)} %get-tuple-element.634), channel_id=1, source_target_pairs={{0,24},{8,0},{16,8},{24,16},{1,25},{9,1},{17,9},{25,17},{2,26},{10... | collective-permute-start | bytes 1572872 | tf_op jit(solution)/shard_map/ppermute | solution.py:72
  401.3 22.6 %collective-permute-start.51 = (bf16[128,2048]{1,0:T(8,128)(2,1)S(1)}, bf16[128,2048]{1,0:T(8,128)(2,1)S(1)}, u32[]{:S(2)}, u32[]{:S(2)}) collective-permute-start(bf16[128,2048]{1,0:T(8,128)(2,1)S(1)} %fusion.44.refs_0_), channel_id=1, source_target_pairs={{0,24},{8,0},{16,8},{24,16},{1,25},{9,1},{17,9},{25,17},{2,26},{10... | collective-permute-start | bytes 1572872 | tf_op jit(solution)/shard_map/ppermute | solution.py:72
  412.7 45.8 %collective-permute-start.52 = (bf16[128,2048]{1,0:T(8,128)(2,1)S(1)}, bf16[128,2048]{1,0:T(8,128)(2,1)S(1)}, u32[]{:S(2)}, u32[]{:S(2)}) collective-permute-start(bf16[128,2048]{1,0:T(8,128)(2,1)S(1)} %fusion.44.refs_0_), channel_id=1, source_target_pairs={{0,16},{8,24},{16,0},{24,8},{1,17},{9,25},{17,1},{25,9},{2,18},{10... | collective-permute-start | bytes 1572872 | tf_op jit(solution)/shard_map/ppermute | solution.py:72
  414.1 44.5 %collective-permute-start.53 = (bf16[128,2048]{1,0:T(8,128)(2,1)S(1)}, bf16[128,2048]{1,0:T(8,128)(2,1)S(1)}, u32[]{:S(2)}, u32[]{:S(2)}) collective-permute-start(bf16[128,2048]{1,0:T(8,128)(2,1)S(1)} %fusion.44.refs_0_), channel_id=1, source_target_pairs={{0,8},{8,16},{16,24},{24,0},{1,9},{9,17},{17,25},{25,1},{2,10},{10... | collective-permute-start | bytes 1572872 | tf_op jit(solution)/shard_map/ppermute | solution.py:72
  504.3 26.0 %collective-permute-start.63 = (bf16[128,2048]{1,0:T(8,128)(2,1)}, bf16[128,2048]{1,0:T(8,128)(2,1)}, u32[]{:S(2)}, u32[]{:S(2)}) collective-permute-start(bf16[128,2048]{1,0:T(8,128)(2,1)} %get-tuple-element.662), channel_id=1, source_target_pairs={{0,16},{8,24},{16,0},{24,8},{1,17},{9,25},{17,1},{25,9},{2,18},{10... | collective-permute-start | bytes 1572872 | tf_op jit(solution)/shard_map/ppermute | solution.py:72
  530.3 24.4 %collective-permute-start.64 = (bf16[128,2048]{1,0:T(8,128)(2,1)}, bf16[128,2048]{1,0:T(8,128)(2,1)S(1)}, u32[]{:S(2)}, u32[]{:S(2)}) collective-permute-start(bf16[128,2048]{1,0:T(8,128)(2,1)} %get-tuple-element.683), channel_id=1, source_target_pairs={{0,8},{8,16},{16,24},{24,0},{1,9},{9,17},{17,25},{25,1},{2,10},{10... | collective-permute-start | bytes 1572872 | tf_op jit(solution)/shard_map/ppermute | solution.py:72
  530.3 24.4 %collective-permute-start.65 = (bf16[128,2048]{1,0:T(8,128)(2,1)}, bf16[128,2048]{1,0:T(8,128)(2,1)S(1)}, u32[]{:S(2)}, u32[]{:S(2)}) collective-permute-start(bf16[128,2048]{1,0:T(8,128)(2,1)} %get-tuple-element.684), channel_id=1, source_target_pairs={{0,24},{8,0},{16,8},{24,16},{1,25},{9,1},{17,9},{25,17},{2,26},{10... | collective-permute-start | bytes 1572872 | tf_op jit(solution)/shard_map/ppermute | solution.py:72
  533.9 34.6 %collective-permute-start.66 = (bf16[384,2048]{1,0:T(8,128)(2,1)}, bf16[384,2048]{1,0:T(8,128)(2,1)S(1)}, u32[]{:S(2)}, u32[]{:S(2)}) collective-permute-start(bf16[384,2048]{1,0:T(8,128)(2,1)} %shard_map.313), channel_id=1, source_target_pairs={{0,2},{2,0},{1,3},{3,1},{4,6},{6,4},{5,7},{7,5},{8,10},{10,8},{9,1... | collective-permute-start | bytes 4718600 | tf_op jit(solution)/shard_map/ppermute | solution.py:72
  534.7 34.4 %collective-permute-start.67 = (bf16[384,2048]{1,0:T(8,128)(2,1)}, bf16[384,2048]{1,0:T(8,128)(2,1)S(1)}, u32[]{:S(2)}, u32[]{:S(2)}) collective-permute-start(bf16[384,2048]{1,0:T(8,128)(2,1)} %shard_map.314), channel_id=1, source_target_pairs={{0,4},{4,0},{1,5},{5,1},{2,6},{6,2},{3,7},{7,3},{8,12},{12,8},{9,1... | collective-permute-start | bytes 4718600 | tf_op jit(solution)/shard_map/ppermute | solution.py:72
  574.9 23.4 %collective-permute-start.68 = (bf16[128,2048]{1,0:T(8,128)(2,1)}, bf16[128,2048]{1,0:T(8,128)(2,1)}, u32[]{:S(2)}, u32[]{:S(2)}) collective-permute-start(bf16[128,2048]{1,0:T(8,128)(2,1)} %fusion.46.refs_0_), channel_id=1, source_target_pairs={{0,24},{8,0},{16,8},{24,16},{1,25},{9,1},{17,9},{25,17},{2,26},{10... | collective-permute-start | bytes 1572872 | tf_op jit(solution)/shard_map/ppermute | solution.py:72
  575.3 43.0 %collective-permute-start.69 = (bf16[128,2048]{1,0:T(8,128)(2,1)}, bf16[128,2048]{1,0:T(8,128)(2,1)}, u32[]{:S(2)}, u32[]{:S(2)}) collective-permute-start(bf16[128,2048]{1,0:T(8,128)(2,1)} %fusion.46.refs_0_), channel_id=1, source_target_pairs={{0,16},{8,24},{16,0},{24,8},{1,17},{9,25},{17,1},{25,9},{2,18},{10... | collective-permute-start | bytes 1572872 | tf_op jit(solution)/shard_map/ppermute | solution.py:72
  575.3 43.0 %collective-permute-start.70 = (bf16[128,2048]{1,0:T(8,128)(2,1)}, bf16[128,2048]{1,0:T(8,128)(2,1)}, u32[]{:S(2)}, u32[]{:S(2)}) collective-permute-start(bf16[128,2048]{1,0:T(8,128)(2,1)} %fusion.46.refs_0_), channel_id=1, source_target_pairs={{0,8},{8,16},{16,24},{24,0},{1,9},{9,17},{17,25},{25,1},{2,10},{10... | collective-permute-start | bytes 1572872 | tf_op jit(solution)/shard_map/ppermute | solution.py:72
  578.5 44.3 %collective-permute-start.71 = (bf16[512,2048]{1,0:T(8,128)(2,1)}, bf16[512,2048]{1,0:T(8,128)(2,1)}, u32[]{:S(2)}, u32[]{:S(2)}) collective-permute-start(bf16[512,2048]{1,0:T(8,128)(2,1)} %pad_maximum_fusion.4), channel_id=1, source_target_pairs={{0,4},{4,0},{1,5},{5,1},{2,6},{6,2},{3,7},{7,3},{8,12},{12,8},{9,1... | collective-permute-start | bytes 6291464 | tf_op jit(solution)/shard_map/ppermute | solution.py:72
  581.3 44.0 %collective-permute-start.72 = (bf16[512,2048]{1,0:T(8,128)(2,1)}, bf16[512,2048]{1,0:T(8,128)(2,1)}, u32[]{:S(2)}, u32[]{:S(2)}) collective-permute-start(bf16[512,2048]{1,0:T(8,128)(2,1)} %pad_maximum_fusion.5), channel_id=1, source_target_pairs={{0,2},{2,0},{1,3},{3,1},{4,6},{6,4},{5,7},{7,5},{8,10},{10,8},{9,1... | collective-permute-start | bytes 6291464 | tf_op jit(solution)/shard_map/ppermute | solution.py:72
  598.3 57.8 %collective-permute-start.78 = (bf16[256,2048]{1,0:T(8,128)(2,1)}, bf16[256,2048]{1,0:T(8,128)(2,1)}, u32[]{:S(2)}, u32[]{:S(2)}) collective-permute-start(bf16[256,2048]{1,0:T(8,128)(2,1)} %pad_maximum_fusion.15), channel_id=1, source_target_pairs={{0,4},{4,0},{1,5},{5,1},{2,6},{6,2},{3,7},{7,3},{8,12},{12,8},{9,1... | collective-permute-start | bytes 3145736 | tf_op jit(solution)/shard_map/ppermute | solution.py:72
  628.3 18.0 %collective-permute-start.73 = (bf16[512,2048]{1,0:T(8,128)(2,1)}, bf16[512,2048]{1,0:T(8,128)(2,1)S(1)}, u32[]{:S(2)}, u32[]{:S(2)}) collective-permute-start(bf16[512,2048]{1,0:T(8,128)(2,1)} %shard_map.316), channel_id=1, source_target_pairs={{0,1},{1,0},{2,3},{3,2},{4,5},{5,4},{6,7},{7,6},{8,9},{9,8},{10,11... | collective-permute-start | bytes 6291464 | tf_op jit(solution)/shard_map/ppermute | solution.py:76
  640.6 24.9 %collective-permute-start.79 = (bf16[256,2048]{1,0:T(8,128)(2,1)S(1)}, bf16[256,2048]{1,0:T(8,128)(2,1)S(1)}, u32[]{:S(2)}, u32[]{:S(2)}) collective-permute-start(bf16[256,2048]{1,0:T(8,128)(2,1)S(1)} %pad_maximum_fusion.16), channel_id=1, source_target_pairs={{0,2},{2,0},{1,3},{3,1},{4,6},{6,4},{5,7},{7,5},{8,10},{10,8},{9,1... | collective-permute-start | bytes 3145736 | tf_op jit(solution)/shard_map/ppermute | solution.py:72
  643.7 21.8 %collective-permute-start.75 = (bf16[64,2048]{1,0:T(8,128)(2,1)S(1)}, bf16[64,2048]{1,0:T(8,128)(2,1)S(1)}, u32[]{:S(2)}, u32[]{:S(2)}) collective-permute-start(bf16[64,2048]{1,0:T(8,128)(2,1)S(1)} %get-tuple-element.1074), channel_id=1, source_target_pairs={{0,8},{8,16},{16,24},{24,0},{1,9},{9,17},{17,25},{25,1},{2,10},{10... | collective-permute-start | bytes 786440 | tf_op jit(solution)/shard_map/ppermute | solution.py:72
  645.2 20.3 %collective-permute-start.76 = (bf16[64,2048]{1,0:T(8,128)(2,1)S(1)}, bf16[64,2048]{1,0:T(8,128)(2,1)S(1)}, u32[]{:S(2)}, u32[]{:S(2)}) collective-permute-start(bf16[64,2048]{1,0:T(8,128)(2,1)S(1)} %get-tuple-element.1073), channel_id=1, source_target_pairs={{0,16},{8,24},{16,0},{24,8},{1,17},{9,25},{17,1},{25,9},{2,18},{10... | collective-permute-start | bytes 786440 | tf_op jit(solution)/shard_map/ppermute | solution.py:72
  646.3 19.2 %collective-permute-start.77 = (bf16[64,2048]{1,0:T(8,128)(2,1)S(1)}, bf16[64,2048]{1,0:T(8,128)(2,1)S(1)}, u32[]{:S(2)}, u32[]{:S(2)}) collective-permute-start(bf16[64,2048]{1,0:T(8,128)(2,1)S(1)} %get-tuple-element.1072), channel_id=1, source_target_pairs={{0,24},{8,0},{16,8},{24,16},{1,25},{9,1},{17,9},{25,17},{2,26},{10... | collective-permute-start | bytes 786440 | tf_op jit(solution)/shard_map/ppermute | solution.py:72
  717.5 25.5 %collective-permute-start.89 = (bf16[128,2048]{1,0:T(8,128)(2,1)}, bf16[128,2048]{1,0:T(8,128)(2,1)}, u32[]{:S(2)}, u32[]{:S(2)}) collective-permute-start(bf16[128,2048]{1,0:T(8,128)(2,1)} %get-tuple-element.751), channel_id=1, source_target_pairs={{0,16},{8,24},{16,0},{24,8},{1,17},{9,25},{17,1},{25,9},{2,18},{10... | collective-permute-start | bytes 1572872 | tf_op jit(solution)/shard_map/ppermute | solution.py:72
  761.0 21.2 %collective-permute-start.94 = (bf16[656,768]{1,0:T(8,128)(2,1)S(1)}, bf16[656,768]{1,0:T(8,128)(2,1)S(1)}, u32[]{:S(2)}, u32[]{:S(2)}) collective-permute-start(bf16[656,768]{1,0:T(8,128)(2,1)S(1)} %pad_maximum_fusion.18), channel_id=1, source_target_pairs={{0,4},{4,0},{1,5},{5,1},{2,6},{6,2},{3,7},{7,3},{8,12},{12,8},{9,1... | collective-permute-start | bytes 3022856 | tf_op jit(solution)/shard_map/ppermute | solution.py:72
  762.1 20.9 %collective-permute-start.95 = (bf16[656,768]{1,0:T(8,128)(2,1)S(1)}, bf16[656,768]{1,0:T(8,128)(2,1)S(1)}, u32[]{:S(2)}, u32[]{:S(2)}) collective-permute-start(bf16[656,768]{1,0:T(8,128)(2,1)S(1)} %pad_maximum_fusion.19), channel_id=1, source_target_pairs={{0,2},{2,0},{1,3},{3,1},{4,6},{6,4},{5,7},{7,5},{8,10},{10,8},{9,1... | collective-permute-start | bytes 3022856 | tf_op jit(solution)/shard_map/ppermute | solution.py:72
  794.7 21.9 %collective-permute-start.98 = (bf16[64,1920]{1,0:T(8,128)(2,1)}, bf16[64,1920]{1,0:T(8,128)(2,1)S(1)}, u32[]{:S(2)}, u32[]{:S(2)}) collective-permute-start(bf16[64,1920]{1,0:T(8,128)(2,1)} %get-tuple-element.853), channel_id=1, source_target_pairs={{0,8},{8,16},{16,24},{24,0},{1,9},{9,17},{17,25},{25,1},{2,10},{10... | collective-permute-start | bytes 737288 | tf_op jit(solution)/shard_map/ppermute | solution.py:72
  794.7 21.9 %collective-permute-start.99 = (bf16[64,1920]{1,0:T(8,128)(2,1)}, bf16[64,1920]{1,0:T(8,128)(2,1)S(1)}, u32[]{:S(2)}, u32[]{:S(2)}) collective-permute-start(bf16[64,1920]{1,0:T(8,128)(2,1)} %get-tuple-element.854), channel_id=1, source_target_pairs={{0,16},{8,24},{16,0},{24,8},{1,17},{9,25},{17,1},{25,9},{2,18},{10... | collective-permute-start | bytes 737288 | tf_op jit(solution)/shard_map/ppermute | solution.py:72
  796.9 19.8 %collective-permute-start.100 = (bf16[64,1920]{1,0:T(8,128)(2,1)}, bf16[64,1920]{1,0:T(8,128)(2,1)S(1)}, u32[]{:S(2)}, u32[]{:S(2)}) collective-permute-start(bf16[64,1920]{1,0:T(8,128)(2,1)} %get-tuple-element.855), channel_id=1, source_target_pairs={{0,24},{8,0},{16,8},{24,16},{1,25},{9,1},{17,9},{25,17},{2,26},{10... | collective-permute-start | bytes 737288 | tf_op jit(solution)/shard_map/ppermute | solution.py:72
  (266 other events, 2370.1 us)

commit v4 on v3

--- a/solution.py
+++ b/solution.py
@@ -179,7 +179,8 @@
 
 
 def z_take(block):
-    return [block if k == 0 else give_to(block, "z", Z, -k) for k in range(Z)]
+    taken = {k: give_to(block, "z", Z, -k) for k in (2, 3, 1)}
+    return [block] + [taken[k] for k in range(1, Z)]
 
 
 def flat_step(step_y, step_x, y_count):
@@ -254,7 +255,8 @@
 
 
 def z_shares(blocks):
-    return [blocks[0]] + [give_to(blocks[k], "z", Z, k) for k in range(1, Z)]
+    given = {k: give_to(blocks[k], "z", Z, k) for k in (2, 3, 1)}
+    return [blocks[0]] + [given[k] for k in range(1, Z)]
 
 
 def add_up(pieces):
@@ -273,7 +275,8 @@
 
 
 def z_send(sends):
-    return [sends(k) if k == 0 else give_to(sends(k), "z", Z, k) for k in range(Z)]
+    given = {k: give_to(sends(k), "z", Z, k) for k in (2, 3, 1)}
+    return [sends(0)] + [given[k] for k in range(1, Z)]
 
 
 def z_place(arrived, zi):
@@ -488,22 +491,6 @@
     frequency = ROPE_BASE ** (-2.0 * jnp.arange(HD // 2, dtype=F32) / HD)
     angles = relative.astype(F32)[:, None] * frequency[None, :]
     cos_tab, sine_tab = jnp.cos(angles), jnp.sin(angles)
-    (
-        token_take, first_rows, first_got, ff_sends, visible, cos_tab, sine_tab, out_pair
-    ) = stage(
-        token_take, first_rows, first_got, ff_sends, visible, cos_tab, sine_tab, out_pair
-    )
-    visible = visible > 0.5
-
-    def rotated(raw_in, gain_in):
-        return rotate(rms_norm(raw_in, gain_in), cos_tab, sine_tab)
-
-    def rotated_own(raw_in, gain_in):
-        return rotate(rms_norm(raw_in, gain_in), cos_tab[:group_rows], sine_tab[:group_rows])
-
-    token_own = stack_rows(token_take)
-    token_other = swap_core(token_own)
-    ff_arrived = [z_send(lambda k: ff_sends[0][k])]
     qkv_mat, misc_all, small_late = place_parts(
         first_rows,
         first_got,
@@ -513,6 +500,24 @@
     gain_all = gain_all.reshape(-1, gain_rows, shard).transpose(1, 0, 2)
     gains = gain_all[:gain_count].reshape(gain_count, -1).astype(F32)
     qk = gain_all[gain_count:, :, :qk_shard].reshape(2, -1).astype(F32)
+    (
+        token_take, qkv_mat, misc_all, small_late, gains, qk, ff_sends, visible, cos_tab, sine_tab,
+        out_pair,
+    ) = stage(
+        token_take, qkv_mat, misc_all, small_late, gains, qk, ff_sends, visible, cos_tab, sine_tab,
+        out_pair,
+    )
+    visible = visible > 0.5
+
+    def rotated(raw_in, gain_in):
+        return rotate(rms_norm(raw_in, gain_in), cos_tab, sine_tab)
+
+    def rotated_own(raw_in, gain_in):
+        return rotate(rms_norm(raw_in, gain_in), cos_tab[:group_rows], sine_tab[:group_rows])
+
+    token_own = stack_rows(token_take)
+    token_other = swap_core(token_own)
+    ff_arrived = [z_send(lambda k: ff_sends[0][k])]
     lr_own = misc_all.reshape(-1, unit, lanes)[:, :shard].reshape(-1, lanes)
     unit_own = unit_norm(token_own.astype(F32))
     unit_other = unit_norm(token_other.astype(F32))

time: 837 us -> 834 us (level)
    unnamed x418 -> x436, local copies, waits for them, and re-layouts: 24.4 us -> 25.1 us
  transfers between devices with their start and end apart: 107 -> 107, of which waited for: 41 -> 39; matrix products, arithmetic and copies ran while one was open for 26% -> 25% of each run, Pallas kernels for 8% -> 8%
where the time goes in v4:
time: 834 us; the launch traced here: 826 us
  waiting for transfers between devices  298 us (36%)
  starting transfers between devices  151 us (18%)
  matrix products  126 us (15%)
  Pallas kernels  94.2 us (11%)
  other arithmetic  88 us (11%)
  local copies, waits for them, and re-layouts  62.9 us (8%)
    ppermute x86, waiting for transfers between devices, give_to(): lax.ppermute(value, axis, [(i, (i + step) % size) for i in range(size)])  291 us
    ppermute x86, starting transfers between devices, give_to(): lax.ppermute(value, axis, [(i, (i + step) % size) for i in range(size)])  121 us
    pallas_call x24, Pallas kernels, shuffle(): pl.pallas_call(kernel, out_shape=[jax.ShapeDtypeStruct(shape, dtype) for...  94.2 us
    dot_general x34, matrix products, over_rows(): jnp.einsum('ra,rb->ab', left_in, right_in, preferred_element_type=F32)  44.3 us
    dot_general x12, matrix products, times_t(): jnp.einsum('...a,ba->...b', left_in, right_in, preferred_element_type=F32)  39.2 us
    dot_general x12, matrix products, times(): jnp.einsum('...a,ab->...b', left_in, right_in, preferred_element_type=F32)  35.5 us
    ppermute x21, starting transfers between devices, swap_core(): return lax.ppermute(value, 'c', [(0, 1), (1, 0)])  30.6 us
    unnamed x436, local copies, waits for them, and re-layouts  25.1 us
  transfers between devices with their start and end apart: 107, of which 39 were waited for; matrix products, arithmetic and copies ran while one was open for 25% of the time, Pallas kernels for 8%

profile of v4, /device:TPU:1, one launch (start us, length us, event | category | flops | bytes accessed | tf_op | source)
XLA Modules:
  0.0 825.5 jit_solution(14742864101308429017)
XLA Ops:
  27.8 12.1 %collective-permute-done.2.refs_2_ = bf16[128,1152]{1,0:T(8,128)(2,1)S(1)} collective-permute-done((bf16[128,1152]{1,0:T(8,128)(2,1)S(1)}, bf16[128,1152]{1,0:T(8,128)(2,1)S(1)}, u32[]{:S(2)}, u32[]{:S(2)}) %collective-permute-start.2) | collective-permute-done | bytes 294944 | tf_op jit(solution)/shard_map/ppermute | solution.py:72
  39.9 7.0 collective-permute-start.6
  56.8 20.5 %collective-permute-done.9.refs_1_ = bf16[512,1152]{1,0:T(8,128)(2,1)} collective-permute-done((bf16[512,1152]{1,0:T(8,128)(2,1)}, bf16[512,1152]{1,0:T(8,128)(2,1)}, u32[]{:S(2)}, u32[]{:S(2)}) %collective-permute-start.9) | collective-permute-done | bytes 1179680 | tf_op jit(solution)/shard_map/ppermute | solution.py:72
  87.3 4.5 shard_map.300
  95.7 5.5 shard_map.299
  105.3 3.7 collective-permute-start.14
  139.6 6.0 collective-permute-done.21.refs_6_
  174.4 3.9 collective-permute-done.30.refs_14_
  179.1 3.7 shard_map.305.refs_0_
  193.0 5.0 collective-permute-done.33
  197.9 25.0 %collective-permute-done.34 = bf16[128,2048]{1,0:T(8,128)(2,1)S(1)} collective-permute-done((bf16[128,2048]{1,0:T(8,128)(2,1)}, bf16[128,2048]{1,0:T(8,128)(2,1)S(1)}, u32[]{:S(2)}, u32[]{:S(2)}) %collective-permute-start.34) | collective-permute-done | bytes 524320 | tf_op jit(solution)/shard_map/ppermute | solution.py:72
  223.0 5.5 collective-permute-done.36.refs_0_.refs_1_
  241.0 4.9 collective-permute-start.38
  248.0 9.8 %collective-permute-done.38.refs_1_ = bf16[128,2048]{1,0:T(8,128)(2,1)S(1)} collective-permute-done((bf16[128,2048]{1,0:T(8,128)(2,1)}, bf16[128,2048]{1,0:T(8,128)(2,1)S(1)}, u32[]{:S(2)}, u32[]{:S(2)}) %collective-permute-start.38) | collective-permute-done | bytes 524320 | tf_op jit(solution)/shard_map/ppermute | solution.py:72
  257.8 34.5 %collective-permute-done.39.refs_2_ = bf16[128,2048]{1,0:T(8,128)(2,1)S(1)} collective-permute-done((bf16[128,2048]{1,0:T(8,128)(2,1)}, bf16[128,2048]{1,0:T(8,128)(2,1)S(1)}, u32[]{:S(2)}, u32[]{:S(2)}) %collective-permute-start.39) | collective-permute-done | bytes 524320 | tf_op jit(solution)/shard_map/ppermute | solution.py:72
  293.3 3.7 shard_map.308.refs_0_
  304.5 8.7 %shard_map.309 = bf16[2048,2048]{1,0:T(8,128)(2,1)} custom-call(s32[16]{0:T(128)} %stack.350.table_ref, bf16[512,2048]{1,0:T(8,128)(2,1)} %shard_map.305.refs_0_, bf16[512,2048]{1,0:T(8,128)(2,1)} %copy-done.54, bf16[512,2048]{1,0:T(8,128)(2,1)} %collective-permute-done.37.refs_0_.refs_2_, bf16[512,2048]{1,0:T(8,128)(2,1)} %copy-done.39, ...), custom_call_target="tpu_custom_call" | custom-call | bytes 16777216 | tf_op jit(solution)/shard_map/pallas_call | solution.py:157
  313.2 7.1 fusion.200
  322.3 6.6 fusion.201
  330.8 5.7 shard_map.310
  336.5 5.9 convolution_convert_fusion
  343.0 5.6 collective-permute-done.46
  348.6 5.2 fusion.195
  358.5 10.7 %collective-permute-done.48 = bf16[128,2048]{1,0:T(8,128)(2,1)S(1)} collective-permute-done((bf16[128,2048]{1,0:T(8,128)(2,1)S(1)}, bf16[128,2048]{1,0:T(8,128)(2,1)S(1)}, u32[]{:S(2)}, u32[]{:S(2)}) %collective-permute-start.48) | collective-permute-done | bytes 524320 | tf_op jit(solution)/shard_map/ppermute | solution.py:72
  369.2 21.6 %collective-permute-done.49 = bf16[128,2048]{1,0:T(8,128)(2,1)S(1)} collective-permute-done((bf16[128,2048]{1,0:T(8,128)(2,1)S(1)}, bf16[128,2048]{1,0:T(8,128)(2,1)S(1)}, u32[]{:S(2)}, u32[]{:S(2)}) %collective-permute-start.49) | collective-permute-done | bytes 524320 | tf_op jit(solution)/shard_map/ppermute | solution.py:72
  396.9 11.6 %collective-permute-start.51 = (bf16[128,2048]{1,0:T(8,128)(2,1)S(1)}, bf16[128,2048]{1,0:T(8,128)(2,1)S(1)}, u32[]{:S(2)}, u32[]{:S(2)}) collective-permute-start(bf16[128,2048]{1,0:T(8,128)(2,1)S(1)} %fusion.44.refs_0_), channel_id=1, source_target_pairs={{0,24},{8,0},{16,8},{24,16},{1,25},{9,1},{17,9},{25,17},{2,26},{10... | collective-permute-start | bytes 1572872 | tf_op jit(solution)/shard_map/ppermute | solution.py:72
  413.3 4.7 collective-permute-done.54
  419.5 34.6 %collective-permute-done.52.refs_2_ = bf16[128,2048]{1,0:T(8,128)(2,1)S(1)} collective-permute-done((bf16[128,2048]{1,0:T(8,128)(2,1)S(1)}, bf16[128,2048]{1,0:T(8,128)(2,1)S(1)}, u32[]{:S(2)}, u32[]{:S(2)}) %collective-permute-start.52) | collective-permute-done | bytes 524320 | tf_op jit(solution)/shard_map/ppermute | solution.py:72
  463.8 6.9 fusion.22
  476.9 5.7 convolution_convert_fusion.2
  489.2 8.6 %fusion.196 = (bf16[512,2048]{1,0:T(8,128)(2,1)S(1)}, f32[512,2048]{1,0:T(8,128)S(1)}) fusion(bf16[512,2048]{1,0:T(8,128)(2,1)} %collective-permute-done.59, bf16[512,2048]{1,0:T(8,128)(2,1)S(1)} %copy-done.7, bf16[2048,2048]{1,0:T(8,128)(2,1)} %shard_map.309), kind=kOutput, calls=%fused_computation.528 | convolution fusion | flops 4298113024 | bytes 18874368 | tf_op jit(solution)/shard_map/...a,ba->...b/dot_general | solution.py:64
  501.6 6.0 shard_map.312
  550.8 13.8 %collective-permute-done.66 = bf16[384,2048]{1,0:T(8,128)(2,1)S(1)} collective-permute-done((bf16[384,2048]{1,0:T(8,128)(2,1)}, bf16[384,2048]{1,0:T(8,128)(2,1)S(1)}, u32[]{:S(2)}, u32[]{:S(2)}) %collective-permute-start.66) | collective-permute-done | bytes 1572896 | tf_op jit(solution)/shard_map/ppermute | solution.py:72
  580.6 6.2 shard_map.315
  595.0 19.7 %collective-permute-done.69.refs_2_ = bf16[128,2048]{1,0:T(8,128)(2,1)} collective-permute-done((bf16[128,2048]{1,0:T(8,128)(2,1)}, bf16[128,2048]{1,0:T(8,128)(2,1)}, u32[]{:S(2)}, u32[]{:S(2)}) %collective-permute-start.69) | collective-permute-done | bytes 524320 | tf_op jit(solution)/shard_map/ppermute | solution.py:72
  614.7 4.5 collective-permute-done.71
  624.7 5.0 collective-permute-start.73
  629.7 4.1 add_convert_fusion
  652.0 9.6 %collective-permute-done.79 = bf16[256,2048]{1,0:T(8,128)(2,1)S(1)} collective-permute-done((bf16[256,2048]{1,0:T(8,128)(2,1)S(1)}, bf16[256,2048]{1,0:T(8,128)(2,1)S(1)}, u32[]{:S(2)}, u32[]{:S(2)}) %collective-permute-start.79) | collective-permute-done | bytes 1048608 | tf_op jit(solution)/shard_map/ppermute | solution.py:72
  668.1 5.1 collective-permute-start.82
  684.3 4.8 fusion.197
  705.7 4.5 fusion.172
  732.9 4.9 shard_map.317
  746.2 7.3 collective-permute-done.91
  767.0 11.4 %collective-permute-done.94 = bf16[656,768]{1,0:T(8,128)(2,1)S(1)} collective-permute-done((bf16[656,768]{1,0:T(8,128)(2,1)S(1)}, bf16[656,768]{1,0:T(8,128)(2,1)S(1)}, u32[]{:S(2)}, u32[]{:S(2)}) %collective-permute-start.94) | collective-permute-done | bytes 1007648 | tf_op jit(solution)/shard_map/ppermute | solution.py:72
  779.9 3.9 collective-permute-start.97
  798.5 3.7 shard_map.320
  807.5 3.7 collective-permute-done.103
  (956 shorter events, 398.5 us)
Async XLA Ops:
  13.9 26.0 %collective-permute-start.4 = (bf16[64,16384]{1,0:T(8,128)(2,1)}, bf16[64,16384]{1,0:T(8,128)(2,1)}, u32[]{:S(2)}, u32[]{:S(2)}) collective-permute-start(bf16[64,16384]{1,0:T(8,128)(2,1)} %pad_maximum_fusion.refs_0_), channel_id=1, source_target_pairs={{0,1},{1,0},{2,3},{3,2},{4,5},{5,4},{6,7},{7,6},{8,9},{9,8},{10,11... | collective-permute-start | bytes 6291464 | tf_op jit(solution)/shard_map/ppermute | solution.py:76
  17.7 22.2 %collective-permute-start.2 = (bf16[128,1152]{1,0:T(8,128)(2,1)S(1)}, bf16[128,1152]{1,0:T(8,128)(2,1)S(1)}, u32[]{:S(2)}, u32[]{:S(2)}) collective-permute-start(bf16[128,1152]{1,0:T(8,128)(2,1)S(1)} %copy-done.205), channel_id=1, source_target_pairs={{0,16},{8,24},{16,0},{24,8},{1,17},{9,25},{17,1},{25,9},{2,18},{10... | collective-permute-start | bytes 884744 | tf_op jit(solution)/shard_map/ppermute | solution.py:72
  20.0 19.9 %collective-permute-start.3 = (bf16[128,1152]{1,0:T(8,128)(2,1)S(1)}, bf16[128,1152]{1,0:T(8,128)(2,1)S(1)}, u32[]{:S(2)}, u32[]{:S(2)}) collective-permute-start(bf16[128,1152]{1,0:T(8,128)(2,1)S(1)} %copy-done.204), channel_id=1, source_target_pairs={{0,24},{8,0},{16,8},{24,16},{1,25},{9,1},{17,9},{25,17},{2,26},{10... | collective-permute-start | bytes 884744 | tf_op jit(solution)/shard_map/ppermute | solution.py:72
  39.9 62.3 %collective-permute-start.6 = (bf16[128,2048]{1,0:T(8,128)(2,1)S(1)}, bf16[128,2048]{1,0:T(8,128)(2,1)}, u32[]{:S(2)}, u32[]{:S(2)}) collective-permute-start(bf16[128,2048]{1,0:T(8,128)(2,1)S(1)} %bitcast.293), channel_id=1, source_target_pairs={{0,24},{8,0},{16,8},{24,16},{1,25},{9,1},{17,9},{25,17},{2,26},{10... | collective-permute-start | bytes 1572872 | tf_op jit(solution)/shard_map/ppermute | solution.py:72
  46.9 55.4 %collective-permute-start.7 = (bf16[128,2048]{1,0:T(8,128)(2,1)S(1)}, bf16[128,2048]{1,0:T(8,128)(2,1)}, u32[]{:S(2)}, u32[]{:S(2)}) collective-permute-start(bf16[128,2048]{1,0:T(8,128)(2,1)S(1)} %bitcast.294), channel_id=1, source_target_pairs={{0,16},{8,24},{16,0},{24,8},{1,17},{9,25},{17,1},{25,9},{2,18},{10... | collective-permute-start | bytes 1572872 | tf_op jit(solution)/shard_map/ppermute | solution.py:72
  47.7 54.5 %collective-permute-start.8 = (bf16[128,2048]{1,0:T(8,128)(2,1)S(1)}, bf16[128,2048]{1,0:T(8,128)(2,1)}, u32[]{:S(2)}, u32[]{:S(2)}) collective-permute-start(bf16[128,2048]{1,0:T(8,128)(2,1)S(1)} %bitcast.295), channel_id=1, source_target_pairs={{0,8},{8,16},{16,24},{24,0},{1,9},{9,17},{17,25},{25,1},{2,10},{10... | collective-permute-start | bytes 1572872 | tf_op jit(solution)/shard_map/ppermute | solution.py:72
  50.8 26.5 %collective-permute-start.9 = (bf16[512,1152]{1,0:T(8,128)(2,1)}, bf16[512,1152]{1,0:T(8,128)(2,1)}, u32[]{:S(2)}, u32[]{:S(2)}) collective-permute-start(bf16[512,1152]{1,0:T(8,128)(2,1)} %shard_map.298.refs_0_), channel_id=1, source_target_pairs={{0,2},{2,0},{1,3},{3,1},{4,6},{6,4},{5,7},{7,5},{8,10},{10,8},{9,1... | collective-permute-start | bytes 3538952 | tf_op jit(solution)/shard_map/ppermute | solution.py:72
  52.0 26.2 %collective-permute-start.10 = (bf16[512,1152]{1,0:T(8,128)(2,1)}, bf16[512,1152]{1,0:T(8,128)(2,1)}, u32[]{:S(2)}, u32[]{:S(2)}) collective-permute-start(bf16[512,1152]{1,0:T(8,128)(2,1)} %shard_map.298.refs_0_), channel_id=1, source_target_pairs={{0,4},{4,0},{1,5},{5,1},{2,6},{6,2},{3,7},{7,3},{8,12},{12,8},{9,1... | collective-permute-start | bytes 3538952 | tf_op jit(solution)/shard_map/ppermute | solution.py:72
  126.4 19.3 %collective-permute-start.19 = (bf16[512,512]{1,0:T(8,128)(2,1)S(1)}, bf16[512,512]{1,0:T(8,128)(2,1)S(1)}, u32[]{:S(2)}, u32[]{:S(2)}) collective-permute-start(bf16[512,512]{1,0:T(8,128)(2,1)S(1)} %get-tuple-element.538), channel_id=1, source_target_pairs={{0,4},{4,0},{1,5},{5,1},{2,6},{6,2},{3,7},{7,3},{8,12},{12,8},{9,1... | collective-permute-start | bytes 1572872 | tf_op jit(solution)/shard_map/ppermute | solution.py:72
  182.8 45.6 %collective-permute-start.36 = (bf16[512,2048]{1,0:T(8,128)(2,1)}, bf16[512,2048]{1,0:T(8,128)(2,1)S(1)}, u32[]{:S(2)}, u32[]{:S(2)}) collective-permute-start(bf16[512,2048]{1,0:T(8,128)(2,1)} %shard_map.305.refs_0_), channel_id=1, source_target_pairs={{0,2},{2,0},{1,3},{3,1},{4,6},{6,4},{5,7},{7,5},{8,10},{10,8},{9,1... | collective-permute-start | bytes 6291464 | tf_op jit(solution)/shard_map/ppermute | solution.py:72
  183.1 45.3 %collective-permute-start.37 = (bf16[512,2048]{1,0:T(8,128)(2,1)}, bf16[512,2048]{1,0:T(8,128)(2,1)}, u32[]{:S(2)}, u32[]{:S(2)}) collective-permute-start(bf16[512,2048]{1,0:T(8,128)(2,1)} %shard_map.305.refs_0_), channel_id=1, source_target_pairs={{0,4},{4,0},{1,5},{5,1},{2,6},{6,2},{3,7},{7,3},{8,12},{12,8},{9,1... | collective-permute-start | bytes 6291464 | tf_op jit(solution)/shard_map/ppermute | solution.py:72
  187.4 35.6 %collective-permute-start.34 = (bf16[128,2048]{1,0:T(8,128)(2,1)}, bf16[128,2048]{1,0:T(8,128)(2,1)S(1)}, u32[]{:S(2)}, u32[]{:S(2)}) collective-permute-start(bf16[128,2048]{1,0:T(8,128)(2,1)} %get-tuple-element.581), channel_id=1, source_target_pairs={{0,16},{8,24},{16,0},{24,8},{1,17},{9,25},{17,1},{25,9},{2,18},{10... | collective-permute-start | bytes 1572872 | tf_op jit(solution)/shard_map/ppermute | solution.py:72
  188.1 34.8 %collective-permute-start.35 = (bf16[128,2048]{1,0:T(8,128)(2,1)}, bf16[128,2048]{1,0:T(8,128)(2,1)S(1)}, u32[]{:S(2)}, u32[]{:S(2)}) collective-permute-start(bf16[128,2048]{1,0:T(8,128)(2,1)} %get-tuple-element.582), channel_id=1, source_target_pairs={{0,24},{8,0},{16,8},{24,16},{1,25},{9,1},{17,9},{25,17},{2,26},{10... | collective-permute-start | bytes 1572872 | tf_op jit(solution)/shard_map/ppermute | solution.py:72
  235.7 56.6 %collective-permute-start.41 = (bf16[512,2048]{1,0:T(8,128)(2,1)}, bf16[512,2048]{1,0:T(8,128)(2,1)S(1)}, u32[]{:S(2)}, u32[]{:S(2)}) collective-permute-start(bf16[512,2048]{1,0:T(8,128)(2,1)} %shard_map.306), channel_id=1, source_target_pairs={{0,4},{4,0},{1,5},{5,1},{2,6},{6,2},{3,7},{7,3},{8,12},{12,8},{9,1... | collective-permute-start | bytes 6291464 | tf_op jit(solution)/shard_map/ppermute | solution.py:72
  240.1 53.2 %collective-permute-start.42 = (bf16[512,2048]{1,0:T(8,128)(2,1)}, bf16[512,2048]{1,0:T(8,128)(2,1)}, u32[]{:S(2)}, u32[]{:S(2)}) collective-permute-start(bf16[512,2048]{1,0:T(8,128)(2,1)} %shard_map.307), channel_id=1, source_target_pairs={{0,2},{2,0},{1,3},{3,1},{4,6},{6,4},{5,7},{7,5},{8,10},{10,8},{9,1... | collective-permute-start | bytes 6291464 | tf_op jit(solution)/shard_map/ppermute | solution.py:72
  241.0 16.8 %collective-permute-start.38 = (bf16[128,2048]{1,0:T(8,128)(2,1)}, bf16[128,2048]{1,0:T(8,128)(2,1)S(1)}, u32[]{:S(2)}, u32[]{:S(2)}) collective-permute-start(bf16[128,2048]{1,0:T(8,128)(2,1)} %multiply_convert_fusion.5.refs_0_), channel_id=1, source_target_pairs={{0,24},{8,0},{16,8},{24,16},{1,25},{9,1},{17,9},{25,17},{2,26},{10... | collective-permute-start | bytes 1572872 | tf_op jit(solution)/shard_map/ppermute | solution.py:72
  245.9 46.4 %collective-permute-start.39 = (bf16[128,2048]{1,0:T(8,128)(2,1)}, bf16[128,2048]{1,0:T(8,128)(2,1)S(1)}, u32[]{:S(2)}, u32[]{:S(2)}) collective-permute-start(bf16[128,2048]{1,0:T(8,128)(2,1)} %multiply_convert_fusion.5.refs_0_), channel_id=1, source_target_pairs={{0,16},{8,24},{16,0},{24,8},{1,17},{9,25},{17,1},{25,9},{2,18},{10... | collective-permute-start | bytes 1572872 | tf_op jit(solution)/shard_map/ppermute | solution.py:72
  247.6 44.7 %collective-permute-start.40 = (bf16[128,2048]{1,0:T(8,128)(2,1)}, bf16[128,2048]{1,0:T(8,128)(2,1)S(1)}, u32[]{:S(2)}, u32[]{:S(2)}) collective-permute-start(bf16[128,2048]{1,0:T(8,128)(2,1)} %multiply_convert_fusion.5.refs_0_), channel_id=1, source_target_pairs={{0,8},{8,16},{16,24},{24,0},{1,9},{9,17},{17,25},{25,1},{2,10},{10... | collective-permute-start | bytes 1572872 | tf_op jit(solution)/shard_map/ppermute | solution.py:72
  297.0 25.3 %collective-permute-start.43 = (bf16[512,2048]{1,0:T(8,128)(2,1)}, bf16[512,2048]{1,0:T(8,128)(2,1)}, u32[]{:S(2)}, u32[]{:S(2)}) collective-permute-start(bf16[512,2048]{1,0:T(8,128)(2,1)} %shard_map.308.refs_0_), channel_id=1, source_target_pairs={{0,1},{1,0},{2,3},{3,2},{4,5},{5,4},{6,7},{7,6},{8,9},{9,8},{10,11... | collective-permute-start | bytes 6291464 | tf_op jit(solution)/shard_map/ppermute | solution.py:76
  302.2 28.6 %collective-permute-start.44 = (bf16[128,2048]{1,0:T(8,128)(2,1)}, bf16[128,2048]{1,0:T(8,128)(2,1)}, u32[]{:S(2)}, u32[]{:S(2)}) collective-permute-start(bf16[128,2048]{1,0:T(8,128)(2,1)} %slice.618), channel_id=1, source_target_pairs={{0,4},{4,0},{1,5},{5,1},{2,6},{6,2},{3,7},{7,3},{8,12},{12,8},{9,1... | collective-permute-start | bytes 1572872 | tf_op jit(solution)/shard_map/ppermute | solution.py:72
  304.2 26.6 %collective-permute-start.45 = (bf16[128,2048]{1,0:T(8,128)(2,1)}, bf16[128,2048]{1,0:T(8,128)(2,1)}, u32[]{:S(2)}, u32[]{:S(2)}) collective-permute-start(bf16[128,2048]{1,0:T(8,128)(2,1)} %slice.619), channel_id=1, source_target_pairs={{0,2},{2,0},{1,3},{3,1},{4,6},{6,4},{5,7},{7,5},{8,10},{10,8},{9,1... | collective-permute-start | bytes 1572872 | tf_op jit(solution)/shard_map/ppermute | solution.py:72
  354.2 36.6 %collective-permute-start.49 = (bf16[128,2048]{1,0:T(8,128)(2,1)S(1)}, bf16[128,2048]{1,0:T(8,128)(2,1)S(1)}, u32[]{:S(2)}, u32[]{:S(2)}) collective-permute-start(bf16[128,2048]{1,0:T(8,128)(2,1)S(1)} %get-tuple-element.633), channel_id=1, source_target_pairs={{0,16},{8,24},{16,0},{24,8},{1,17},{9,25},{17,1},{25,9},{2,18},{10... | collective-permute-start | bytes 1572872 | tf_op jit(solution)/shard_map/ppermute | solution.py:72
  354.7 36.1 %collective-permute-start.50 = (bf16[128,2048]{1,0:T(8,128)(2,1)S(1)}, bf16[128,2048]{1,0:T(8,128)(2,1)S(1)}, u32[]{:S(2)}, u32[]{:S(2)}) collective-permute-start(bf16[128,2048]{1,0:T(8,128)(2,1)S(1)} %get-tuple-element.634), channel_id=1, source_target_pairs={{0,24},{8,0},{16,8},{24,16},{1,25},{9,1},{17,9},{25,17},{2,26},{10... | collective-permute-start | bytes 1572872 | tf_op jit(solution)/shard_map/ppermute | solution.py:72
  396.9 22.6 %collective-permute-start.51 = (bf16[128,2048]{1,0:T(8,128)(2,1)S(1)}, bf16[128,2048]{1,0:T(8,128)(2,1)S(1)}, u32[]{:S(2)}, u32[]{:S(2)}) collective-permute-start(bf16[128,2048]{1,0:T(8,128)(2,1)S(1)} %fusion.44.refs_0_), channel_id=1, source_target_pairs={{0,24},{8,0},{16,8},{24,16},{1,25},{9,1},{17,9},{25,17},{2,26},{10... | collective-permute-start | bytes 1572872 | tf_op jit(solution)/shard_map/ppermute | solution.py:72
  408.5 45.6 %collective-permute-start.52 = (bf16[128,2048]{1,0:T(8,128)(2,1)S(1)}, bf16[128,2048]{1,0:T(8,128)(2,1)S(1)}, u32[]{:S(2)}, u32[]{:S(2)}) collective-permute-start(bf16[128,2048]{1,0:T(8,128)(2,1)S(1)} %fusion.44.refs_0_), channel_id=1, source_target_pairs={{0,16},{8,24},{16,0},{24,8},{1,17},{9,25},{17,1},{25,9},{2,18},{10... | collective-permute-start | bytes 1572872 | tf_op jit(solution)/shard_map/ppermute | solution.py:72
  409.6 44.5 %collective-permute-start.53 = (bf16[128,2048]{1,0:T(8,128)(2,1)S(1)}, bf16[128,2048]{1,0:T(8,128)(2,1)S(1)}, u32[]{:S(2)}, u32[]{:S(2)}) collective-permute-start(bf16[128,2048]{1,0:T(8,128)(2,1)S(1)} %fusion.44.refs_0_), channel_id=1, source_target_pairs={{0,8},{8,16},{16,24},{24,0},{1,9},{9,17},{17,25},{25,1},{2,10},{10... | collective-permute-start | bytes 1572872 | tf_op jit(solution)/shard_map/ppermute | solution.py:72
  500.1 26.1 %collective-permute-start.63 = (bf16[128,2048]{1,0:T(8,128)(2,1)}, bf16[128,2048]{1,0:T(8,128)(2,1)}, u32[]{:S(2)}, u32[]{:S(2)}) collective-permute-start(bf16[128,2048]{1,0:T(8,128)(2,1)} %get-tuple-element.662), channel_id=1, source_target_pairs={{0,16},{8,24},{16,0},{24,8},{1,17},{9,25},{17,1},{25,9},{2,18},{10... | collective-permute-start | bytes 1572872 | tf_op jit(solution)/shard_map/ppermute | solution.py:72
  526.2 24.6 %collective-permute-start.64 = (bf16[128,2048]{1,0:T(8,128)(2,1)}, bf16[128,2048]{1,0:T(8,128)(2,1)S(1)}, u32[]{:S(2)}, u32[]{:S(2)}) collective-permute-start(bf16[128,2048]{1,0:T(8,128)(2,1)} %get-tuple-element.683), channel_id=1, source_target_pairs={{0,8},{8,16},{16,24},{24,0},{1,9},{9,17},{17,25},{25,1},{2,10},{10... | collective-permute-start | bytes 1572872 | tf_op jit(solution)/shard_map/ppermute | solution.py:72
  526.2 24.6 %collective-permute-start.65 = (bf16[128,2048]{1,0:T(8,128)(2,1)}, bf16[128,2048]{1,0:T(8,128)(2,1)S(1)}, u32[]{:S(2)}, u32[]{:S(2)}) collective-permute-start(bf16[128,2048]{1,0:T(8,128)(2,1)} %get-tuple-element.684), channel_id=1, source_target_pairs={{0,24},{8,0},{16,8},{24,16},{1,25},{9,1},{17,9},{25,17},{2,26},{10... | collective-permute-start | bytes 1572872 | tf_op jit(solution)/shard_map/ppermute | solution.py:72
  529.8 34.8 %collective-permute-start.66 = (bf16[384,2048]{1,0:T(8,128)(2,1)}, bf16[384,2048]{1,0:T(8,128)(2,1)S(1)}, u32[]{:S(2)}, u32[]{:S(2)}) collective-permute-start(bf16[384,2048]{1,0:T(8,128)(2,1)} %shard_map.313), channel_id=1, source_target_pairs={{0,2},{2,0},{1,3},{3,1},{4,6},{6,4},{5,7},{7,5},{8,10},{10,8},{9,1... | collective-permute-start | bytes 4718600 | tf_op jit(solution)/shard_map/ppermute | solution.py:72
  530.8 34.5 %collective-permute-start.67 = (bf16[384,2048]{1,0:T(8,128)(2,1)}, bf16[384,2048]{1,0:T(8,128)(2,1)S(1)}, u32[]{:S(2)}, u32[]{:S(2)}) collective-permute-start(bf16[384,2048]{1,0:T(8,128)(2,1)} %shard_map.314), channel_id=1, source_target_pairs={{0,4},{4,0},{1,5},{5,1},{2,6},{6,2},{3,7},{7,3},{8,12},{12,8},{9,1... | collective-permute-start | bytes 4718600 | tf_op jit(solution)/shard_map/ppermute | solution.py:72
  571.2 23.5 %collective-permute-start.68 = (bf16[128,2048]{1,0:T(8,128)(2,1)}, bf16[128,2048]{1,0:T(8,128)(2,1)}, u32[]{:S(2)}, u32[]{:S(2)}) collective-permute-start(bf16[128,2048]{1,0:T(8,128)(2,1)} %fusion.46.refs_0_), channel_id=1, source_target_pairs={{0,24},{8,0},{16,8},{24,16},{1,25},{9,1},{17,9},{25,17},{2,26},{10... | collective-permute-start | bytes 1572872 | tf_op jit(solution)/shard_map/ppermute | solution.py:72
  571.5 43.1 %collective-permute-start.69 = (bf16[128,2048]{1,0:T(8,128)(2,1)}, bf16[128,2048]{1,0:T(8,128)(2,1)}, u32[]{:S(2)}, u32[]{:S(2)}) collective-permute-start(bf16[128,2048]{1,0:T(8,128)(2,1)} %fusion.46.refs_0_), channel_id=1, source_target_pairs={{0,16},{8,24},{16,0},{24,8},{1,17},{9,25},{17,1},{25,9},{2,18},{10... | collective-permute-start | bytes 1572872 | tf_op jit(solution)/shard_map/ppermute | solution.py:72
  571.5 43.1 %collective-permute-start.70 = (bf16[128,2048]{1,0:T(8,128)(2,1)}, bf16[128,2048]{1,0:T(8,128)(2,1)}, u32[]{:S(2)}, u32[]{:S(2)}) collective-permute-start(bf16[128,2048]{1,0:T(8,128)(2,1)} %fusion.46.refs_0_), channel_id=1, source_target_pairs={{0,8},{8,16},{16,24},{24,0},{1,9},{9,17},{17,25},{25,1},{2,10},{10... | collective-permute-start | bytes 1572872 | tf_op jit(solution)/shard_map/ppermute | solution.py:72
  574.8 44.4 %collective-permute-start.71 = (bf16[512,2048]{1,0:T(8,128)(2,1)}, bf16[512,2048]{1,0:T(8,128)(2,1)}, u32[]{:S(2)}, u32[]{:S(2)}) collective-permute-start(bf16[512,2048]{1,0:T(8,128)(2,1)} %pad_maximum_fusion.4), channel_id=1, source_target_pairs={{0,4},{4,0},{1,5},{5,1},{2,6},{6,2},{3,7},{7,3},{8,12},{12,8},{9,1... | collective-permute-start | bytes 6291464 | tf_op jit(solution)/shard_map/ppermute | solution.py:72
  577.6 44.1 %collective-permute-start.72 = (bf16[512,2048]{1,0:T(8,128)(2,1)}, bf16[512,2048]{1,0:T(8,128)(2,1)}, u32[]{:S(2)}, u32[]{:S(2)}) collective-permute-start(bf16[512,2048]{1,0:T(8,128)(2,1)} %pad_maximum_fusion.5), channel_id=1, source_target_pairs={{0,2},{2,0},{1,3},{3,1},{4,6},{6,4},{5,7},{7,5},{8,10},{10,8},{9,1... | collective-permute-start | bytes 6291464 | tf_op jit(solution)/shard_map/ppermute | solution.py:72
  594.7 57.3 %collective-permute-start.78 = (bf16[256,2048]{1,0:T(8,128)(2,1)}, bf16[256,2048]{1,0:T(8,128)(2,1)}, u32[]{:S(2)}, u32[]{:S(2)}) collective-permute-start(bf16[256,2048]{1,0:T(8,128)(2,1)} %pad_maximum_fusion.15), channel_id=1, source_target_pairs={{0,4},{4,0},{1,5},{5,1},{2,6},{6,2},{3,7},{7,3},{8,12},{12,8},{9,1... | collective-permute-start | bytes 3145736 | tf_op jit(solution)/shard_map/ppermute | solution.py:72
  624.7 17.5 %collective-permute-start.73 = (bf16[512,2048]{1,0:T(8,128)(2,1)}, bf16[512,2048]{1,0:T(8,128)(2,1)S(1)}, u32[]{:S(2)}, u32[]{:S(2)}) collective-permute-start(bf16[512,2048]{1,0:T(8,128)(2,1)} %shard_map.316), channel_id=1, source_target_pairs={{0,1},{1,0},{2,3},{3,2},{4,5},{5,4},{6,7},{7,6},{8,9},{9,8},{10,11... | collective-permute-start | bytes 6291464 | tf_op jit(solution)/shard_map/ppermute | solution.py:76
  636.8 24.9 %collective-permute-start.79 = (bf16[256,2048]{1,0:T(8,128)(2,1)S(1)}, bf16[256,2048]{1,0:T(8,128)(2,1)S(1)}, u32[]{:S(2)}, u32[]{:S(2)}) collective-permute-start(bf16[256,2048]{1,0:T(8,128)(2,1)S(1)} %pad_maximum_fusion.16), channel_id=1, source_target_pairs={{0,2},{2,0},{1,3},{3,1},{4,6},{6,4},{5,7},{7,5},{8,10},{10,8},{9,1... | collective-permute-start | bytes 3145736 | tf_op jit(solution)/shard_map/ppermute | solution.py:72
  639.6 22.0 %collective-permute-start.75 = (bf16[64,2048]{1,0:T(8,128)(2,1)S(1)}, bf16[64,2048]{1,0:T(8,128)(2,1)S(1)}, u32[]{:S(2)}, u32[]{:S(2)}) collective-permute-start(bf16[64,2048]{1,0:T(8,128)(2,1)S(1)} %get-tuple-element.1082), channel_id=1, source_target_pairs={{0,8},{8,16},{16,24},{24,0},{1,9},{9,17},{17,25},{25,1},{2,10},{10... | collective-permute-start | bytes 786440 | tf_op jit(solution)/shard_map/ppermute | solution.py:72
  641.1 20.5 %collective-permute-start.76 = (bf16[64,2048]{1,0:T(8,128)(2,1)S(1)}, bf16[64,2048]{1,0:T(8,128)(2,1)S(1)}, u32[]{:S(2)}, u32[]{:S(2)}) collective-permute-start(bf16[64,2048]{1,0:T(8,128)(2,1)S(1)} %get-tuple-element.1081), channel_id=1, source_target_pairs={{0,16},{8,24},{16,0},{24,8},{1,17},{9,25},{17,1},{25,9},{2,18},{10... | collective-permute-start | bytes 786440 | tf_op jit(solution)/shard_map/ppermute | solution.py:72
  642.2 19.4 %collective-permute-start.77 = (bf16[64,2048]{1,0:T(8,128)(2,1)S(1)}, bf16[64,2048]{1,0:T(8,128)(2,1)S(1)}, u32[]{:S(2)}, u32[]{:S(2)}) collective-permute-start(bf16[64,2048]{1,0:T(8,128)(2,1)S(1)} %get-tuple-element.1080), channel_id=1, source_target_pairs={{0,24},{8,0},{16,8},{24,16},{1,25},{9,1},{17,9},{25,17},{2,26},{10... | collective-permute-start | bytes 786440 | tf_op jit(solution)/shard_map/ppermute | solution.py:72
  713.5 25.5 %collective-permute-start.89 = (bf16[128,2048]{1,0:T(8,128)(2,1)}, bf16[128,2048]{1,0:T(8,128)(2,1)}, u32[]{:S(2)}, u32[]{:S(2)}) collective-permute-start(bf16[128,2048]{1,0:T(8,128)(2,1)} %get-tuple-element.751), channel_id=1, source_target_pairs={{0,16},{8,24},{16,0},{24,8},{1,17},{9,25},{17,1},{25,9},{2,18},{10... | collective-permute-start | bytes 1572872 | tf_op jit(solution)/shard_map/ppermute | solution.py:72
  757.2 21.2 %collective-permute-start.94 = (bf16[656,768]{1,0:T(8,128)(2,1)S(1)}, bf16[656,768]{1,0:T(8,128)(2,1)S(1)}, u32[]{:S(2)}, u32[]{:S(2)}) collective-permute-start(bf16[656,768]{1,0:T(8,128)(2,1)S(1)} %pad_maximum_fusion.18), channel_id=1, source_target_pairs={{0,4},{4,0},{1,5},{5,1},{2,6},{6,2},{3,7},{7,3},{8,12},{12,8},{9,1... | collective-permute-start | bytes 3022856 | tf_op jit(solution)/shard_map/ppermute | solution.py:72
  758.3 20.9 %collective-permute-start.95 = (bf16[656,768]{1,0:T(8,128)(2,1)S(1)}, bf16[656,768]{1,0:T(8,128)(2,1)S(1)}, u32[]{:S(2)}, u32[]{:S(2)}) collective-permute-start(bf16[656,768]{1,0:T(8,128)(2,1)S(1)} %pad_maximum_fusion.19), channel_id=1, source_target_pairs={{0,2},{2,0},{1,3},{3,1},{4,6},{6,4},{5,7},{7,5},{8,10},{10,8},{9,1... | collective-permute-start | bytes 3022856 | tf_op jit(solution)/shard_map/ppermute | solution.py:72
  791.0 21.9 %collective-permute-start.98 = (bf16[64,1920]{1,0:T(8,128)(2,1)}, bf16[64,1920]{1,0:T(8,128)(2,1)S(1)}, u32[]{:S(2)}, u32[]{:S(2)}) collective-permute-start(bf16[64,1920]{1,0:T(8,128)(2,1)} %get-tuple-element.853), channel_id=1, source_target_pairs={{0,8},{8,16},{16,24},{24,0},{1,9},{9,17},{17,25},{25,1},{2,10},{10... | collective-permute-start | bytes 737288 | tf_op jit(solution)/shard_map/ppermute | solution.py:72
  791.0 21.9 %collective-permute-start.99 = (bf16[64,1920]{1,0:T(8,128)(2,1)}, bf16[64,1920]{1,0:T(8,128)(2,1)S(1)}, u32[]{:S(2)}, u32[]{:S(2)}) collective-permute-start(bf16[64,1920]{1,0:T(8,128)(2,1)} %get-tuple-element.854), channel_id=1, source_target_pairs={{0,16},{8,24},{16,0},{24,8},{1,17},{9,25},{17,1},{25,9},{2,18},{10... | collective-permute-start | bytes 737288 | tf_op jit(solution)/shard_map/ppermute | solution.py:72
  793.1 19.8 %collective-permute-start.100 = (bf16[64,1920]{1,0:T(8,128)(2,1)}, bf16[64,1920]{1,0:T(8,128)(2,1)S(1)}, u32[]{:S(2)}, u32[]{:S(2)}) collective-permute-start(bf16[64,1920]{1,0:T(8,128)(2,1)} %get-tuple-element.855), channel_id=1, source_target_pairs={{0,24},{8,0},{16,8},{24,16},{1,25},{9,1},{17,9},{25,17},{2,26},{10... | collective-permute-start | bytes 737288 | tf_op jit(solution)/shard_map/ppermute | solution.py:72
  (275 other events, 2746.1 us)
